TPU v7x, 32 devices: a whole 2x2x4 slice. The times are simulated.
32 devices in a mesh: segment: 2 (over core), seq: 8 (over z, x), head: 2 (over y).
Axes of the slice: x: 2, y: 2, z: 4, core: 2. Of those that a mesh axis runs over, the one named last changes fastest.
Arguments:
- stream_in: bfloat16 [2, 2048, 3072], P('segment', 'seq'), may hold values from -6 to 6
- queries: bfloat16 [2, 2048, 1536], P('segment', 'seq', 'head'), may hold values from -8 to 8
- keys: bfloat16 [2, 2048, 1536], P('segment', 'seq', 'head'), may hold values from -8 to 8
- values: bfloat16 [2, 2048, 1536], P('segment', 'seq', 'head'), may hold values from -6 to 6
- out_weight: bfloat16 [2, 1536, 3072], P('segment', 'head'), may hold values from -0.15625 to 0.15625
- gate_scale: float32 [2, 3072], P('segment'), may hold values from 0.5 to 2
Outputs:
- stream_out: bfloat16 [2, 2048, 3072], P('segment', 'seq', 'head')
All inputs are finite; a program needn't handle non-finite values.
Results may differ from a plain program's by a relative error of at most 0.0065.
Values may be sent and summed in bfloat16 or wider, within the bound.
No kernel may reach another device: no remote copies, remote signals or barrier semaphores. Data moves between devices by JAX's collectives and lax.ppermute only.
A program may use at most 64 MiB of HBM per device.

v0:
```python
import math

import jax
import jax.numpy as jnp
from jax import lax
from jax.sharding import PartitionSpec as P

HD = 128


def passed_along(shard, axis, by):
    count = lax.axis_size(axis)
    return lax.ppermute(shard, axis, [(i, (i + by) % count) for i in range(count)])


def per_device(stream_in, queries, keys, values, out_weight, gate_scale):
    tok_rows = queries.shape[1]
    head_width = queries.shape[2]
    heads_dev = head_width // HD
    score_scale = 1.0 / math.sqrt(HD)
    cycle_len = min(32, lax.axis_size("seq"))
    stride = lax.axis_size("seq") // cycle_len
    query_heads = queries[0].reshape(tok_rows, heads_dev, HD)

    def absorb(running, block):
        row_max, row_sum, accumulated = running
        key_count = block.shape[1]
        key_block = block[0].reshape(key_count, heads_dev, HD)
        value_block = block[1].reshape(key_count, heads_dev, HD)
        scores = (
            jnp.einsum("qhd,khd->hqk", query_heads, key_block, preferred_element_type=jnp.float32)
            * score_scale
        )
        new_max = jnp.maximum(row_max, jnp.max(scores, axis=2))
        shrink = jnp.exp(row_max - new_max)
        raised = jnp.exp(scores - new_max[:, :, None])
        row_sum = row_sum * shrink + jnp.sum(raised, axis=2)
        mixed = jnp.einsum(
            "hqk,khd->qhd",
            raised.astype(jnp.bfloat16),
            value_block,
            preferred_element_type=jnp.float32,
        )
        accumulated = accumulated * shrink.T[:, :, None] + mixed
        return (new_max, row_sum, accumulated)

    initial = (
        jnp.full((heads_dev, tok_rows), -1e30, jnp.float32),
        jnp.zeros((heads_dev, tok_rows), jnp.float32),
        jnp.zeros((tok_rows, heads_dev, HD), jnp.float32),
    )
    own_block = jnp.stack([keys[0], values[0]])

    def turn(index, carry):
        running, current = carry
        arrived = passed_along(current, "seq", stride)
        running = absorb(running, current)
        return (running, arrived)

    running, current = lax.fori_loop(0, cycle_len - 1, turn, (initial, own_block))
    running = absorb(running, current)
    row_max, row_sum, accumulated = running
    attended = (
        (accumulated / row_sum.T[:, :, None]).astype(jnp.bfloat16).reshape(tok_rows, head_width)
    )
    partial_value = jnp.dot(attended, out_weight[0], preferred_element_type=jnp.float32)
    residual = stream_in[0].astype(jnp.float32)
    column_share = lax.psum_scatter(
        partial_value.astype(jnp.bfloat16), "head", scatter_dimension=1, tiled=True
    ).astype(jnp.float32)
    col_count = column_share.shape[1]
    col_start = lax.axis_index("head") * col_count
    own_cols = lax.dynamic_slice_in_dim(residual, col_start, col_count, 1)
    own_gate = lax.dynamic_slice_in_dim(gate_scale[0], col_start, col_count, 0)
    updated = (own_cols + own_gate[None, :] * column_share).astype(jnp.bfloat16)
    return passed_along(updated[None], "segment", 1)


def solution(mesh):
    return jax.shard_map(
        per_device,
        mesh=mesh,
        in_specs=(
            P("segment", "seq", None),
            P("segment", "seq", "head"),
            P("segment", "seq", "head"),
            P("segment", "seq", "head"),
            P("segment", "head", None),
            P("segment", None),
        ),
        out_specs=P("segment", "seq", "head"),
        check_vma=False,
    )
```

profile of v0, /device:TPU:0, one launch (start us, length us, event | category | flops | bytes accessed | tf_op | source)
XLA Modules:
  0.0 190.4 jit_solution(3936654093119951408)
XLA Ops:
  6.6 1.2 copy.16
  7.8 0.9 copy.17
  9.2 139.9 %while.17 = (s32[]{:T(128)}, f32[6,256]{1,0:T(8,128)}, f32[6,256]{1,0:T(8,128)}, f32[256,6,128]{2,0,1:T(8,128)}, bf16[2,256,768]{1,2,0:T(8,128)(2,1)S(1)}, /*ind...) while((s32[]{:T(128)}, f32[6,256]{1,0:T(8,128)}, f32[6,256]{1,0:T(8,128)}, ...), condition=%wide.region_3.0_spmd.clone, body=%wide.region_0.0_spmd.clone.sunk | while | flops 204284928 | bytes 15532309 | solution.py:60
  9.3 3.0 %collective-permute-start = (bf16[2,256,768]{1,2,0:T(8,128)(2,1)S(1)}, bf16[2,256,768]{1,2,0:T(8,128)(2,1)S(1)}, u32[]{:S(2)}, u32[]{:S(2)}) collective-permute-start(bf16[2,256,768]{1,2,0:T(8,128)(2,1)S(1)} %copy.37), channel_id=1, source_target_pairs={{0,2},{2,4},{4,6},{6,8},{8,10},{10,12},{12,14},{14,0},{1,3},{3,5},... | collective-permute-start | bytes 2359304 | tf_op jit(solution)/shard_map/while/body/eval_jaxpr/ppermute | solution.py:13
  12.4 1.0 fusion.48
  13.4 1.3 fusion.49
  15.3 0.6 copy-done.14
  16.5 2.1 %fusion.52 = f32[256,6,128]{2,0,1:T(8,128)} fusion(bf16[256,6,128]{0,2,1:T(8,128)(2,1)S(1)} %bitcast.69, f32[6,256,256]{1,2,0:T(8,128)S(1)} %get-tuple-element.141, f32[256,6,128]{2,0,1:T(8,128)} %get-tuple-element.155, f32[6,256]{1,0:T(8,128)} %copy-done.4, f32[256,6]{0,1:T(8,128)} %get-tuple-element.143, pred[]{:T(512)S(6)} %compare.3), kind=kOutput, calls=%fused_computation.5.clone.1 | convolution fusion | flops 102039552 | bytes 3551233 | tf_op jit(solution)/shard_map/while/body/eval_jaxpr/hqk,khd->qhd/dot_general | solution.py:38
  18.7 14.2 %collective-permute-done = bf16[2,256,768]{1,2,0:T(8,128)(2,1)S(1)} collective-permute-done((bf16[2,256,768]{1,2,0:T(8,128)(2,1)S(1)}, bf16[2,256,768]{1,2,0:T(8,128)(2,1)S(1)}, u32[]{:S(2)}, u32[]{:S(2)}) %collective-permute-start) | collective-permute-done | bytes 786464 | tf_op jit(solution)/shard_map/while/body/eval_jaxpr/ppermute | solution.py:13
  33.1 0.8 copy-done.2
  33.9 1.0 fusion.48
  34.9 1.4 fusion.49
  36.9 0.6 copy-done.14
  38.1 2.6 %fusion.52 = f32[256,6,128]{2,0,1:T(8,128)} fusion(bf16[256,6,128]{0,2,1:T(8,128)(2,1)S(1)} %bitcast.69, f32[6,256,256]{1,2,0:T(8,128)S(1)} %get-tuple-element.141, f32[256,6,128]{2,0,1:T(8,128)} %get-tuple-element.155, f32[6,256]{1,0:T(8,128)} %copy-done.4, f32[256,6]{0,1:T(8,128)} %get-tuple-element.143, pred[]{:T(512)S(6)} %compare.3), kind=kOutput, calls=%fused_computation.5.clone.1 | convolution fusion | flops 102039552 | bytes 3551233 | tf_op jit(solution)/shard_map/while/body/eval_jaxpr/hqk,khd->qhd/dot_general | solution.py:38
  40.6 13.7 %collective-permute-done = bf16[2,256,768]{1,2,0:T(8,128)(2,1)S(1)} collective-permute-done((bf16[2,256,768]{1,2,0:T(8,128)(2,1)S(1)}, bf16[2,256,768]{1,2,0:T(8,128)(2,1)S(1)}, u32[]{:S(2)}, u32[]{:S(2)}) %collective-permute-start) | collective-permute-done | bytes 786464 | tf_op jit(solution)/shard_map/while/body/eval_jaxpr/ppermute | solution.py:13
  54.6 0.8 copy-done.2
  55.4 1.0 fusion.48
  56.4 1.4 fusion.49
  58.4 0.6 copy-done.14
  59.6 2.6 %fusion.52 = f32[256,6,128]{2,0,1:T(8,128)} fusion(bf16[256,6,128]{0,2,1:T(8,128)(2,1)S(1)} %bitcast.69, f32[6,256,256]{1,2,0:T(8,128)S(1)} %get-tuple-element.141, f32[256,6,128]{2,0,1:T(8,128)} %get-tuple-element.155, f32[6,256]{1,0:T(8,128)} %copy-done.4, f32[256,6]{0,1:T(8,128)} %get-tuple-element.143, pred[]{:T(512)S(6)} %compare.3), kind=kOutput, calls=%fused_computation.5.clone.1 | convolution fusion | flops 102039552 | bytes 3551233 | tf_op jit(solution)/shard_map/while/body/eval_jaxpr/hqk,khd->qhd/dot_general | solution.py:38
  62.2 12.9 %collective-permute-done = bf16[2,256,768]{1,2,0:T(8,128)(2,1)S(1)} collective-permute-done((bf16[2,256,768]{1,2,0:T(8,128)(2,1)S(1)}, bf16[2,256,768]{1,2,0:T(8,128)(2,1)S(1)}, u32[]{:S(2)}, u32[]{:S(2)}) %collective-permute-start) | collective-permute-done | bytes 786464 | tf_op jit(solution)/shard_map/while/body/eval_jaxpr/ppermute | solution.py:13
  75.2 0.8 copy-done.2
  76.0 1.0 fusion.48
  77.1 1.4 fusion.49
  80.2 2.6 %fusion.52 = f32[256,6,128]{2,0,1:T(8,128)} fusion(bf16[256,6,128]{0,2,1:T(8,128)(2,1)S(1)} %bitcast.69, f32[6,256,256]{1,2,0:T(8,128)S(1)} %get-tuple-element.141, f32[256,6,128]{2,0,1:T(8,128)} %get-tuple-element.155, f32[6,256]{1,0:T(8,128)} %copy-done.4, f32[256,6]{0,1:T(8,128)} %get-tuple-element.143, pred[]{:T(512)S(6)} %compare.3), kind=kOutput, calls=%fused_computation.5.clone.1 | convolution fusion | flops 102039552 | bytes 3551233 | tf_op jit(solution)/shard_map/while/body/eval_jaxpr/hqk,khd->qhd/dot_general | solution.py:38
  82.8 12.0 %collective-permute-done = bf16[2,256,768]{1,2,0:T(8,128)(2,1)S(1)} collective-permute-done((bf16[2,256,768]{1,2,0:T(8,128)(2,1)S(1)}, bf16[2,256,768]{1,2,0:T(8,128)(2,1)S(1)}, u32[]{:S(2)}, u32[]{:S(2)}) %collective-permute-start) | collective-permute-done | bytes 786464 | tf_op jit(solution)/shard_map/while/body/eval_jaxpr/ppermute | solution.py:13
  95.0 0.8 copy-done.2
  95.8 1.0 fusion.48
  96.9 1.4 fusion.49
  100.0 2.6 %fusion.52 = f32[256,6,128]{2,0,1:T(8,128)} fusion(bf16[256,6,128]{0,2,1:T(8,128)(2,1)S(1)} %bitcast.69, f32[6,256,256]{1,2,0:T(8,128)S(1)} %get-tuple-element.141, f32[256,6,128]{2,0,1:T(8,128)} %get-tuple-element.155, f32[6,256]{1,0:T(8,128)} %copy-done.4, f32[256,6]{0,1:T(8,128)} %get-tuple-element.143, pred[]{:T(512)S(6)} %compare.3), kind=kOutput, calls=%fused_computation.5.clone.1 | convolution fusion | flops 102039552 | bytes 3551233 | tf_op jit(solution)/shard_map/while/body/eval_jaxpr/hqk,khd->qhd/dot_general | solution.py:38
  102.6 11.2 %collective-permute-done = bf16[2,256,768]{1,2,0:T(8,128)(2,1)S(1)} collective-permute-done((bf16[2,256,768]{1,2,0:T(8,128)(2,1)S(1)}, bf16[2,256,768]{1,2,0:T(8,128)(2,1)S(1)}, u32[]{:S(2)}, u32[]{:S(2)}) %collective-permute-start) | collective-permute-done | bytes 786464 | tf_op jit(solution)/shard_map/while/body/eval_jaxpr/ppermute | solution.py:13
  114.0 0.8 copy-done.2
  114.8 1.0 fusion.48
  115.8 1.4 fusion.49
  119.0 2.6 %fusion.52 = f32[256,6,128]{2,0,1:T(8,128)} fusion(bf16[256,6,128]{0,2,1:T(8,128)(2,1)S(1)} %bitcast.69, f32[6,256,256]{1,2,0:T(8,128)S(1)} %get-tuple-element.141, f32[256,6,128]{2,0,1:T(8,128)} %get-tuple-element.155, f32[6,256]{1,0:T(8,128)} %copy-done.4, f32[256,6]{0,1:T(8,128)} %get-tuple-element.143, pred[]{:T(512)S(6)} %compare.3), kind=kOutput, calls=%fused_computation.5.clone.1 | convolution fusion | flops 102039552 | bytes 3551233 | tf_op jit(solution)/shard_map/while/body/eval_jaxpr/hqk,khd->qhd/dot_general | solution.py:38
  121.6 10.3 %collective-permute-done = bf16[2,256,768]{1,2,0:T(8,128)(2,1)S(1)} collective-permute-done((bf16[2,256,768]{1,2,0:T(8,128)(2,1)S(1)}, bf16[2,256,768]{1,2,0:T(8,128)(2,1)S(1)}, u32[]{:S(2)}, u32[]{:S(2)}) %collective-permute-start) | collective-permute-done | bytes 786464 | tf_op jit(solution)/shard_map/while/body/eval_jaxpr/ppermute | solution.py:13
  132.1 0.8 copy-done.2
  132.9 1.0 fusion.48
  133.9 1.4 fusion.49
  137.1 2.6 %fusion.52 = f32[256,6,128]{2,0,1:T(8,128)} fusion(bf16[256,6,128]{0,2,1:T(8,128)(2,1)S(1)} %bitcast.69, f32[6,256,256]{1,2,0:T(8,128)S(1)} %get-tuple-element.141, f32[256,6,128]{2,0,1:T(8,128)} %get-tuple-element.155, f32[6,256]{1,0:T(8,128)} %copy-done.4, f32[256,6]{0,1:T(8,128)} %get-tuple-element.143, pred[]{:T(512)S(6)} %compare.3), kind=kOutput, calls=%fused_computation.5.clone.1 | convolution fusion | flops 102039552 | bytes 3551233 | tf_op jit(solution)/shard_map/while/body/eval_jaxpr/hqk,khd->qhd/dot_general | solution.py:38
  139.6 9.5 %collective-permute-done = bf16[2,256,768]{1,2,0:T(8,128)(2,1)S(1)} collective-permute-done((bf16[2,256,768]{1,2,0:T(8,128)(2,1)S(1)}, bf16[2,256,768]{1,2,0:T(8,128)(2,1)S(1)}, u32[]{:S(2)}, u32[]{:S(2)}) %collective-permute-start) | collective-permute-done | bytes 786464 | tf_op jit(solution)/shard_map/while/body/eval_jaxpr/ppermute | solution.py:13
  149.1 0.8 fusion.25
  152.8 1.1 copy-done.3
  153.8 2.6 %fusion.9 = bf16[256,3072]{1,0:T(8,128)(2,1)} fusion(bf16[256,768]{0,1:T(8,128)(2,1)S(1)} %bitcast.73, bf16[1,768,3072]{2,1,0:T(8,128)(2,1)S(1)} %copy-done.3), kind=kOutput, calls=%fused_computation.15 | convolution fusion | flops 1208745984 | bytes 6684672 | tf_op jit(solution)/shard_map/dot_general | solution.py:66
  156.5 22.4 %reduce-scatter.2.cloned.1.call-done = bf16[256,1536]{1,0:T(8,128)(2,1)} async-done(((bf16[256,3072]{1,0:T(8,128)(2,1)}), bf16[256,1536]{1,0:T(8,128)(2,1)}) %reduce-scatter.2.cloned.1.call-update) | async-done | bytes 786448 | tf_op jit(solution)/shard_map/reduce_scatter | solution.py:68
  178.9 1.4 fusion.20
  180.4 2.3 %collective-permute-done.1 = bf16[1,256,1536]{2,1,0:T(8,128)(2,1)S(1)} collective-permute-done((bf16[1,256,1536]{2,1,0:T(8,128)(2,1)S(1)}, bf16[1,256,1536]{2,1,0:T(8,128)(2,1)S(1)}, u32[]{:S(2)}, u32[]{:S(2)}) %collective-permute-start.1) | collective-permute-done | bytes 786464 | tf_op jit(solution)/shard_map/ppermute | solution.py:13
  182.6 0.9 copy.44
  (139 shorter events, 15.0 us)
Async XLA Ops:
  6.5 149.9 %copy-start = (f32[1,3072]{1,0:T(1,128)S(1)}, f32[1,3072]{1,0:T(1,128)}, u32[]{:S(2)}) copy-start(f32[1,3072]{1,0:T(1,128)} %param.13) | copy-start | bytes 36868
  6.5 2.2 %copy-start.9 = (bf16[1,256,768]{2,1,0:T(8,128)(2,1)S(1)}, bf16[1,256,768]{2,1,0:T(8,128)(2,1)}, u32[]{:S(2)}) copy-start(bf16[1,256,768]{2,1,0:T(8,128)(2,1)} %param.10) | copy-start | bytes 1179652
  6.5 2.4 %copy-start.10 = (bf16[1,256,768]{2,1,0:T(8,128)(2,1)S(1)}, bf16[1,256,768]{2,1,0:T(8,128)(2,1)}, u32[]{:S(2)}) copy-start(bf16[1,256,768]{2,1,0:T(8,128)(2,1)} %param.11) | copy-start | bytes 1179652
  6.5 172.3 %reduce-scatter.2.cloned.1.call-start = ((), (), s32[]{:S(2)}) async-start(), calls=%async_computation.1 | async-start | bytes 2359296 | tf_op jit(solution)/shard_map/reduce_scatter | solution.py:68
  7.8 1.3 copy-start.5
  9.2 3.1 %copy-start.2 = (bf16[256,6,128]{2,0,1:T(8,128)(2,1)S(1)}, bf16[256,6,128]{2,0,1:T(8,128)(2,1)}, u32[]{:S(2)}) copy-start(bf16[256,6,128]{2,0,1:T(8,128)(2,1)} %get-tuple-element.165) | copy-start | bytes 1179652 | tf_op jit(solution)/shard_map/while
  9.3 23.6 %collective-permute-start = (bf16[2,256,768]{1,2,0:T(8,128)(2,1)S(1)}, bf16[2,256,768]{1,2,0:T(8,128)(2,1)S(1)}, u32[]{:S(2)}, u32[]{:S(2)}) collective-permute-start(bf16[2,256,768]{1,2,0:T(8,128)(2,1)S(1)} %copy.37), channel_id=1, source_target_pairs={{0,2},{2,4},{4,6},{6,8},{8,10},{10,12},{12,14},{14,0},{1,3},{3,5},... | collective-permute-start | bytes 2359304 | tf_op jit(solution)/shard_map/while/body/eval_jaxpr/ppermute | solution.py:13
  13.4 1.6 copy-start.7
  13.4 1.6 copy-start.13
  15.3 0.6 copy-start.14
  32.9 1.0 copy-start.2
  32.9 21.5 %collective-permute-start = (bf16[2,256,768]{1,2,0:T(8,128)(2,1)S(1)}, bf16[2,256,768]{1,2,0:T(8,128)(2,1)S(1)}, u32[]{:S(2)}, u32[]{:S(2)}) collective-permute-start(bf16[2,256,768]{1,2,0:T(8,128)(2,1)S(1)} %copy.37), channel_id=1, source_target_pairs={{0,2},{2,4},{4,6},{6,8},{8,10},{10,12},{12,14},{14,0},{1,3},{3,5},... | collective-permute-start | bytes 2359304 | tf_op jit(solution)/shard_map/while/body/eval_jaxpr/ppermute | solution.py:13
  34.9 1.6 copy-start.7
  34.9 1.6 copy-start.13
  36.9 0.6 copy-start.14
  54.4 1.0 copy-start.2
  54.4 20.6 %collective-permute-start = (bf16[2,256,768]{1,2,0:T(8,128)(2,1)S(1)}, bf16[2,256,768]{1,2,0:T(8,128)(2,1)S(1)}, u32[]{:S(2)}, u32[]{:S(2)}) collective-permute-start(bf16[2,256,768]{1,2,0:T(8,128)(2,1)S(1)} %copy.37), channel_id=1, source_target_pairs={{0,2},{2,4},{4,6},{6,8},{8,10},{10,12},{12,14},{14,0},{1,3},{3,5},... | collective-permute-start | bytes 2359304 | tf_op jit(solution)/shard_map/while/body/eval_jaxpr/ppermute | solution.py:13
  56.4 1.6 copy-start.7
  56.4 1.6 copy-start.13
  58.4 0.6 copy-start.14
  75.0 1.0 copy-start.2
  75.1 19.7 %collective-permute-start = (bf16[2,256,768]{1,2,0:T(8,128)(2,1)S(1)}, bf16[2,256,768]{1,2,0:T(8,128)(2,1)S(1)}, u32[]{:S(2)}, u32[]{:S(2)}) collective-permute-start(bf16[2,256,768]{1,2,0:T(8,128)(2,1)S(1)} %copy.37), channel_id=1, source_target_pairs={{0,2},{2,4},{4,6},{6,8},{8,10},{10,12},{12,14},{14,0},{1,3},{3,5},... | collective-permute-start | bytes 2359304 | tf_op jit(solution)/shard_map/while/body/eval_jaxpr/ppermute | solution.py:13
  77.1 1.6 copy-start.7
  77.1 1.6 copy-start.13
  79.0 0.6 copy-start.14
  94.8 1.0 copy-start.2
  94.9 18.9 %collective-permute-start = (bf16[2,256,768]{1,2,0:T(8,128)(2,1)S(1)}, bf16[2,256,768]{1,2,0:T(8,128)(2,1)S(1)}, u32[]{:S(2)}, u32[]{:S(2)}) collective-permute-start(bf16[2,256,768]{1,2,0:T(8,128)(2,1)S(1)} %copy.37), channel_id=1, source_target_pairs={{0,2},{2,4},{4,6},{6,8},{8,10},{10,12},{12,14},{14,0},{1,3},{3,5},... | collective-permute-start | bytes 2359304 | tf_op jit(solution)/shard_map/while/body/eval_jaxpr/ppermute | solution.py:13
  96.9 1.6 copy-start.7
  96.9 1.6 copy-start.13
  98.8 0.6 copy-start.14
  113.8 1.0 copy-start.2
  113.8 18.0 %collective-permute-start = (bf16[2,256,768]{1,2,0:T(8,128)(2,1)S(1)}, bf16[2,256,768]{1,2,0:T(8,128)(2,1)S(1)}, u32[]{:S(2)}, u32[]{:S(2)}) collective-permute-start(bf16[2,256,768]{1,2,0:T(8,128)(2,1)S(1)} %copy.37), channel_id=1, source_target_pairs={{0,2},{2,4},{4,6},{6,8},{8,10},{10,12},{12,14},{14,0},{1,3},{3,5},... | collective-permute-start | bytes 2359304 | tf_op jit(solution)/shard_map/while/body/eval_jaxpr/ppermute | solution.py:13
  115.8 1.6 copy-start.7
  115.8 1.6 copy-start.13
  117.8 0.6 copy-start.14
  131.9 1.0 copy-start.2
  131.9 17.2 %collective-permute-start = (bf16[2,256,768]{1,2,0:T(8,128)(2,1)S(1)}, bf16[2,256,768]{1,2,0:T(8,128)(2,1)S(1)}, u32[]{:S(2)}, u32[]{:S(2)}) collective-permute-start(bf16[2,256,768]{1,2,0:T(8,128)(2,1)S(1)} %copy.37), channel_id=1, source_target_pairs={{0,2},{2,4},{4,6},{6,8},{8,10},{10,12},{12,14},{14,0},{1,3},{3,5},... | collective-permute-start | bytes 2359304 | tf_op jit(solution)/shard_map/while/body/eval_jaxpr/ppermute | solution.py:13
  133.9 1.6 copy-start.7
  133.9 1.6 copy-start.13
  135.9 0.6 copy-start.14
  149.1 1.1 copy-start.6
  149.9 1.2 copy-start.1
  150.2 1.1 copy-start.8
  151.1 0.7 copy-start.15
  151.3 1.0 copy-start.12
  151.4 2.4 %copy-start.3 = (bf16[1,768,3072]{2,1,0:T(8,128)(2,1)S(1)}, bf16[1,768,3072]{2,1,0:T(8,128)(2,1)}, u32[]{:S(2)}) copy-start(bf16[1,768,3072]{2,1,0:T(8,128)(2,1)} %param.12) | copy-start | bytes 14155780
  156.4 22.5 %copy-start.11 = (bf16[1,256,3072]{2,1,0:T(8,128)(2,1)S(1)}, bf16[1,256,3072]{2,1,0:T(8,128)(2,1)}, u32[]{:S(2)}) copy-start(bf16[1,256,3072]{2,1,0:T(8,128)(2,1)} %param.8) | copy-start | bytes 4718596
  180.3 2.4 %collective-permute-start.1 = (bf16[1,256,1536]{2,1,0:T(8,128)(2,1)S(1)}, bf16[1,256,1536]{2,1,0:T(8,128)(2,1)S(1)}, u32[]{:S(2)}, u32[]{:S(2)}) collective-permute-start(bf16[1,256,1536]{2,1,0:T(8,128)(2,1)S(1)} %fusion.20), channel_id=1, source_target_pairs={{0,16},{16,0},{1,17},{17,1},{2,18},{18,2},{3,19},{19,3},{4,20},{20... | collective-permute-start | bytes 2359304 | tf_op jit(solution)/shard_map/ppermute | solution.py:13
  (7 other events, 4.1 us)
Sparse Core Ops, SparseCore 0:
  156.6 22.2 reduce-scatter.1
where the time goes:
time: 191 us; the launch traced here: 190 us
  waiting for transfers between devices  109 us (57%)
  matrix products  28.2 us (15%)
  local copies, waits for them, and re-layouts  23.3 us (12%)
  between operations  13.6 us (7%)
  other arithmetic  12.9 us (7%)
  starting transfers between devices  3.44 us (2%)
    ppermute x8, waiting for transfers between devices, passed_along(): lax.ppermute(shard, axis, [(i, (i + by) % count) for i in range(count)])  86.1 us
    reduce_scatter x1, waiting for transfers between devices, per_device(): lax.psum_scatter(partial_value.astype(jnp.bfloat16), 'head', scatter_dime...  22.4 us
    dot_general x8, matrix products, absorb(): jnp.einsum('hqk,khd->qhd', raised.astype(jnp.bfloat16), value_block, pref...  18.1 us
    while x84, local copies, waits for them, and re-layouts  15.9 us
    transpose x8, other arithmetic, absorb(): accumulated = accumulated * shrink.T[:, :, None] + mixed  9.58 us
    dot_general x8, matrix products, absorb(): jnp.einsum('qhd,khd->hqk', query_heads, key_block, preferred_element_type...  7.55 us
    unnamed x27, local copies, waits for them, and re-layouts  5.89 us
  transfers between devices with their start and end apart: 9, of which 9 were waited for; matrix products, arithmetic and copies ran while one was open for 21% of the time, Pallas kernels for 0%

commit v1 on v0

v1 whole, which is shorter than its diff:
```python
import functools
import math

import jax
import jax.numpy as jnp
from jax import lax
from jax.experimental import pallas as pl
from jax.experimental.pallas import tpu as pltpu
from jax.sharding import PartitionSpec as P


HD = 128
STATE = HD + 16
UNROLL = 8
LOG2E = 1.4426950408889634
VMEM = pl.BlockSpec(memory_space=pltpu.VMEM)


def limit(mib):
    return pltpu.CompilerParams(vmem_limit_bytes=mib << 20)


def pack_kernel(groups, k_ref, v_ref, *out_refs):
    rows = k_ref.shape[0]
    for heads, out in zip(groups, out_refs):
        for place, head in enumerate(heads):
            lanes = slice(head * HD, (head + 1) * HD)
            base = place * 2 * HD
            for piece in range(rows // HD):
                out[base : base + HD, piece * HD : (piece + 1) * HD] = k_ref[
                    piece * HD : (piece + 1) * HD, lanes
                ]
            out[base + HD : base + 2 * HD, :] = v_ref[:, lanes].T


def pack(keys, values, groups):
    rows = keys.shape[0]
    return pl.pallas_call(
        functools.partial(pack_kernel, groups),
        out_shape=tuple(
            jax.ShapeDtypeStruct((len(heads) * 2 * HD, rows), jnp.bfloat16) for heads in groups
        ),
        in_specs=[VMEM] * 2,
        out_specs=(VMEM,) * len(groups),
        compiler_params=limit(8),
        name="pack",
    )(keys, values)


def turn_kernel(x_ref, out_ref):
    for head in range(x_ref.shape[1] // HD):
        lanes = slice(head * HD, (head + 1) * HD)
        out_ref[lanes, :] = x_ref[:, lanes].T


def turned(x):
    return pl.pallas_call(
        turn_kernel,
        out_shape=jax.ShapeDtypeStruct((x.shape[1], x.shape[0]), x.dtype),
        in_specs=[VMEM],
        out_specs=VMEM,
        compiler_params=limit(8),
        name="turned",
    )(x)


def absorb_kernel(groups, first, last, *refs):
    q_ref = refs[0]
    kv_refs = refs[1 : 1 + len(groups)]
    out = refs[-1]
    state = None if first else refs[-2]
    keys = kv_refs[0].shape[1]
    factor = LOG2E / math.sqrt(HD)
    at = 0
    for kv, heads in zip(kv_refs, groups):
        for place, head in enumerate(heads):
            base = place * 2 * HD
            query = q_ref[head * HD : (head + 1) * HD, :]
            key = jnp.concatenate(
                [
                    kv[base : base + HD, piece * HD : (piece + 1) * HD]
                    for piece in range(keys // HD)
                ],
                axis=0,
            )
            scores = jnp.dot(key, query, preferred_element_type=jnp.float32)
            top = jnp.max(scores, axis=0, keepdims=True)
            if not first:
                top_old = state[at, HD + 8 : HD + 9, :]
                top = jnp.maximum(top_old, top)
            raised = jnp.exp2((scores - top) * factor).astype(jnp.bfloat16)
            value = kv[base + HD : base + 2 * HD, :]
            tall = jnp.concatenate([value, jnp.ones((16, keys), jnp.bfloat16)], axis=0)
            both = jnp.dot(tall, raised, preferred_element_type=jnp.float32)
            mixed, total = both[:HD], both[HD : HD + 8]
            if not first:
                shrink = jnp.exp2((top_old - top) * factor)
                mixed = state[at, :HD, :] * shrink + mixed
                total = state[at, HD : HD + 8, :] * shrink + total
            if last:
                done = mixed / total[:1]
                out[:, at * HD : (at + 1) * HD] = done.T.astype(jnp.bfloat16)
            else:
                out[at, :HD, :] = mixed
                out[at, HD : HD + 8, :] = total
                out[at, HD + 8 :, :] = jnp.broadcast_to(top, total.shape)
            at += 1


def absorb(query, blocks, groups, state, last):
    rows = query.shape[1]
    keys = blocks[0].shape[1]
    count = sum(len(heads) for heads in groups)
    first = state is None
    if last:
        out_shape = jax.ShapeDtypeStruct((rows, count * HD), jnp.bfloat16)
    else:
        out_shape = jax.ShapeDtypeStruct((count, STATE, rows), jnp.float32)
    operands = [query, *blocks] + ([] if first else [state])
    return pl.pallas_call(
        functools.partial(absorb_kernel, groups, first, last),
        out_shape=out_shape,
        in_specs=[VMEM] * len(operands),
        out_specs=VMEM,
        input_output_aliases={} if first or last else {len(operands) - 1: 0},
        cost_estimate=pl.CostEstimate(
            flops=4 * count * rows * keys * HD,
            bytes_accessed=count * rows * HD * 12,
            transcendentals=count * rows * keys,
        ),
        compiler_params=limit(8),
        name="absorb",
    )(*operands)


def main_kernel(plan, *refs):
    out = refs[-1]
    refs = list(refs[1:-1])
    total = None
    for layout in plan:
        pieces = [refs.pop(0) for _ in layout]
        weight = refs.pop(0)
        slots = {}
        for piece, heads in zip(pieces, layout):
            for place, head in enumerate(heads):
                slots[head] = piece[:, place * HD : (place + 1) * HD]
        order = sorted(slots)
        left = jnp.concatenate([slots[head] for head in order], axis=1)
        if len(order) * HD == weight.shape[0]:
            right = weight[...]
        else:
            right = jnp.concatenate(
                [weight[head * HD : (head + 1) * HD, :] for head in order], axis=0
            )
        term = jnp.dot(left, right, preferred_element_type=jnp.float32)
        total = term if total is None else total + term
    out[...] = total


def project_main(share, sources, wide):
    rows = sources[0][0][0].shape[0]
    cols = [s[2].shape[1] for s in sources if not s[3]]
    cols = cols[0] if cols else sources[0][2].shape[1]
    steps = cols // wide
    operands, specs, plan = [], [], []
    for pieces, layout, weight, whole in sources:
        for piece in pieces:
            operands.append(piece)
            specs.append(pl.BlockSpec(piece.shape, lambda j, s: (0, 0)))
        operands.append(weight)
        specs.append(
            pl.BlockSpec(
                (weight.shape[0], wide),
                (lambda j, s: (0, s[0] * steps + j)) if whole else (lambda j, s: (0, j)),
            )
        )
        plan.append(layout)
    return pl.pallas_call(
        functools.partial(main_kernel, plan),
        out_shape=jax.ShapeDtypeStruct((rows, cols), jnp.float32),
        grid_spec=pltpu.PrefetchScalarGridSpec(
            num_scalar_prefetch=1,
            grid=(steps,),
            in_specs=specs,
            out_specs=pl.BlockSpec((rows, wide), lambda j, s: (0, j)),
        ),
        cost_estimate=pl.CostEstimate(
            flops=4 * rows * 768 * cols, bytes_accessed=rows * cols * 4, transcendentals=0
        ),
        compiler_params=limit(12),
        name="project_main",
    )(share, *operands)


def last_kernel(counts, *refs):
    out, gate, stream, total = refs[-1], refs[-2], refs[-3], refs[-4]
    refs = list(refs[1:-4])
    branch = total[...]
    for count in counts:
        piece = refs.pop(0)
        right = jnp.concatenate([refs.pop(0)[...] for _ in range(count)], axis=0)
        branch = branch + jnp.dot(piece[...], right, preferred_element_type=jnp.float32)
    out[...] = (stream[...].astype(jnp.float32) + gate[...] * branch).astype(jnp.bfloat16)


def project_last(share, late, total, stream, gate, wide):
    rows, cols = total.shape
    steps = cols // wide
    operands, specs, counts = [], [], []
    for piece, heads, weight in late:
        operands.append(piece)
        specs.append(pl.BlockSpec(piece.shape, lambda j, s: (0, 0)))
        for head in heads:
            operands.append(weight)
            specs.append(pl.BlockSpec((HD, wide), lambda j, s, head=head: (head, j)))
        counts.append(len(heads))
    operands += [total, stream, gate]
    specs += [
        pl.BlockSpec((rows, wide), lambda j, s: (0, j)),
        pl.BlockSpec((rows, wide), lambda j, s: (0, s[0] * steps + j)),
        pl.BlockSpec((1, wide), lambda j, s: (0, s[0] * steps + j)),
    ]
    return pl.pallas_call(
        functools.partial(last_kernel, counts),
        out_shape=jax.ShapeDtypeStruct((rows, cols), jnp.bfloat16),
        grid_spec=pltpu.PrefetchScalarGridSpec(
            num_scalar_prefetch=1,
            grid=(steps,),
            in_specs=specs,
            out_specs=pl.BlockSpec((rows, wide), lambda j, s: (0, j)),
        ),
        cost_estimate=pl.CostEstimate(
            flops=2 * rows * 256 * cols, bytes_accessed=rows * cols * 8, transcendentals=0
        ),
        compiler_params=limit(12),
        name="project_last",
    )(share, *operands)


def per_device(stream_in, queries, keys, values, out_weight, gate_scale):
    sections = lax.axis_size("segment")
    seq_count = lax.axis_size("seq")
    shares = lax.axis_size("head")
    heads_dev = queries.shape[2] // HD
    cycle_len = min(32, seq_count)
    stride = seq_count // cycle_len

    ring = list(range(0, cycle_len, 2)) + list(range(1, cycle_len, 2))[::-1]
    after = {ring[at]: ring[(at + 1) % cycle_len] for at in range(cycle_len)}
    before = {target: source for source, target in after.items()}
    ways = (after, before)

    def hop(block, towards, shift):
        pairs = []
        for section in range(sections):
            for member in range(cycle_len):
                for video in range(stride):
                    pairs.append(
                        (
                            section * seq_count + member * stride + video,
                            (section + shift) % sections * seq_count
                            + towards[member] * stride
                            + video,
                        )
                    )
        return lax.ppermute(block, ("segment", "seq"), pairs)

    def next_core(block):
        return lax.ppermute(
            block, "segment", [(at, (at + 1) % sections) for at in range(sections)]
        )

    def across(block, by, shift):
        pairs = []
        for section in range(sections):
            for share in range(shares):
                pairs.append(
                    (
                        section * shares + share,
                        (section + shift) % sections * shares + (share + by) % shares,
                    )
                )
        return lax.ppermute(block, ("segment", "head"), pairs)

    half = heads_dev // 2
    early = half - max(1, half // 3)
    cuts = [(0, early), (early, half)] if early else [(0, half)]
    chains = [(tuple(range(a, b)), tuple(range(half + a, half + b))) for a, b in cuts]

    packed = pack(keys[0], values[0], [heads for chain in chains for heads in chain])
    own = [packed[2 * at : 2 * at + 2] for at in range(len(chains))]
    moving = []
    for at in range(len(chains)):
        moving.append([])
        for side, block in enumerate(own[at]):
            moving[at].append(hop(block, ways[side], 1))
    query = next_core(turned(queries[0]))
    here = [[next_core(block) for block in own[at]] for at in range(len(chains))]

    share = lax.axis_index("head")
    col_count = out_weight.shape[2] // shares
    weights = {}
    for by in range(1, shares):
        start = lax.rem(share + by, shares) * col_count
        part = lax.dynamic_slice_in_dim(out_weight[0], start, col_count, 1)
        weights[by] = across(part, by, 1)
    weights[0] = next_core(out_weight[0])
    stream = next_core(stream_in[0])
    gate = next_core(gate_scale)

    def fold(at, arrived, held, last):
        return absorb(query, arrived, chains[at], held, last)

    def send(arrived):
        sent = []
        for side, block in enumerate(arrived):
            sent.append(hop(block, ways[side], 0))
        return sent

    everyone = range(len(chains))
    state = [fold(at, here[at], None, False) for at in everyone]
    if cycle_len <= UNROLL:
        for _ in range(1, cycle_len - 1):
            for at in everyone:
                arrived = moving[at]
                moving[at] = send(arrived)
                state[at] = fold(at, arrived, state[at], False)
    else:

        def turn(_, carry):
            moving, state = carry
            onward = [send(moving[at]) for at in everyone]
            return onward, [fold(at, moving[at], state[at], False) for at in everyone]

        moving, state = lax.fori_loop(1, cycle_len - 1, turn, (moving, state))
    attended = [fold(at, moving[at], state[at], True) for at in everyone]
    others = []
    for at in range(len(chains)):
        others.append([across(attended[at], by, 0) for by in range(1, shares)])

    flat = [first + second for first, second in chains]
    sources = [(attended, flat, weights[0], True)]
    if len(chains) > 1:
        for by in range(1, shares):
            sources.append(([other[by - 1] for other in others[:-1]], flat[:-1], weights[by], False))
    share_ref = share.astype(jnp.int32).reshape(1)
    total = project_main(share_ref, sources, 512)
    late = [(others[-1][by - 1], flat[-1], weights[by]) for by in range(1, shares)]
    return project_last(share_ref, late, total, stream, gate, 512)[None]


def solution(mesh):
    return jax.shard_map(
        per_device,
        mesh=mesh,
        in_specs=(
            P("segment", "seq", None),
            P("segment", "seq", "head"),
            P("segment", "seq", "head"),
            P("segment", "seq", "head"),
            P("segment", "head", None),
            P("segment", None),
        ),
        out_specs=P("segment", "seq", "head"),
        check_vma=False,
    )
```

time: 191 us -> 117 us (0.61)
  waiting for transfers between devices: 109 us -> 46.6 us
  starting transfers between devices: 3.44 us -> 44.4 us
  matrix products: 28.2 us -> 0 us
  Pallas kernels: 0 us -> 21.8 us
  local copies, waits for them, and re-layouts: 23.3 us -> 3.82 us
  between operations: 13.6 us -> 0.24 us
  other arithmetic: 12.9 us -> 0 us
    ppermute x8 -> x39, starting transfers between devices: 3.44 us -> 44.4 us  [the longest x28 38 us: hop(): return lax.ppermute(block, ('segment', 'seq'), pairs)]
    ppermute x8 -> x39, waiting for transfers between devices: 86.1 us -> 46.6 us  [the longest x28 44.2 us: hop(): return lax.ppermute(block, ('segment', 'seq'), pairs)]
    dot_general x17 -> x0, matrix products: 28.2 us -> none  [the longest x8 18.1 us: absorb(): jnp.einsum('hqk,khd->qhd', raised.astype(jnp.bfloat16), value_block, pref...]
    reduce_scatter x1 -> x0, waiting for transfers between devices: 22.4 us -> none  [per_device(): lax.psum_scatter(partial_value.astype(jnp.bfloat16), 'head', scatter_dime...]
    pallas_call x0 -> x20, Pallas kernels: none -> 21.8 us  [the longest x16 16 us: absorb(): pl.pallas_call(functools.partial(absorb_kernel, groups, first, last), out...]
    while x85 -> x0, local copies, waits for them, and re-layouts: 16.2 us -> none
    transpose x9 -> x0, other arithmetic: 9.59 us -> none  [the longest x8 9.58 us: absorb(): accumulated = accumulated * shrink.T[:, :, None] + mixed]
    unnamed x27 -> x10, local copies, waits for them, and re-layouts: 5.89 us -> 2 us
  transfers between devices with their start and end apart: 9 -> 39, of which waited for: 9 -> 17; matrix products, arithmetic and copies ran while one was open for 21% -> 2% of each run, Pallas kernels for 0% -> 17%
where the time goes in v1:
time: 117 us
  waiting for transfers between devices  46.6 us (40%)
  starting transfers between devices  44.4 us (38%)
  Pallas kernels  21.8 us (19%)
  local copies, waits for them, and re-layouts  3.82 us (3%)
    ppermute x28, waiting for transfers between devices, hop(): return lax.ppermute(block, ('segment', 'seq'), pairs)  44.2 us
    ppermute x28, starting transfers between devices, hop(): return lax.ppermute(block, ('segment', 'seq'), pairs)  38 us
    pallas_call x16, Pallas kernels, absorb(): pl.pallas_call(functools.partial(absorb_kernel, groups, first, last), out...  16 us
    ppermute x3, starting transfers between devices, across(): return lax.ppermute(block, ('segment', 'head'), pairs)  4.15 us
    pallas_call x1, Pallas kernels, project_main(): pl.pallas_call(functools.partial(main_kernel, plan), out_shape=jax.ShapeD...  3.4 us
    ppermute x8, waiting for transfers between devices, next_core(): lax.ppermute(block, 'segment', [(at, (at + 1) % sections) for at in range...  2.47 us
  transfers between devices with their start and end apart: 39, of which 17 were waited for; matrix products, arithmetic and copies ran while one was open for 2% of the time, Pallas kernels for 17%

profile of v1, /device:TPU:0, one launch (start us, length us, event | category | flops | bytes accessed | tf_op | source)
XLA Modules:
  0.0 116.9 jit_solution(18418845389998984003)
XLA Ops:
  3.3 2.7 %collective-permute-start.1 = (bf16[256,256]{1,0:T(8,128)(2,1)S(1)}, bf16[256,256]{1,0:T(8,128)(2,1)S(1)}, u32[]{:S(2)}, u32[]{:S(2)}) collective-permute-start(bf16[256,256]{1,0:T(8,128)(2,1)S(1)} %get-tuple-element.9), channel_id=1, source_target_pairs={{0,20},{2,16},{4,24},{6,18},{8,28},{10,22},{12,30},{14,26},{16,4},... | collective-permute-start | bytes 393224 | tf_op jit(solution)/shard_map/ppermute | solution.py:266
  6.0 2.5 %collective-permute-done.15.refs_1_ = bf16[256,256]{1,0:T(8,128)(2,1)S(1)} collective-permute-done((bf16[256,256]{1,0:T(8,128)(2,1)S(1)}, bf16[256,256]{1,0:T(8,128)(2,1)S(1)}, u32[]{:S(2)}, u32[]{:S(2)}) %collective-permute-start.15) | collective-permute-done | bytes 131104 | tf_op jit(solution)/shard_map/ppermute | solution.py:269
  8.4 2.6 %collective-permute-start.8 = (bf16[256,256]{1,0:T(8,128)(2,1)S(1)}, bf16[256,256]{1,0:T(8,128)(2,1)S(1)}, u32[]{:S(2)}, u32[]{:S(2)}) collective-permute-start(bf16[256,256]{1,0:T(8,128)(2,1)S(1)} %get-tuple-element.10), channel_id=1, source_target_pairs={{0,18},{2,22},{4,16},{6,26},{8,20},{10,30},{12,24},{14,28},{16,2},... | collective-permute-start | bytes 393224 | tf_op jit(solution)/shard_map/ppermute | solution.py:266
  12.0 2.6 %collective-permute-done.8.refs_2_ = bf16[256,256]{1,0:T(8,128)(2,1)S(1)} collective-permute-done((bf16[256,256]{1,0:T(8,128)(2,1)S(1)}, bf16[256,256]{1,0:T(8,128)(2,1)S(1)}, u32[]{:S(2)}, u32[]{:S(2)}) %collective-permute-start.8) | collective-permute-done | bytes 131104 | tf_op jit(solution)/shard_map/ppermute | solution.py:266
  14.6 2.2 %collective-permute-start.26 = (bf16[512,256]{1,0:T(8,128)(2,1)S(1)}, bf16[512,256]{1,0:T(8,128)(2,1)S(1)}, u32[]{:S(2)}, u32[]{:S(2)}) collective-permute-start(bf16[512,256]{1,0:T(8,128)(2,1)S(1)} %get-tuple-element.12), channel_id=1, source_target_pairs={{0,18},{2,22},{4,16},{6,26},{8,20},{10,30},{12,24},{14,28},{16,2},... | collective-permute-start | bytes 786440 | tf_op jit(solution)/shard_map/ppermute | solution.py:266
  16.8 1.6 %collective-permute-start.9 = (bf16[256,256]{1,0:T(8,128)(2,1)S(1)}, bf16[256,256]{1,0:T(8,128)(2,1)S(1)}, u32[]{:S(2)}, u32[]{:S(2)}) collective-permute-start(bf16[256,256]{1,0:T(8,128)(2,1)S(1)} %collective-permute-done.8.refs_2_), channel_id=1, source_target_pairs={{0,2},{2,6},{4,0},{6,10},{8,4},{10,14},{12,8},{14,12},{16,18},{18,... | collective-permute-start | bytes 393224 | tf_op jit(solution)/shard_map/ppermute | solution.py:266
  18.4 1.8 %dynamic-slice_bitcast_fusion = bf16[768,1536]{1,0:T(8,128)(2,1)S(1)} fusion(bf16[1,768,3072]{2,1,0:T(8,128)(2,1)} %param.10, s32[]{:T(128)S(6)} %select_n.3), kind=kLoop, calls=%fused_computation | loop fusion | bytes 4718596 | tf_op jit(solution)/shard_map/dynamic_slice | solution.py:305
  22.1 1.3 %collective-permute-done.26.refs_2_ = bf16[512,256]{1,0:T(8,128)(2,1)S(1)} collective-permute-done((bf16[512,256]{1,0:T(8,128)(2,1)S(1)}, bf16[512,256]{1,0:T(8,128)(2,1)S(1)}, u32[]{:S(2)}, u32[]{:S(2)}) %collective-permute-start.26) | collective-permute-done | bytes 262176 | tf_op jit(solution)/shard_map/ppermute | solution.py:266
  23.5 1.3 %collective-permute-start.2 = (bf16[256,256]{1,0:T(8,128)(2,1)S(1)}, bf16[256,256]{1,0:T(8,128)(2,1)S(1)}, u32[]{:S(2)}, u32[]{:S(2)}) collective-permute-start(bf16[256,256]{1,0:T(8,128)(2,1)S(1)} %collective-permute-done.1.refs_1_), channel_id=1, source_target_pairs={{0,4},{2,0},{4,8},{6,2},{8,12},{10,6},{12,14},{14,10},{16,20},{18,... | collective-permute-start | bytes 393224 | tf_op jit(solution)/shard_map/ppermute | solution.py:266
  24.8 1.7 %collective-permute-done.9.refs_2_ = bf16[256,256]{1,0:T(8,128)(2,1)S(1)} collective-permute-done((bf16[256,256]{1,0:T(8,128)(2,1)S(1)}, bf16[256,256]{1,0:T(8,128)(2,1)S(1)}, u32[]{:S(2)}, u32[]{:S(2)}) %collective-permute-start.9) | collective-permute-done | bytes 131104 | tf_op jit(solution)/shard_map/ppermute | solution.py:266
  26.6 1.6 %collective-permute-start.10 = (bf16[256,256]{1,0:T(8,128)(2,1)S(1)}, bf16[256,256]{1,0:T(8,128)(2,1)S(1)}, u32[]{:S(2)}, u32[]{:S(2)}) collective-permute-start(bf16[256,256]{1,0:T(8,128)(2,1)S(1)} %collective-permute-done.9.refs_2_), channel_id=1, source_target_pairs={{0,2},{2,6},{4,0},{6,10},{8,4},{10,14},{12,8},{14,12},{16,18},{18,... | collective-permute-start | bytes 393224 | tf_op jit(solution)/shard_map/ppermute | solution.py:266
  28.2 1.6 %collective-permute-done.2.refs_1_ = bf16[256,256]{1,0:T(8,128)(2,1)S(1)} collective-permute-done((bf16[256,256]{1,0:T(8,128)(2,1)S(1)}, bf16[256,256]{1,0:T(8,128)(2,1)S(1)}, u32[]{:S(2)}, u32[]{:S(2)}) %collective-permute-start.2) | collective-permute-done | bytes 131104 | tf_op jit(solution)/shard_map/ppermute | solution.py:266
  31.8 1.5 %collective-permute-start.20 = (bf16[512,256]{1,0:T(8,128)(2,1)S(1)}, bf16[512,256]{1,0:T(8,128)(2,1)S(1)}, u32[]{:S(2)}, u32[]{:S(2)}) collective-permute-start(bf16[512,256]{1,0:T(8,128)(2,1)S(1)} %collective-permute-done.19.refs_1_), channel_id=1, source_target_pairs={{0,4},{2,0},{4,8},{6,2},{8,12},{10,6},{12,14},{14,10},{16,20},{18,... | collective-permute-start | bytes 786440 | tf_op jit(solution)/shard_map/ppermute | solution.py:266
  33.2 2.9 %collective-permute-done.3.refs_1_ = bf16[256,256]{1,0:T(8,128)(2,1)S(1)} collective-permute-done((bf16[256,256]{1,0:T(8,128)(2,1)S(1)}, bf16[256,256]{1,0:T(8,128)(2,1)S(1)}, u32[]{:S(2)}, u32[]{:S(2)}) %collective-permute-start.3) | collective-permute-done | bytes 131104 | tf_op jit(solution)/shard_map/ppermute | solution.py:266
  36.1 1.6 %collective-permute-start.27 = (bf16[512,256]{1,0:T(8,128)(2,1)S(1)}, bf16[512,256]{1,0:T(8,128)(2,1)S(1)}, u32[]{:S(2)}, u32[]{:S(2)}) collective-permute-start(bf16[512,256]{1,0:T(8,128)(2,1)S(1)} %collective-permute-done.26.refs_2_), channel_id=1, source_target_pairs={{0,2},{2,6},{4,0},{6,10},{8,4},{10,14},{12,8},{14,12},{16,18},{18,... | collective-permute-start | bytes 786440 | tf_op jit(solution)/shard_map/ppermute | solution.py:266
  37.8 1.6 %collective-permute-start.11 = (bf16[256,256]{1,0:T(8,128)(2,1)S(1)}, bf16[256,256]{1,0:T(8,128)(2,1)S(1)}, u32[]{:S(2)}, u32[]{:S(2)}) collective-permute-start(bf16[256,256]{1,0:T(8,128)(2,1)S(1)} %collective-permute-done.10.refs_2_), channel_id=1, source_target_pairs={{0,2},{2,6},{4,0},{6,10},{8,4},{10,14},{12,8},{14,12},{16,18},{18,... | collective-permute-start | bytes 393224 | tf_op jit(solution)/shard_map/ppermute | solution.py:266
  39.3 1.5 %collective-permute-done.20.refs_1_ = bf16[512,256]{1,0:T(8,128)(2,1)S(1)} collective-permute-done((bf16[512,256]{1,0:T(8,128)(2,1)S(1)}, bf16[512,256]{1,0:T(8,128)(2,1)S(1)}, u32[]{:S(2)}, u32[]{:S(2)}) %collective-permute-start.20) | collective-permute-done | bytes 262176 | tf_op jit(solution)/shard_map/ppermute | solution.py:266
  40.8 1.5 %collective-permute-start.4 = (bf16[256,256]{1,0:T(8,128)(2,1)S(1)}, bf16[256,256]{1,0:T(8,128)(2,1)S(1)}, u32[]{:S(2)}, u32[]{:S(2)}) collective-permute-start(bf16[256,256]{1,0:T(8,128)(2,1)S(1)} %collective-permute-done.3.refs_1_), channel_id=1, source_target_pairs={{0,4},{2,0},{4,8},{6,2},{8,12},{10,6},{12,14},{14,10},{16,20},{18,... | collective-permute-start | bytes 393224 | tf_op jit(solution)/shard_map/ppermute | solution.py:266
  42.3 3.3 %collective-permute-done.11.refs_2_ = bf16[256,256]{1,0:T(8,128)(2,1)S(1)} collective-permute-done((bf16[256,256]{1,0:T(8,128)(2,1)S(1)}, bf16[256,256]{1,0:T(8,128)(2,1)S(1)}, u32[]{:S(2)}, u32[]{:S(2)}) %collective-permute-start.11) | collective-permute-done | bytes 131104 | tf_op jit(solution)/shard_map/ppermute | solution.py:266
  45.6 1.7 %collective-permute-start.12 = (bf16[256,256]{1,0:T(8,128)(2,1)S(1)}, bf16[256,256]{1,0:T(8,128)(2,1)S(1)}, u32[]{:S(2)}, u32[]{:S(2)}) collective-permute-start(bf16[256,256]{1,0:T(8,128)(2,1)S(1)} %collective-permute-done.11.refs_2_), channel_id=1, source_target_pairs={{0,2},{2,6},{4,0},{6,10},{8,4},{10,14},{12,8},{14,12},{16,18},{18,... | collective-permute-start | bytes 393224 | tf_op jit(solution)/shard_map/ppermute | solution.py:266
  47.7 1.7 %collective-permute-start.28 = (bf16[512,256]{1,0:T(8,128)(2,1)S(1)}, bf16[512,256]{1,0:T(8,128)(2,1)S(1)}, u32[]{:S(2)}, u32[]{:S(2)}) collective-permute-start(bf16[512,256]{1,0:T(8,128)(2,1)S(1)} %collective-permute-done.27.refs_2_), channel_id=1, source_target_pairs={{0,2},{2,6},{4,0},{6,10},{8,4},{10,14},{12,8},{14,12},{16,18},{18,... | collective-permute-start | bytes 786440 | tf_op jit(solution)/shard_map/ppermute | solution.py:266
  49.3 2.7 %collective-permute-done.12.refs_2_ = bf16[256,256]{1,0:T(8,128)(2,1)S(1)} collective-permute-done((bf16[256,256]{1,0:T(8,128)(2,1)S(1)}, bf16[256,256]{1,0:T(8,128)(2,1)S(1)}, u32[]{:S(2)}, u32[]{:S(2)}) %collective-permute-start.12) | collective-permute-done | bytes 131104 | tf_op jit(solution)/shard_map/ppermute | solution.py:266
  52.0 1.7 %collective-permute-start.5 = (bf16[256,256]{1,0:T(8,128)(2,1)S(1)}, bf16[256,256]{1,0:T(8,128)(2,1)S(1)}, u32[]{:S(2)}, u32[]{:S(2)}) collective-permute-start(bf16[256,256]{1,0:T(8,128)(2,1)S(1)} %collective-permute-done.4.refs_1_), channel_id=1, source_target_pairs={{0,4},{2,0},{4,8},{6,2},{8,12},{10,6},{12,14},{14,10},{16,20},{18,... | collective-permute-start | bytes 393224 | tf_op jit(solution)/shard_map/ppermute | solution.py:266
  53.8 3.2 %collective-permute-done.5.refs_1_ = bf16[256,256]{1,0:T(8,128)(2,1)S(1)} collective-permute-done((bf16[256,256]{1,0:T(8,128)(2,1)S(1)}, bf16[256,256]{1,0:T(8,128)(2,1)S(1)}, u32[]{:S(2)}, u32[]{:S(2)}) %collective-permute-start.5) | collective-permute-done | bytes 131104 | tf_op jit(solution)/shard_map/ppermute | solution.py:266
  57.0 1.2 %collective-permute-start.13 = (bf16[256,256]{1,0:T(8,128)(2,1)S(1)}, bf16[256,256]{1,0:T(8,128)(2,1)S(1)}, u32[]{:S(2)}, u32[]{:S(2)}) collective-permute-start(bf16[256,256]{1,0:T(8,128)(2,1)S(1)} %collective-permute-done.12.refs_2_), channel_id=1, source_target_pairs={{0,2},{2,6},{4,0},{6,10},{8,4},{10,14},{12,8},{14,12},{16,18},{18,... | collective-permute-start | bytes 393224 | tf_op jit(solution)/shard_map/ppermute | solution.py:266
  59.1 3.0 %collective-permute-done.13.refs_2_ = bf16[256,256]{1,0:T(8,128)(2,1)S(1)} collective-permute-done((bf16[256,256]{1,0:T(8,128)(2,1)S(1)}, bf16[256,256]{1,0:T(8,128)(2,1)S(1)}, u32[]{:S(2)}, u32[]{:S(2)}) %collective-permute-start.13) | collective-permute-done | bytes 131104 | tf_op jit(solution)/shard_map/ppermute | solution.py:266
  62.0 1.2 %collective-permute-start.29 = (bf16[512,256]{1,0:T(8,128)(2,1)S(1)}, bf16[512,256]{1,0:T(8,128)(2,1)S(1)}, u32[]{:S(2)}, u32[]{:S(2)}) collective-permute-start(bf16[512,256]{1,0:T(8,128)(2,1)S(1)} %collective-permute-done.28.refs_2_), channel_id=1, source_target_pairs={{0,2},{2,6},{4,0},{6,10},{8,4},{10,14},{12,8},{14,12},{16,18},{18,... | collective-permute-start | bytes 786440 | tf_op jit(solution)/shard_map/ppermute | solution.py:266
  63.3 3.7 %collective-permute-done.22.refs_1_ = bf16[512,256]{1,0:T(8,128)(2,1)S(1)} collective-permute-done((bf16[512,256]{1,0:T(8,128)(2,1)S(1)}, bf16[512,256]{1,0:T(8,128)(2,1)S(1)}, u32[]{:S(2)}, u32[]{:S(2)}) %collective-permute-start.22) | collective-permute-done | bytes 262176 | tf_op jit(solution)/shard_map/ppermute | solution.py:266
  68.4 1.2 %collective-permute-start.30 = (bf16[512,256]{1,0:T(8,128)(2,1)S(1)}, bf16[512,256]{1,0:T(8,128)(2,1)S(1)}, u32[]{:S(2)}, u32[]{:S(2)}) collective-permute-start(bf16[512,256]{1,0:T(8,128)(2,1)S(1)} %collective-permute-done.29.refs_2_), channel_id=1, source_target_pairs={{0,2},{2,6},{4,0},{6,10},{8,4},{10,14},{12,8},{14,12},{16,18},{18,... | collective-permute-start | bytes 786440 | tf_op jit(solution)/shard_map/ppermute | solution.py:266
  69.6 5.4 %collective-permute-done.23.refs_1_ = bf16[512,256]{1,0:T(8,128)(2,1)S(1)} collective-permute-done((bf16[512,256]{1,0:T(8,128)(2,1)S(1)}, bf16[512,256]{1,0:T(8,128)(2,1)S(1)}, u32[]{:S(2)}, u32[]{:S(2)}) %collective-permute-start.23) | collective-permute-done | bytes 262176 | tf_op jit(solution)/shard_map/ppermute | solution.py:266
  75.5 1.6 %collective-permute-start.31 = (bf16[512,256]{1,0:T(8,128)(2,1)S(1)}, bf16[512,256]{1,0:T(8,128)(2,1)S(1)}, u32[]{:S(2)}, u32[]{:S(2)}) collective-permute-start(bf16[512,256]{1,0:T(8,128)(2,1)S(1)} %collective-permute-done.30.refs_2_), channel_id=1, source_target_pairs={{0,2},{2,6},{4,0},{6,10},{8,4},{10,14},{12,8},{14,12},{16,18},{18,... | collective-permute-start | bytes 786440 | tf_op jit(solution)/shard_map/ppermute | solution.py:266
  77.1 5.3 %collective-permute-done.24.refs_1_ = bf16[512,256]{1,0:T(8,128)(2,1)S(1)} collective-permute-done((bf16[512,256]{1,0:T(8,128)(2,1)S(1)}, bf16[512,256]{1,0:T(8,128)(2,1)S(1)}, u32[]{:S(2)}, u32[]{:S(2)}) %collective-permute-start.24) | collective-permute-done | bytes 262176 | tf_op jit(solution)/shard_map/ppermute | solution.py:266
  82.7 1.7 %collective-permute-start.32 = (bf16[512,256]{1,0:T(8,128)(2,1)S(1)}, bf16[512,256]{1,0:T(8,128)(2,1)S(1)}, u32[]{:S(2)}, u32[]{:S(2)}) collective-permute-start(bf16[512,256]{1,0:T(8,128)(2,1)S(1)} %collective-permute-done.31.refs_2_), channel_id=1, source_target_pairs={{0,2},{2,6},{4,0},{6,10},{8,4},{10,14},{12,8},{14,12},{16,18},{18,... | collective-permute-start | bytes 786440 | tf_op jit(solution)/shard_map/ppermute | solution.py:266
  84.4 4.4 %collective-permute-done.25.refs_1_ = bf16[512,256]{1,0:T(8,128)(2,1)S(1)} collective-permute-done((bf16[512,256]{1,0:T(8,128)(2,1)S(1)}, bf16[512,256]{1,0:T(8,128)(2,1)S(1)}, u32[]{:S(2)}, u32[]{:S(2)}) %collective-permute-start.25) | collective-permute-done | bytes 262176 | tf_op jit(solution)/shard_map/ppermute | solution.py:266
  89.1 1.2 %absorb.24.refs_3_ = f32[4,144,256]{2,1,0:T(8,128)S(1)} custom-call(bf16[768,256]{1,0:T(8,128)(2,1)S(1)} %collective-permute-done.refs_0_, bf16[512,256]{1,0:T(8,128)(2,1)S(1)} %collective-permute-done.33.refs_1_, bf16[512,256]{1,0:T(8,128)(2,1)S(1)} %collective-permute-done.34.refs_2_), custom_call_target="tpu_custom_call" | custom-call | flops 134217728 | bytes 1572864 | tf_op jit(solution)/shard_map/absorb/pallas_call | solution.py:120
  90.4 1.3 %absorb.25.refs_3_ = f32[4,144,256]{2,1,0:T(8,128)S(1)} custom-call(bf16[768,256]{1,0:T(8,128)(2,1)S(1)} %collective-permute-done.refs_0_, bf16[512,256]{1,0:T(8,128)(2,1)S(1)} %collective-permute-done.19.refs_1_, bf16[512,256]{1,0:T(8,128)(2,1)S(1)} %collective-permute-done.26.refs_2_, ...), custom_call_target="tpu_custom_call", output_to_operand_aliasing={{}: (3, {})} | custom-call | flops 134217728 | bytes 1572864 | tf_op jit(solution)/shard_map/absorb/pallas_call | solution.py:120
  91.7 1.3 %absorb.26.refs_3_ = f32[4,144,256]{2,1,0:T(8,128)S(1)} custom-call(bf16[768,256]{1,0:T(8,128)(2,1)S(1)} %collective-permute-done.refs_0_, bf16[512,256]{1,0:T(8,128)(2,1)S(1)} %collective-permute-done.20.refs_1_, bf16[512,256]{1,0:T(8,128)(2,1)S(1)} %collective-permute-done.27.refs_2_, ...), custom_call_target="tpu_custom_call", output_to_operand_aliasing={{}: (3, {})} | custom-call | flops 134217728 | bytes 1572864 | tf_op jit(solution)/shard_map/absorb/pallas_call | solution.py:120
  92.9 1.3 %absorb.27.refs_3_ = f32[4,144,256]{2,1,0:T(8,128)S(1)} custom-call(bf16[768,256]{1,0:T(8,128)(2,1)S(1)} %collective-permute-done.refs_0_, bf16[512,256]{1,0:T(8,128)(2,1)S(1)} %collective-permute-done.21.refs_1_, bf16[512,256]{1,0:T(8,128)(2,1)S(1)} %collective-permute-done.28.refs_2_, ...), custom_call_target="tpu_custom_call", output_to_operand_aliasing={{}: (3, {})} | custom-call | flops 134217728 | bytes 1572864 | tf_op jit(solution)/shard_map/absorb/pallas_call | solution.py:120
  94.2 1.3 %absorb.28.refs_3_ = f32[4,144,256]{2,1,0:T(8,128)S(1)} custom-call(bf16[768,256]{1,0:T(8,128)(2,1)S(1)} %collective-permute-done.refs_0_, bf16[512,256]{1,0:T(8,128)(2,1)S(1)} %collective-permute-done.22.refs_1_, bf16[512,256]{1,0:T(8,128)(2,1)S(1)} %collective-permute-done.29.refs_2_, ...), custom_call_target="tpu_custom_call", output_to_operand_aliasing={{}: (3, {})} | custom-call | flops 134217728 | bytes 1572864 | tf_op jit(solution)/shard_map/absorb/pallas_call | solution.py:120
  95.5 1.3 %absorb.29.refs_3_ = f32[4,144,256]{2,1,0:T(8,128)S(1)} custom-call(bf16[768,256]{1,0:T(8,128)(2,1)S(1)} %collective-permute-done.refs_0_, bf16[512,256]{1,0:T(8,128)(2,1)S(1)} %collective-permute-done.23.refs_1_, bf16[512,256]{1,0:T(8,128)(2,1)S(1)} %collective-permute-done.30.refs_2_, ...), custom_call_target="tpu_custom_call", output_to_operand_aliasing={{}: (3, {})} | custom-call | flops 134217728 | bytes 1572864 | tf_op jit(solution)/shard_map/absorb/pallas_call | solution.py:120
  96.8 1.8 %collective-permute-start.14 = (bf16[256,256]{1,0:T(8,128)(2,1)S(1)}, bf16[256,256]{1,0:T(8,128)(2,1)S(1)}, u32[]{:S(2)}, u32[]{:S(2)}) collective-permute-start(bf16[256,256]{1,0:T(8,128)(2,1)S(1)} %collective-permute-done.13.refs_2_), channel_id=1, source_target_pairs={{0,2},{2,6},{4,0},{6,10},{8,4},{10,14},{12,8},{14,12},{16,18},{18,... | collective-permute-start | bytes 393224 | tf_op jit(solution)/shard_map/ppermute | solution.py:266
  98.6 1.3 %absorb.30.refs_3_ = f32[4,144,256]{2,1,0:T(8,128)S(1)} custom-call(bf16[768,256]{1,0:T(8,128)(2,1)S(1)} %collective-permute-done.refs_0_, bf16[512,256]{1,0:T(8,128)(2,1)S(1)} %collective-permute-done.24.refs_1_, bf16[512,256]{1,0:T(8,128)(2,1)S(1)} %collective-permute-done.31.refs_2_, ...), custom_call_target="tpu_custom_call", output_to_operand_aliasing={{}: (3, {})} | custom-call | flops 134217728 | bytes 1572864 | tf_op jit(solution)/shard_map/absorb/pallas_call | solution.py:120
  99.8 1.4 %absorb.31.refs_1_ = bf16[256,512]{1,0:T(8,128)(2,1)S(1)} custom-call(bf16[768,256]{1,0:T(8,128)(2,1)S(1)} %collective-permute-done.refs_0_, bf16[512,256]{1,0:T(8,128)(2,1)S(1)} %collective-permute-done.25.refs_1_, bf16[512,256]{1,0:T(8,128)(2,1)S(1)} %collective-permute-done.32.refs_2_, f32[4,144,256]{2,1,0:T(8,128)S(1)} %absorb.30.refs_3_), custom_call_target="tpu_custom_call" | custom-call | flops 134217728 | bytes 1572864 | tf_op jit(solution)/shard_map/absorb/pallas_call | solution.py:120
  101.2 1.6 %collective-permute-start.36 = (bf16[256,512]{1,0:T(8,128)(2,1)S(1)}, bf16[256,512]{1,0:T(8,128)(2,1)S(1)}, u32[]{:S(2)}, u32[]{:S(2)}) collective-permute-start(bf16[256,512]{1,0:T(8,128)(2,1)S(1)} %absorb.31.refs_1_), channel_id=1, source_target_pairs={{0,1},{1,0},{16,17},{17,16},{2,3},{3,2},{18,19},{19,18},{4,5},{5,4... | collective-permute-start | bytes 786440 | tf_op jit(solution)/shard_map/ppermute | solution.py:283
  102.8 1.1 collective-permute-start.7
  109.8 1.6 %collective-permute-start.17 = (bf16[256,256]{1,0:T(8,128)(2,1)S(1)}, bf16[256,256]{1,0:T(8,128)(2,1)S(1)}, u32[]{:S(2)}, u32[]{:S(2)}) collective-permute-start(bf16[256,256]{1,0:T(8,128)(2,1)S(1)} %absorb.23.refs_2_), channel_id=1, source_target_pairs={{0,1},{1,0},{16,17},{17,16},{2,3},{3,2},{18,19},{19,18},{4,5},{5,4... | collective-permute-start | bytes 393224 | tf_op jit(solution)/shard_map/ppermute | solution.py:283
  111.4 3.4 %project_main.1.refs_4_ = f32[256,1536]{1,0:T(8,128)S(1)} custom-call(s32[1]{0:T(128)} %bitcast.refs_0_, bf16[256,512]{1,0:T(8,128)(2,1)S(1)} %absorb.31.refs_1_, bf16[256,256]{1,0:T(8,128)(2,1)S(1)} %absorb.23.refs_2_, bf16[768,3072]{1,0:T(8,128)(2,1)} %collective-permute-done.35.refs_3_, bf16[256,512]{1,0:T(8,128)(2,1)S(1)} %collective-permute-done.36.refs_4_, ...), custom_call_target="tpu_custom_call" | custom-call | flops 1207959552 | bytes 1572864 | tf_op jit(solution)/shard_map/project_main/pallas_call | solution.py:178
  114.8 2.1 %project_last.1 = bf16[256,1536]{1,0:T(8,128)(2,1)} custom-call(s32[1]{0:T(128)} %bitcast.refs_0_, bf16[256,256]{1,0:T(8,128)(2,1)S(1)} %collective-permute-done.17.refs_1_, bf16[768,1536]{1,0:T(8,128)(2,1)S(1)} %collective-permute-done.18.refs_5_.refs_2_.refs_3_, bf16[768,1536]{1,0:T(8,128)(2,1)S(1)} %collective-permute-done.18.refs_5_.refs_2_.refs_3_, ...), custom_call_target="tpu_custom_call" | custom-call | flops 201326592 | bytes 3145728 | tf_op jit(solution)/shard_map/project_last/pallas_call | solution.py:223
  (61 shorter events, 17.8 us)
Async XLA Ops:
  0.0 111.4 %collective-permute-start.35 = (bf16[768,3072]{1,0:T(8,128)(2,1)}, bf16[768,3072]{1,0:T(8,128)(2,1)}, u32[]{:S(2)}, u32[]{:S(2)}) collective-permute-start(bf16[768,3072]{1,0:T(8,128)(2,1)} %bitcast.12), channel_id=1, source_target_pairs={{0,16},{16,0},{1,17},{17,1},{2,18},{18,2},{3,19},{19,3},{4,20},{20... | collective-permute-start | bytes 14155784 | tf_op jit(solution)/shard_map/ppermute | solution.py:269
  0.5 1.0 copy-start
  1.5 1.0 copy-start.1
  2.6 5.8 %collective-permute-start.15 = (bf16[256,256]{1,0:T(8,128)(2,1)S(1)}, bf16[256,256]{1,0:T(8,128)(2,1)S(1)}, u32[]{:S(2)}, u32[]{:S(2)}) collective-permute-start(bf16[256,256]{1,0:T(8,128)(2,1)S(1)} %get-tuple-element.9), channel_id=1, source_target_pairs={{0,16},{16,0},{1,17},{17,1},{2,18},{18,2},{3,19},{19,3},{4,20},{20... | collective-permute-start | bytes 393224 | tf_op jit(solution)/shard_map/ppermute | solution.py:269
  2.7 14.1 %collective-permute-start.33 = (bf16[512,256]{1,0:T(8,128)(2,1)S(1)}, bf16[512,256]{1,0:T(8,128)(2,1)S(1)}, u32[]{:S(2)}, u32[]{:S(2)}) collective-permute-start(bf16[512,256]{1,0:T(8,128)(2,1)S(1)} %get-tuple-element.11), channel_id=1, source_target_pairs={{0,16},{16,0},{1,17},{17,1},{2,18},{18,2},{3,19},{19,3},{4,20},{20... | collective-permute-start | bytes 786440 | tf_op jit(solution)/shard_map/ppermute | solution.py:269
  3.2 7.8 %collective-permute-start.16 = (bf16[256,256]{1,0:T(8,128)(2,1)S(1)}, bf16[256,256]{1,0:T(8,128)(2,1)S(1)}, u32[]{:S(2)}, u32[]{:S(2)}) collective-permute-start(bf16[256,256]{1,0:T(8,128)(2,1)S(1)} %get-tuple-element.10), channel_id=1, source_target_pairs={{0,16},{16,0},{1,17},{17,1},{2,18},{18,2},{3,19},{19,3},{4,20},{20... | collective-permute-start | bytes 393224 | tf_op jit(solution)/shard_map/ppermute | solution.py:269
  3.3 8.4 %collective-permute-start.1 = (bf16[256,256]{1,0:T(8,128)(2,1)S(1)}, bf16[256,256]{1,0:T(8,128)(2,1)S(1)}, u32[]{:S(2)}, u32[]{:S(2)}) collective-permute-start(bf16[256,256]{1,0:T(8,128)(2,1)S(1)} %get-tuple-element.9), channel_id=1, source_target_pairs={{0,20},{2,16},{4,24},{6,18},{8,28},{10,22},{12,30},{14,26},{16,4},... | collective-permute-start | bytes 393224 | tf_op jit(solution)/shard_map/ppermute | solution.py:266
  8.4 6.2 %collective-permute-start.8 = (bf16[256,256]{1,0:T(8,128)(2,1)S(1)}, bf16[256,256]{1,0:T(8,128)(2,1)S(1)}, u32[]{:S(2)}, u32[]{:S(2)}) collective-permute-start(bf16[256,256]{1,0:T(8,128)(2,1)S(1)} %get-tuple-element.10), channel_id=1, source_target_pairs={{0,18},{2,22},{4,16},{6,26},{8,20},{10,30},{12,24},{14,28},{16,2},... | collective-permute-start | bytes 393224 | tf_op jit(solution)/shard_map/ppermute | solution.py:266
  11.0 10.3 %collective-permute-start.19 = (bf16[512,256]{1,0:T(8,128)(2,1)S(1)}, bf16[512,256]{1,0:T(8,128)(2,1)S(1)}, u32[]{:S(2)}, u32[]{:S(2)}) collective-permute-start(bf16[512,256]{1,0:T(8,128)(2,1)S(1)} %get-tuple-element.11), channel_id=1, source_target_pairs={{0,20},{2,16},{4,24},{6,18},{8,28},{10,22},{12,30},{14,26},{16,4},... | collective-permute-start | bytes 786440 | tf_op jit(solution)/shard_map/ppermute | solution.py:266
  11.7 9.5 %copy-start.2 = (bf16[1,256,768]{2,1,0:T(8,128)(2,1)S(1)}, bf16[1,256,768]{2,1,0:T(8,128)(2,1)}, u32[]{:S(2)}) copy-start(bf16[1,256,768]{2,1,0:T(8,128)(2,1)} %param.7) | copy-start | bytes 1179652
  11.7 46.5 %copy-start.3 = (bf16[1,256,3072]{2,1,0:T(8,128)(2,1)S(1)}, bf16[1,256,3072]{2,1,0:T(8,128)(2,1)}, u32[]{:S(2)}) copy-start(bf16[1,256,3072]{2,1,0:T(8,128)(2,1)} %param.6) | copy-start | bytes 4718596
  11.7 8.5 %collective-permute-start.34 = (bf16[512,256]{1,0:T(8,128)(2,1)S(1)}, bf16[512,256]{1,0:T(8,128)(2,1)S(1)}, u32[]{:S(2)}, u32[]{:S(2)}) collective-permute-start(bf16[512,256]{1,0:T(8,128)(2,1)S(1)} %get-tuple-element.12), channel_id=1, source_target_pairs={{0,16},{16,0},{1,17},{17,1},{2,18},{18,2},{3,19},{19,3},{4,20},{20... | collective-permute-start | bytes 786440 | tf_op jit(solution)/shard_map/ppermute | solution.py:269
  14.6 8.9 %collective-permute-start.26 = (bf16[512,256]{1,0:T(8,128)(2,1)S(1)}, bf16[512,256]{1,0:T(8,128)(2,1)S(1)}, u32[]{:S(2)}, u32[]{:S(2)}) collective-permute-start(bf16[512,256]{1,0:T(8,128)(2,1)S(1)} %get-tuple-element.12), channel_id=1, source_target_pairs={{0,18},{2,22},{4,16},{6,26},{8,20},{10,30},{12,24},{14,28},{16,2},... | collective-permute-start | bytes 786440 | tf_op jit(solution)/shard_map/ppermute | solution.py:266
  16.8 9.8 %collective-permute-start.9 = (bf16[256,256]{1,0:T(8,128)(2,1)S(1)}, bf16[256,256]{1,0:T(8,128)(2,1)S(1)}, u32[]{:S(2)}, u32[]{:S(2)}) collective-permute-start(bf16[256,256]{1,0:T(8,128)(2,1)S(1)} %collective-permute-done.8.refs_2_), channel_id=1, source_target_pairs={{0,2},{2,6},{4,0},{6,10},{8,4},{10,14},{12,8},{14,12},{16,18},{18,... | collective-permute-start | bytes 393224 | tf_op jit(solution)/shard_map/ppermute | solution.py:266
  20.2 91.1 %collective-permute-start.18 = (bf16[768,1536]{1,0:T(8,128)(2,1)S(1)}, bf16[768,1536]{1,0:T(8,128)(2,1)S(1)}, u32[]{:S(2)}, u32[]{:S(2)}) collective-permute-start(bf16[768,1536]{1,0:T(8,128)(2,1)S(1)} %dynamic-slice_bitcast_fusion), channel_id=1, source_target_pairs={{0,17},{1,16},{16,1},{17,0},{2,19},{3,18},{18,3},{19,2},{4,21},{5,... | collective-permute-start | bytes 7077896 | tf_op jit(solution)/shard_map/ppermute | solution.py:283
  21.4 16.4 %collective-permute-start = (bf16[768,256]{1,0:T(8,128)(2,1)S(1)}, bf16[768,256]{1,0:T(8,128)(2,1)S(1)}, u32[]{:S(2)}, u32[]{:S(2)}) collective-permute-start(bf16[768,256]{1,0:T(8,128)(2,1)S(1)} %turned.1), channel_id=1, source_target_pairs={{0,16},{16,0},{1,17},{17,1},{2,18},{18,2},{3,19},{19,3},{4,20},{20... | collective-permute-start | bytes 1179656 | tf_op jit(solution)/shard_map/ppermute | solution.py:269
  23.5 6.3 %collective-permute-start.2 = (bf16[256,256]{1,0:T(8,128)(2,1)S(1)}, bf16[256,256]{1,0:T(8,128)(2,1)S(1)}, u32[]{:S(2)}, u32[]{:S(2)}) collective-permute-start(bf16[256,256]{1,0:T(8,128)(2,1)S(1)} %collective-permute-done.1.refs_1_), channel_id=1, source_target_pairs={{0,4},{2,0},{4,8},{6,2},{8,12},{10,6},{12,14},{14,10},{16,20},{18,... | collective-permute-start | bytes 393224 | tf_op jit(solution)/shard_map/ppermute | solution.py:266
  26.6 5.2 %collective-permute-start.10 = (bf16[256,256]{1,0:T(8,128)(2,1)S(1)}, bf16[256,256]{1,0:T(8,128)(2,1)S(1)}, u32[]{:S(2)}, u32[]{:S(2)}) collective-permute-start(bf16[256,256]{1,0:T(8,128)(2,1)S(1)} %collective-permute-done.9.refs_2_), channel_id=1, source_target_pairs={{0,2},{2,6},{4,0},{6,10},{8,4},{10,14},{12,8},{14,12},{16,18},{18,... | collective-permute-start | bytes 393224 | tf_op jit(solution)/shard_map/ppermute | solution.py:266
  29.7 6.4 %collective-permute-start.3 = (bf16[256,256]{1,0:T(8,128)(2,1)S(1)}, bf16[256,256]{1,0:T(8,128)(2,1)S(1)}, u32[]{:S(2)}, u32[]{:S(2)}) collective-permute-start(bf16[256,256]{1,0:T(8,128)(2,1)S(1)} %collective-permute-done.2.refs_1_), channel_id=1, source_target_pairs={{0,4},{2,0},{4,8},{6,2},{8,12},{10,6},{12,14},{14,10},{16,20},{18,... | collective-permute-start | bytes 393224 | tf_op jit(solution)/shard_map/ppermute | solution.py:266
  31.8 9.1 %collective-permute-start.20 = (bf16[512,256]{1,0:T(8,128)(2,1)S(1)}, bf16[512,256]{1,0:T(8,128)(2,1)S(1)}, u32[]{:S(2)}, u32[]{:S(2)}) collective-permute-start(bf16[512,256]{1,0:T(8,128)(2,1)S(1)} %collective-permute-done.19.refs_1_), channel_id=1, source_target_pairs={{0,4},{2,0},{4,8},{6,2},{8,12},{10,6},{12,14},{14,10},{16,20},{18,... | collective-permute-start | bytes 786440 | tf_op jit(solution)/shard_map/ppermute | solution.py:266
  36.1 11.2 %collective-permute-start.27 = (bf16[512,256]{1,0:T(8,128)(2,1)S(1)}, bf16[512,256]{1,0:T(8,128)(2,1)S(1)}, u32[]{:S(2)}, u32[]{:S(2)}) collective-permute-start(bf16[512,256]{1,0:T(8,128)(2,1)S(1)} %collective-permute-done.26.refs_2_), channel_id=1, source_target_pairs={{0,2},{2,6},{4,0},{6,10},{8,4},{10,14},{12,8},{14,12},{16,18},{18,... | collective-permute-start | bytes 786440 | tf_op jit(solution)/shard_map/ppermute | solution.py:266
  37.8 7.9 %collective-permute-start.11 = (bf16[256,256]{1,0:T(8,128)(2,1)S(1)}, bf16[256,256]{1,0:T(8,128)(2,1)S(1)}, u32[]{:S(2)}, u32[]{:S(2)}) collective-permute-start(bf16[256,256]{1,0:T(8,128)(2,1)S(1)} %collective-permute-done.10.refs_2_), channel_id=1, source_target_pairs={{0,2},{2,6},{4,0},{6,10},{8,4},{10,14},{12,8},{14,12},{16,18},{18,... | collective-permute-start | bytes 393224 | tf_op jit(solution)/shard_map/ppermute | solution.py:266
  40.8 6.8 %collective-permute-start.4 = (bf16[256,256]{1,0:T(8,128)(2,1)S(1)}, bf16[256,256]{1,0:T(8,128)(2,1)S(1)}, u32[]{:S(2)}, u32[]{:S(2)}) collective-permute-start(bf16[256,256]{1,0:T(8,128)(2,1)S(1)} %collective-permute-done.3.refs_1_), channel_id=1, source_target_pairs={{0,4},{2,0},{4,8},{6,2},{8,12},{10,6},{12,14},{14,10},{16,20},{18,... | collective-permute-start | bytes 393224 | tf_op jit(solution)/shard_map/ppermute | solution.py:266
  45.6 6.4 %collective-permute-start.12 = (bf16[256,256]{1,0:T(8,128)(2,1)S(1)}, bf16[256,256]{1,0:T(8,128)(2,1)S(1)}, u32[]{:S(2)}, u32[]{:S(2)}) collective-permute-start(bf16[256,256]{1,0:T(8,128)(2,1)S(1)} %collective-permute-done.11.refs_2_), channel_id=1, source_target_pairs={{0,2},{2,6},{4,0},{6,10},{8,4},{10,14},{12,8},{14,12},{16,18},{18,... | collective-permute-start | bytes 393224 | tf_op jit(solution)/shard_map/ppermute | solution.py:266
  47.3 10.9 %collective-permute-start.21 = (bf16[512,256]{1,0:T(8,128)(2,1)S(1)}, bf16[512,256]{1,0:T(8,128)(2,1)S(1)}, u32[]{:S(2)}, u32[]{:S(2)}) collective-permute-start(bf16[512,256]{1,0:T(8,128)(2,1)S(1)} %collective-permute-done.20.refs_1_), channel_id=1, source_target_pairs={{0,4},{2,0},{4,8},{6,2},{8,12},{10,6},{12,14},{14,10},{16,20},{18,... | collective-permute-start | bytes 786440 | tf_op jit(solution)/shard_map/ppermute | solution.py:266
  47.7 10.6 %collective-permute-start.28 = (bf16[512,256]{1,0:T(8,128)(2,1)S(1)}, bf16[512,256]{1,0:T(8,128)(2,1)S(1)}, u32[]{:S(2)}, u32[]{:S(2)}) collective-permute-start(bf16[512,256]{1,0:T(8,128)(2,1)S(1)} %collective-permute-done.27.refs_2_), channel_id=1, source_target_pairs={{0,2},{2,6},{4,0},{6,10},{8,4},{10,14},{12,8},{14,12},{16,18},{18,... | collective-permute-start | bytes 786440 | tf_op jit(solution)/shard_map/ppermute | solution.py:266
  52.0 5.0 %collective-permute-start.5 = (bf16[256,256]{1,0:T(8,128)(2,1)S(1)}, bf16[256,256]{1,0:T(8,128)(2,1)S(1)}, u32[]{:S(2)}, u32[]{:S(2)}) collective-permute-start(bf16[256,256]{1,0:T(8,128)(2,1)S(1)} %collective-permute-done.4.refs_1_), channel_id=1, source_target_pairs={{0,4},{2,0},{4,8},{6,2},{8,12},{10,6},{12,14},{14,10},{16,20},{18,... | collective-permute-start | bytes 393224 | tf_op jit(solution)/shard_map/ppermute | solution.py:266
  57.0 5.1 %collective-permute-start.13 = (bf16[256,256]{1,0:T(8,128)(2,1)S(1)}, bf16[256,256]{1,0:T(8,128)(2,1)S(1)}, u32[]{:S(2)}, u32[]{:S(2)}) collective-permute-start(bf16[256,256]{1,0:T(8,128)(2,1)S(1)} %collective-permute-done.12.refs_2_), channel_id=1, source_target_pairs={{0,2},{2,6},{4,0},{6,10},{8,4},{10,14},{12,8},{14,12},{16,18},{18,... | collective-permute-start | bytes 393224 | tf_op jit(solution)/shard_map/ppermute | solution.py:266
  58.2 56.6 %collective-permute-start.37 = (bf16[256,3072]{1,0:T(8,128)(2,1)S(1)}, bf16[256,3072]{1,0:T(8,128)(2,1)S(1)}, u32[]{:S(2)}, u32[]{:S(2)}) collective-permute-start(bf16[256,3072]{1,0:T(8,128)(2,1)S(1)} %bitcast.13), channel_id=1, source_target_pairs={{0,16},{16,0},{1,17},{17,1},{2,18},{18,2},{3,19},{19,3},{4,20},{20... | collective-permute-start | bytes 4718600 | tf_op jit(solution)/shard_map/ppermute | solution.py:269
  58.2 8.7 %collective-permute-start.22 = (bf16[512,256]{1,0:T(8,128)(2,1)S(1)}, bf16[512,256]{1,0:T(8,128)(2,1)S(1)}, u32[]{:S(2)}, u32[]{:S(2)}) collective-permute-start(bf16[512,256]{1,0:T(8,128)(2,1)S(1)} %collective-permute-done.21.refs_1_), channel_id=1, source_target_pairs={{0,4},{2,0},{4,8},{6,2},{8,12},{10,6},{12,14},{14,10},{16,20},{18,... | collective-permute-start | bytes 786440 | tf_op jit(solution)/shard_map/ppermute | solution.py:266
  62.0 6.4 %collective-permute-start.29 = (bf16[512,256]{1,0:T(8,128)(2,1)S(1)}, bf16[512,256]{1,0:T(8,128)(2,1)S(1)}, u32[]{:S(2)}, u32[]{:S(2)}) collective-permute-start(bf16[512,256]{1,0:T(8,128)(2,1)S(1)} %collective-permute-done.28.refs_2_), channel_id=1, source_target_pairs={{0,2},{2,6},{4,0},{6,10},{8,4},{10,14},{12,8},{14,12},{16,18},{18,... | collective-permute-start | bytes 786440 | tf_op jit(solution)/shard_map/ppermute | solution.py:266
  66.9 8.1 %collective-permute-start.23 = (bf16[512,256]{1,0:T(8,128)(2,1)S(1)}, bf16[512,256]{1,0:T(8,128)(2,1)S(1)}, u32[]{:S(2)}, u32[]{:S(2)}) collective-permute-start(bf16[512,256]{1,0:T(8,128)(2,1)S(1)} %collective-permute-done.22.refs_1_), channel_id=1, source_target_pairs={{0,4},{2,0},{4,8},{6,2},{8,12},{10,6},{12,14},{14,10},{16,20},{18,... | collective-permute-start | bytes 786440 | tf_op jit(solution)/shard_map/ppermute | solution.py:266
  68.4 7.1 %collective-permute-start.30 = (bf16[512,256]{1,0:T(8,128)(2,1)S(1)}, bf16[512,256]{1,0:T(8,128)(2,1)S(1)}, u32[]{:S(2)}, u32[]{:S(2)}) collective-permute-start(bf16[512,256]{1,0:T(8,128)(2,1)S(1)} %collective-permute-done.29.refs_2_), channel_id=1, source_target_pairs={{0,2},{2,6},{4,0},{6,10},{8,4},{10,14},{12,8},{14,12},{16,18},{18,... | collective-permute-start | bytes 786440 | tf_op jit(solution)/shard_map/ppermute | solution.py:266
  75.1 7.3 %collective-permute-start.24 = (bf16[512,256]{1,0:T(8,128)(2,1)S(1)}, bf16[512,256]{1,0:T(8,128)(2,1)S(1)}, u32[]{:S(2)}, u32[]{:S(2)}) collective-permute-start(bf16[512,256]{1,0:T(8,128)(2,1)S(1)} %collective-permute-done.23.refs_1_), channel_id=1, source_target_pairs={{0,4},{2,0},{4,8},{6,2},{8,12},{10,6},{12,14},{14,10},{16,20},{18,... | collective-permute-start | bytes 786440 | tf_op jit(solution)/shard_map/ppermute | solution.py:266
  75.5 7.1 %collective-permute-start.31 = (bf16[512,256]{1,0:T(8,128)(2,1)S(1)}, bf16[512,256]{1,0:T(8,128)(2,1)S(1)}, u32[]{:S(2)}, u32[]{:S(2)}) collective-permute-start(bf16[512,256]{1,0:T(8,128)(2,1)S(1)} %collective-permute-done.30.refs_2_), channel_id=1, source_target_pairs={{0,2},{2,6},{4,0},{6,10},{8,4},{10,14},{12,8},{14,12},{16,18},{18,... | collective-permute-start | bytes 786440 | tf_op jit(solution)/shard_map/ppermute | solution.py:266
  82.4 6.5 %collective-permute-start.25 = (bf16[512,256]{1,0:T(8,128)(2,1)S(1)}, bf16[512,256]{1,0:T(8,128)(2,1)S(1)}, u32[]{:S(2)}, u32[]{:S(2)}) collective-permute-start(bf16[512,256]{1,0:T(8,128)(2,1)S(1)} %collective-permute-done.24.refs_1_), channel_id=1, source_target_pairs={{0,4},{2,0},{4,8},{6,2},{8,12},{10,6},{12,14},{14,10},{16,20},{18,... | collective-permute-start | bytes 786440 | tf_op jit(solution)/shard_map/ppermute | solution.py:266
  82.7 14.1 %collective-permute-start.32 = (bf16[512,256]{1,0:T(8,128)(2,1)S(1)}, bf16[512,256]{1,0:T(8,128)(2,1)S(1)}, u32[]{:S(2)}, u32[]{:S(2)}) collective-permute-start(bf16[512,256]{1,0:T(8,128)(2,1)S(1)} %collective-permute-done.31.refs_2_), channel_id=1, source_target_pairs={{0,2},{2,6},{4,0},{6,10},{8,4},{10,14},{12,8},{14,12},{16,18},{18,... | collective-permute-start | bytes 786440 | tf_op jit(solution)/shard_map/ppermute | solution.py:266
  88.9 12.4 %collective-permute-start.6 = (bf16[256,256]{1,0:T(8,128)(2,1)S(1)}, bf16[256,256]{1,0:T(8,128)(2,1)S(1)}, u32[]{:S(2)}, u32[]{:S(2)}) collective-permute-start(bf16[256,256]{1,0:T(8,128)(2,1)S(1)} %collective-permute-done.5.refs_1_), channel_id=1, source_target_pairs={{0,4},{2,0},{4,8},{6,2},{8,12},{10,6},{12,14},{14,10},{16,20},{18,... | collective-permute-start | bytes 393224 | tf_op jit(solution)/shard_map/ppermute | solution.py:266
  96.8 6.0 %collective-permute-start.14 = (bf16[256,256]{1,0:T(8,128)(2,1)S(1)}, bf16[256,256]{1,0:T(8,128)(2,1)S(1)}, u32[]{:S(2)}, u32[]{:S(2)}) collective-permute-start(bf16[256,256]{1,0:T(8,128)(2,1)S(1)} %collective-permute-done.13.refs_2_), channel_id=1, source_target_pairs={{0,2},{2,6},{4,0},{6,10},{8,4},{10,14},{12,8},{14,12},{16,18},{18,... | collective-permute-start | bytes 393224 | tf_op jit(solution)/shard_map/ppermute | solution.py:266
  101.2 10.1 %collective-permute-start.36 = (bf16[256,512]{1,0:T(8,128)(2,1)S(1)}, bf16[256,512]{1,0:T(8,128)(2,1)S(1)}, u32[]{:S(2)}, u32[]{:S(2)}) collective-permute-start(bf16[256,512]{1,0:T(8,128)(2,1)S(1)} %absorb.31.refs_1_), channel_id=1, source_target_pairs={{0,1},{1,0},{16,17},{17,16},{2,3},{3,2},{18,19},{19,18},{4,5},{5,4... | collective-permute-start | bytes 786440 | tf_op jit(solution)/shard_map/ppermute | solution.py:283
  102.8 6.1 %collective-permute-start.7 = (bf16[256,256]{1,0:T(8,128)(2,1)S(1)}, bf16[256,256]{1,0:T(8,128)(2,1)S(1)}, u32[]{:S(2)}, u32[]{:S(2)}) collective-permute-start(bf16[256,256]{1,0:T(8,128)(2,1)S(1)} %collective-permute-done.6.refs_1_), channel_id=1, source_target_pairs={{0,4},{2,0},{4,8},{6,2},{8,12},{10,6},{12,14},{14,10},{16,20},{18,... | collective-permute-start | bytes 393224 | tf_op jit(solution)/shard_map/ppermute | solution.py:266
  106.8 4.6 %copy-start.4 = (f32[1,3072]{1,0:T(1,128)S(1)}, f32[1,3072]{1,0:T(1,128)}, u32[]{:S(2)}) copy-start(f32[1,3072]{1,0:T(1,128)} %param.11) | copy-start | bytes 36868
  109.8 5.0 %collective-permute-start.17 = (bf16[256,256]{1,0:T(8,128)(2,1)S(1)}, bf16[256,256]{1,0:T(8,128)(2,1)S(1)}, u32[]{:S(2)}, u32[]{:S(2)}) collective-permute-start(bf16[256,256]{1,0:T(8,128)(2,1)S(1)} %absorb.23.refs_2_), channel_id=1, source_target_pairs={{0,1},{1,0},{16,17},{17,16},{2,3},{3,2},{18,19},{19,18},{4,5},{5,4... | collective-permute-start | bytes 393224 | tf_op jit(solution)/shard_map/ppermute | solution.py:283
  111.3 3.4 %collective-permute-start.38 = (f32[1,3072]{1,0:T(1,128)S(1)}, f32[1,3072]{1,0:T(1,128)S(1)}, u32[]{:S(2)}, u32[]{:S(2)}) collective-permute-start(f32[1,3072]{1,0:T(1,128)S(1)} %copy-done.4), channel_id=1, source_target_pairs={{0,16},{16,0},{1,17},{17,1},{2,18},{18,2},{3,19},{19,3},{4,20},{20... | collective-permute-start | bytes 36872 | tf_op jit(solution)/shard_map/ppermute | solution.py:269

commit v2 on v0

v2 whole, which is shorter than its diff:
```python
import functools
import math

import jax
import jax.numpy as jnp
from jax import lax
from jax.experimental import pallas as pl
from jax.experimental.pallas import tpu as pltpu
from jax.sharding import PartitionSpec as P


HD = 128
STATE = HD + 16
LOG2E = 1.4426950408889634
VMEM = pl.BlockSpec(memory_space=pltpu.VMEM)


def limit(mib):
    return pltpu.CompilerParams(vmem_limit_bytes=mib << 20)


def pack_kernel(groups, role_ref, k_ref, v_ref, *out_refs):
    rows, width = k_ref.shape
    half = width // 2
    for side in range(2):
        role = role_ref[0] if side == 0 else 1 - role_ref[0]
        for heads, out in zip(groups, out_refs[side * len(groups) :]):
            for place, head in enumerate(heads):
                lanes = pl.ds(pl.multiple_of(role * half + head * HD, HD), HD)
                base = place * 2 * HD
                for piece in range(rows // HD):
                    out[base : base + HD, piece * HD : (piece + 1) * HD] = k_ref[
                        piece * HD : (piece + 1) * HD, lanes
                    ]
                out[base + HD : base + 2 * HD, :] = v_ref[:, lanes].T


SMEM = pl.BlockSpec(memory_space=pltpu.SMEM)


def pack(role, keys, values, groups):
    rows = keys.shape[0]
    shapes = [jax.ShapeDtypeStruct((len(heads) * 2 * HD, rows), jnp.bfloat16) for heads in groups]
    return pl.pallas_call(
        functools.partial(pack_kernel, groups),
        out_shape=tuple(shapes + shapes),
        in_specs=[SMEM, VMEM, VMEM],
        out_specs=(VMEM,) * (2 * len(groups)),
        compiler_params=limit(8),
        name="pack",
    )(role, keys, values)


def turn_kernel(role_ref, x_ref, mine_ref, give_ref):
    half = x_ref.shape[1] // 2
    for out, role in ((mine_ref, role_ref[0]), (give_ref, 1 - role_ref[0])):
        for head in range(half // HD):
            lanes = pl.ds(pl.multiple_of(role * half + head * HD, HD), HD)
            out[head * HD : (head + 1) * HD, :] = x_ref[:, lanes].T


def turned(role, x):
    shape = jax.ShapeDtypeStruct((x.shape[1] // 2, x.shape[0]), x.dtype)
    return pl.pallas_call(
        turn_kernel,
        out_shape=(shape, shape),
        in_specs=[SMEM, VMEM],
        out_specs=(VMEM, VMEM),
        compiler_params=limit(8),
        name="turned",
    )(role, x)


def absorb_kernel(heads, count, first, last, *refs):
    q_refs, kv_refs, rest = refs[:2], refs[2 : 2 + count], refs[2 + count :]
    state = None if first else rest[0]
    outs = rest if first else rest[1:]
    keys = kv_refs[0].shape[1]
    factor = LOG2E / math.sqrt(HD)
    for place, head in enumerate(heads):
        base = place * 2 * HD
        key = jnp.concatenate(
            [
                kv[base : base + HD, piece * HD : (piece + 1) * HD]
                for kv in kv_refs
                for piece in range(keys // HD)
            ],
            axis=0,
        )
        value = jnp.concatenate([kv[base + HD : base + 2 * HD, :] for kv in kv_refs], axis=1)
        tall = jnp.concatenate([value, jnp.ones((16, value.shape[1]), jnp.bfloat16)], axis=0)
        for side, q_ref in enumerate(q_refs):
            query = q_ref[head * HD : (head + 1) * HD, :]
            scores = jnp.dot(key, query, preferred_element_type=jnp.float32)
            top = jnp.max(scores, axis=0, keepdims=True)
            if not first:
                top_old = state[place, side, HD + 8 : HD + 9, :]
                top = jnp.maximum(top_old, top)
            raised = jnp.exp2((scores - top) * factor).astype(jnp.bfloat16)
            both = jnp.dot(tall, raised, preferred_element_type=jnp.float32)
            mixed, total = both[:HD], both[HD : HD + 8]
            if not first:
                shrink = jnp.exp2((top_old - top) * factor)
                mixed = state[place, side, :HD, :] * shrink + mixed
                total = state[place, side, HD : HD + 8, :] * shrink + total
            if last:
                done = mixed / total[:1]
                outs[side][:, place * HD : (place + 1) * HD] = done.T.astype(jnp.bfloat16)
            else:
                outs[0][place, side, :HD, :] = mixed
                outs[0][place, side, HD : HD + 8, :] = total
                outs[0][place, side, HD + 8 :, :] = jnp.broadcast_to(top, total.shape)


def absorb(asking, blocks, heads, state, last):
    rows = asking[0].shape[1]
    keys = blocks[0].shape[1] * len(blocks)
    count = len(heads)
    first = state is None
    if last:
        shape = jax.ShapeDtypeStruct((rows, count * HD), jnp.bfloat16)
        out_shape, out_specs = (shape, shape), (VMEM, VMEM)
    else:
        out_shape = jax.ShapeDtypeStruct((count, 2, STATE, rows), jnp.float32)
        out_specs = VMEM
    operands = [*asking, *blocks] + ([] if first else [state])
    return pl.pallas_call(
        functools.partial(absorb_kernel, heads, len(blocks), first, last),
        out_shape=out_shape,
        in_specs=[VMEM] * len(operands),
        out_specs=out_specs,
        input_output_aliases={} if first or last else {len(operands) - 1: 0},
        cost_estimate=pl.CostEstimate(
            flops=8 * count * rows * keys * HD,
            bytes_accessed=count * rows * HD * 12,
            transcendentals=2 * count * rows * keys,
        ),
        compiler_params=limit(12),
        name="absorb",
    )(*operands)


def project_kernel(uses, finish, *refs):
    out = refs[-1]
    refs = list(refs[1:-1])
    total = None
    if finish:
        total = refs[-3][...]
    for weight_count, pieces in uses:
        lefts = [refs.pop(0)[...] for _ in range(pieces)]
        rights = [refs.pop(0)[...] for _ in range(weight_count)]
        left = lefts[0] if pieces == 1 else jnp.concatenate(lefts, axis=1)
        right = rights[0] if weight_count == 1 else jnp.concatenate(rights, axis=0)
        term = jnp.dot(left, right, preferred_element_type=jnp.float32)
        total = term if total is None else total + term
    if finish:
        stream, gate = refs[-2], refs[-1]
        total = stream[...].astype(jnp.float32) + gate[...] * total
    out[...] = total.astype(out.dtype)


def project(where, sources, cols, wide, finishing=None):
    rows = sources[0][0][0].shape[0]
    steps = cols // wide
    operands, specs, uses = [], [], []
    for pieces, weight, whole, flip, heads in sources:
        for piece in pieces:
            operands.append(piece)
            specs.append(pl.BlockSpec(piece.shape, lambda j, s: (0, 0)))
        per_role = weight.shape[0] // HD // 2

        def place(j, s, head, whole=whole, flip=flip, per_role=per_role, unit=HD):
            role = 1 - s[1] if flip else s[1]
            at = role if unit != HD else role * per_role + head
            return at, (s[0] * steps + j if whole else j)

        if tuple(heads) == tuple(range(per_role)):
            operands.append(weight)
            specs.append(
                pl.BlockSpec(
                    (per_role * HD, wide), functools.partial(place, head=0, unit=per_role * HD)
                )
            )
            uses.append((1, len(pieces)))
        else:
            for head in heads:
                operands.append(weight)
                specs.append(pl.BlockSpec((HD, wide), functools.partial(place, head=head)))
            uses.append((len(heads), len(pieces)))
    if finishing is not None:
        operands += list(finishing)
        specs += [
            pl.BlockSpec((rows, wide), lambda j, s: (0, j)),
            pl.BlockSpec((rows, wide), lambda j, s: (0, s[0] * steps + j)),
            pl.BlockSpec((1, wide), lambda j, s: (0, s[0] * steps + j)),
        ]
    depth = sum(len(source[4]) for source in sources) * HD
    return pl.pallas_call(
        functools.partial(project_kernel, uses, finishing is not None),
        out_shape=jax.ShapeDtypeStruct(
            (rows, cols), jnp.float32 if finishing is None else jnp.bfloat16
        ),
        grid_spec=pltpu.PrefetchScalarGridSpec(
            num_scalar_prefetch=1,
            grid=(steps,),
            in_specs=specs,
            out_specs=pl.BlockSpec((rows, wide), lambda j, s: (0, j)),
        ),
        cost_estimate=pl.CostEstimate(
            flops=2 * rows * depth * cols, bytes_accessed=rows * cols * 4, transcendentals=0
        ),
        compiler_params=limit(12),
        name="project",
    )(where, *operands)


def role_of(member):
    return (member // 2 + 1) // 2 % 2


def per_device(stream_in, queries, keys, values, out_weight, gate_scale):
    sections = lax.axis_size("segment")
    seq_count = lax.axis_size("seq")
    shares = lax.axis_size("head")
    local = queries.shape[2] // HD // 2
    cycle_len = min(32, seq_count)
    stride = seq_count // cycle_len
    planes = cycle_len // 2
    rounds = planes // 2

    partner = {m: m ^ 2 for m in range(cycle_len)}
    beside = {m: m ^ 1 for m in range(cycle_len)}
    beyond = {}
    for role in range(2):
        for column in range(2):
            line = [p * 2 + column for p in range(planes) if role_of(p * 2) == role]
            for at, m in enumerate(line):
                beyond[m] = line[(at + 1) % len(line)]

    def hop(block, towards, shift=0, by=0):
        pairs = []
        for section in range(sections):
            for member in range(cycle_len):
                for video in range(stride):
                    for share in range(shares):
                        origin = section * seq_count + member * stride + video
                        target = (
                            (section + shift) % sections * seq_count
                            + towards[member] * stride
                            + video
                        )
                        pairs.append(
                            (origin * shares + share, target * shares + (share + by) % shares)
                        )
        return lax.ppermute(block, ("segment", "seq", "head"), pairs)

    still = {m: m for m in range(cycle_len)}
    share = lax.axis_index("head").astype(jnp.int32)
    role = role_of(lax.axis_index("seq").astype(jnp.int32) // stride)
    role_ref = role.reshape(1)
    where = jnp.stack([share, role])

    early = local - max(1, local // 3)
    groups = [tuple(range(early)), tuple(range(early, local))] if early else [tuple(range(local))]
    everyone = range(len(groups))

    packed = pack(role_ref, keys[0], values[0], groups)
    mine, give = packed[: len(groups)], packed[len(groups) :]
    my_query, give_query = turned(role_ref, queries[0])
    got = [None] * len(groups)
    far = [[None] * 2 for _ in groups]
    near = [[None] * 2 for _ in groups]
    own = [None] * len(groups)
    for g in everyone:
        got[g] = hop(give[g], partner, 1)
        far[g][0] = hop(mine[g], beyond, 1)
        near[g][0] = hop(mine[g], beside, 1)
        own[g] = hop(mine[g], still, 1)
    asking = [hop(my_query, still, 1), hop(give_query, partner, 1)]

    col_count = out_weight.shape[2] // shares
    weights = {}
    for by in range(1, shares):
        start = lax.rem(share + by, shares) * col_count
        part = lax.dynamic_slice_in_dim(out_weight[0], start, col_count, 1)
        weights[by] = hop(part, still, 1, by)
    weights[0] = hop(out_weight[0], still, 1)
    stream = hop(stream_in[0], still, 1)
    gate = hop(gate_scale, still, 1)

    def fold(g, blocks, held, last=False):
        return absorb(asking, blocks, groups[g], held, last)

    attended = []
    for g in everyone:
        far[g][1] = hop(got[g], beyond)
        near[g][1] = hop(got[g], beside)
        state = fold(g, [own[g], got[g]], None)
        state = fold(g, near[g], state)
        arrived = far[g]
        for turn in range(1, rounds):
            onward = [hop(arrived[i], beside) for i in range(2)]
            following = None
            if turn < rounds - 1:
                following = [hop(arrived[i], beyond) for i in range(2)]
            state = fold(g, arrived, state)
            if turn < rounds - 1:
                state = fold(g, onward, state)
            elif g < len(groups) - 1:
                attended.append(fold(g, onward, state, True))
            else:
                state = fold(g, onward[:1], state)
                attended.append(fold(g, onward[1:], state, True))
            arrived = following

    sources, late = [], []
    for g in everyone:
        ours, theirs = attended[g]
        back = hop(theirs, partner)
        pieces = [(ours, 0, False), (back, 0, True)]
        for by in range(1, shares):
            pieces.append((hop(ours, still, 0, by), by, False))
            pieces.append((hop(theirs, partner, 0, by), by, True))
        for piece, by, flip in pieces:
            source = ([piece], weights[by], by == 0, flip, groups[g])
            if g == len(groups) - 1 and (by or flip):
                late.append(source)
            else:
                sources.append(source)
    if len(groups) > 1:
        mergeable = [source for source in sources if source[2] and not source[3]]
        sources = [source for source in sources if not (source[2] and not source[3])]
        merged = [source[0][0] for source in mergeable]
        sources.append((merged, weights[0], True, False, sum((s[4] for s in mergeable), ())))
    total = project(where, sources, col_count, 512)
    return project(where, late, col_count, 512, (total, stream, gate))[None]


def solution(mesh):
    return jax.shard_map(
        per_device,
        mesh=mesh,
        in_specs=(
            P("segment", "seq", None),
            P("segment", "seq", "head"),
            P("segment", "seq", "head"),
            P("segment", "seq", "head"),
            P("segment", "head", None),
            P("segment", None),
        ),
        out_specs=P("segment", "seq", "head"),
        check_vma=False,
    )
```

time: 191 us -> 103 us (0.54)
  waiting for transfers between devices: 109 us -> 36.6 us
  starting transfers between devices: 3.44 us -> 42.4 us
  matrix products: 28.2 us -> 0 us
  local copies, waits for them, and re-layouts: 23.3 us -> 3.38 us
  Pallas kernels: 0 us -> 19.8 us
  between operations: 13.6 us -> 0.2 us
  other arithmetic: 12.9 us -> 0.07 us
    ppermute x8 -> x28, waiting for transfers between devices: 86.1 us -> 36.6 us  [hop(): return lax.ppermute(block, ('segment', 'seq', 'head'), pairs)]
    ppermute x8 -> x28, starting transfers between devices: 3.44 us -> 42.4 us  [hop(): return lax.ppermute(block, ('segment', 'seq', 'head'), pairs)]
    dot_general x17 -> x0, matrix products: 28.2 us -> none  [the longest x8 18.1 us: absorb(): jnp.einsum('hqk,khd->qhd', raised.astype(jnp.bfloat16), value_block, pref...]
    reduce_scatter x1 -> x0, waiting for transfers between devices: 22.4 us -> none  [per_device(): lax.psum_scatter(partial_value.astype(jnp.bfloat16), 'head', scatter_dime...]
    pallas_call x0 -> x13, Pallas kernels: none -> 19.8 us  [the longest x9 11.5 us: absorb(): pl.pallas_call(functools.partial(absorb_kernel, heads, len(blocks), first...]
    while x85 -> x0, local copies, waits for them, and re-layouts: 16.2 us -> none
    transpose x9 -> x0, other arithmetic: 9.59 us -> none  [the longest x8 9.58 us: absorb(): accumulated = accumulated * shrink.T[:, :, None] + mixed]
    unnamed x27 -> x8, local copies, waits for them, and re-layouts: 5.89 us -> 0.02 us
  transfers between devices with their start and end apart: 9 -> 28, of which waited for: 9 -> 10; matrix products, arithmetic and copies ran while one was open for 21% -> 3% of each run, Pallas kernels for 0% -> 16%
where the time goes in v2:
time: 103 us; the launch traced here: 102 us
  starting transfers between devices  42.4 us (41%)
  waiting for transfers between devices  36.6 us (36%)
  Pallas kernels  19.8 us (19%)
  local copies, waits for them, and re-layouts  3.38 us (3%)
    ppermute x28, starting transfers between devices, hop(): return lax.ppermute(block, ('segment', 'seq', 'head'), pairs)  42.4 us
    ppermute x28, waiting for transfers between devices, hop(): return lax.ppermute(block, ('segment', 'seq', 'head'), pairs)  36.6 us
    pallas_call x9, Pallas kernels, absorb(): pl.pallas_call(functools.partial(absorb_kernel, heads, len(blocks), first...  11.5 us
    pallas_call x2, Pallas kernels, project(): pl.pallas_call(functools.partial(project_kernel, uses, finishing is not N...  7.97 us
    dynamic_slice x1, local copies, waits for them, and re-layouts, per_device(): part = lax.dynamic_slice_in_dim(out_weight[0], start, col_count, 1)  3.36 us
  transfers between devices with their start and end apart: 28, of which 10 were waited for; matrix products, arithmetic and copies ran while one was open for 3% of the time, Pallas kernels for 16%

profile of v2, /device:TPU:0, one launch (start us, length us, event | category | flops | bytes accessed | tf_op | source)
XLA Modules:
  0.0 102.4 jit_solution(1734057552612860859)
XLA Ops:
  0.0 0.5 collective-permute-start.11
  0.5 3.4 %dynamic-slice_bitcast_fusion = bf16[768,1536]{1,0:T(8,128)(2,1)} fusion(bf16[1,768,3072]{2,1,0:T(8,128)(2,1)} %param.10, s32[]{:T(128)S(6)} %select_n.21), kind=kLoop, calls=%fused_computation | loop fusion | bytes 4718596 | tf_op jit(solution)/shard_map/dynamic_slice | solution.py:285
  3.9 2.6 %collective-permute-start.13 = (bf16[768,1536]{1,0:T(8,128)(2,1)}, bf16[768,1536]{1,0:T(8,128)(2,1)S(1)}, u32[]{:S(2)}, u32[]{:S(2)}) collective-permute-start(bf16[768,1536]{1,0:T(8,128)(2,1)} %dynamic-slice_bitcast_fusion), channel_id=1, source_target_pairs={{0,17},{1,16},{2,19},{3,18},{4,21},{5,20},{6,23},{7,22},{8,25},{9,... | collective-permute-start | bytes 7077896 | tf_op jit(solution)/shard_map/ppermute | solution.py:255
  6.5 0.2 pack.1
  6.7 1.3 %collective-permute-start.2 = (bf16[256,256]{1,0:T(8,128)(2,1)S(1)}, bf16[256,256]{1,0:T(8,128)(2,1)S(1)}, u32[]{:S(2)}, u32[]{:S(2)}) collective-permute-start(bf16[256,256]{1,0:T(8,128)(2,1)S(1)} %get-tuple-element.17), channel_id=1, source_target_pairs={{0,20},{1,21},{2,22},{3,23},{4,16},{5,17},{6,18},{7,19},{8,28},{9,... | collective-permute-start | bytes 393224 | tf_op jit(solution)/shard_map/ppermute | solution.py:255
  7.9 0.5 collective-permute-start.9
  8.4 1.1 %collective-permute-start.7 = (bf16[256,256]{1,0:T(8,128)(2,1)S(1)}, bf16[256,256]{1,0:T(8,128)(2,1)S(1)}, u32[]{:S(2)}, u32[]{:S(2)}) collective-permute-start(bf16[256,256]{1,0:T(8,128)(2,1)S(1)} %get-tuple-element.18), channel_id=1, source_target_pairs={{0,18},{1,19},{2,16},{3,17},{4,22},{5,23},{6,20},{7,21},{8,26},{9,... | collective-permute-start | bytes 393224 | tf_op jit(solution)/shard_map/ppermute | solution.py:255
  9.5 2.8 %collective-permute-done.2.refs_3_ = bf16[256,256]{1,0:T(8,128)(2,1)S(1)} collective-permute-done((bf16[256,256]{1,0:T(8,128)(2,1)S(1)}, bf16[256,256]{1,0:T(8,128)(2,1)S(1)}, u32[]{:S(2)}, u32[]{:S(2)}) %collective-permute-start.2) | collective-permute-done | bytes 131104 | tf_op jit(solution)/shard_map/ppermute | solution.py:255
  12.3 3.5 %collective-permute-start.5 = (bf16[256,256]{1,0:T(8,128)(2,1)S(1)}, bf16[256,256]{1,0:T(8,128)(2,1)S(1)}, u32[]{:S(2)}, u32[]{:S(2)}) collective-permute-start(bf16[256,256]{1,0:T(8,128)(2,1)S(1)} %get-tuple-element.18), channel_id=1, source_target_pairs={{0,28},{1,29},{2,30},{3,31},{4,24},{5,25},{6,26},{7,27},{8,20},{9,... | collective-permute-start | bytes 393224 | tf_op jit(solution)/shard_map/ppermute | solution.py:255
  15.8 0.2 turned.1
  16.0 0.3 collective-permute-start
  16.3 3.5 %collective-permute-done.5.refs_2_ = bf16[256,256]{1,0:T(8,128)(2,1)S(1)} collective-permute-done((bf16[256,256]{1,0:T(8,128)(2,1)S(1)}, bf16[256,256]{1,0:T(8,128)(2,1)S(1)}, u32[]{:S(2)}, u32[]{:S(2)}) %collective-permute-start.5) | collective-permute-done | bytes 131104 | tf_op jit(solution)/shard_map/ppermute | solution.py:255
  19.8 1.5 %collective-permute-start.8 = (bf16[256,256]{1,0:T(8,128)(2,1)S(1)}, bf16[256,256]{1,0:T(8,128)(2,1)S(1)}, u32[]{:S(2)}, u32[]{:S(2)}) collective-permute-start(bf16[256,256]{1,0:T(8,128)(2,1)S(1)} %collective-permute-done.2.refs_3_), channel_id=1, source_target_pairs={{0,2},{1,3},{2,0},{3,1},{4,6},{5,7},{6,4},{7,5},{8,10},{9,11},{10,... | collective-permute-start | bytes 393224 | tf_op jit(solution)/shard_map/ppermute | solution.py:255
  21.3 0.2 collective-permute-start.26
  21.5 2.7 %collective-permute-done.1.refs_1_ = bf16[384,256]{1,0:T(8,128)(2,1)S(1)} collective-permute-done((bf16[384,256]{1,0:T(8,128)(2,1)S(1)}, bf16[384,256]{1,0:T(8,128)(2,1)S(1)}, u32[]{:S(2)}, u32[]{:S(2)}) %collective-permute-start.1) | collective-permute-done | bytes 196640 | tf_op jit(solution)/shard_map/ppermute | solution.py:255
  24.1 1.6 %collective-permute-start.17 = (bf16[512,256]{1,0:T(8,128)(2,1)S(1)}, bf16[512,256]{1,0:T(8,128)(2,1)S(1)}, u32[]{:S(2)}, u32[]{:S(2)}) collective-permute-start(bf16[512,256]{1,0:T(8,128)(2,1)S(1)} %get-tuple-element.22), channel_id=1, source_target_pairs={{0,20},{1,21},{2,22},{3,23},{4,16},{5,17},{6,18},{7,19},{8,28},{9,... | collective-permute-start | bytes 786440 | tf_op jit(solution)/shard_map/ppermute | solution.py:255
  25.7 6.7 %collective-permute-done.17.refs_3_ = bf16[512,256]{1,0:T(8,128)(2,1)S(1)} collective-permute-done((bf16[512,256]{1,0:T(8,128)(2,1)S(1)}, bf16[512,256]{1,0:T(8,128)(2,1)S(1)}, u32[]{:S(2)}, u32[]{:S(2)}) %collective-permute-start.17) | collective-permute-done | bytes 262176 | tf_op jit(solution)/shard_map/ppermute | solution.py:255
  32.4 1.6 %collective-permute-start.20 = (bf16[512,256]{1,0:T(8,128)(2,1)S(1)}, bf16[512,256]{1,0:T(8,128)(2,1)S(1)}, u32[]{:S(2)}, u32[]{:S(2)}) collective-permute-start(bf16[512,256]{1,0:T(8,128)(2,1)S(1)} %get-tuple-element.21), channel_id=1, source_target_pairs={{0,18},{1,19},{2,16},{3,17},{4,22},{5,23},{6,20},{7,21},{8,26},{9,... | collective-permute-start | bytes 786440 | tf_op jit(solution)/shard_map/ppermute | solution.py:255
  34.0 1.1 %collective-permute-start.15 = (bf16[512,256]{1,0:T(8,128)(2,1)S(1)}, bf16[512,256]{1,0:T(8,128)(2,1)S(1)}, u32[]{:S(2)}, u32[]{:S(2)}) collective-permute-start(bf16[512,256]{1,0:T(8,128)(2,1)S(1)} %get-tuple-element.21), channel_id=1, source_target_pairs={{0,28},{1,29},{2,30},{3,31},{4,24},{5,25},{6,26},{7,27},{8,20},{9,... | collective-permute-start | bytes 786440 | tf_op jit(solution)/shard_map/ppermute | solution.py:255
  35.0 5.2 %collective-permute-done.20.refs_2_ = bf16[512,256]{1,0:T(8,128)(2,1)S(1)} collective-permute-done((bf16[512,256]{1,0:T(8,128)(2,1)S(1)}, bf16[512,256]{1,0:T(8,128)(2,1)S(1)}, u32[]{:S(2)}, u32[]{:S(2)}) %collective-permute-start.20) | collective-permute-done | bytes 262176 | tf_op jit(solution)/shard_map/ppermute | solution.py:255
  40.3 1.5 %collective-permute-start.21 = (bf16[512,256]{1,0:T(8,128)(2,1)S(1)}, bf16[512,256]{1,0:T(8,128)(2,1)S(1)}, u32[]{:S(2)}, u32[]{:S(2)}) collective-permute-start(bf16[512,256]{1,0:T(8,128)(2,1)S(1)} %collective-permute-done.17.refs_3_), channel_id=1, source_target_pairs={{0,2},{1,3},{2,0},{3,1},{4,6},{5,7},{6,4},{7,5},{8,10},{9,11},{10,... | collective-permute-start | bytes 786440 | tf_op jit(solution)/shard_map/ppermute | solution.py:255
  41.8 2.5 %collective-permute-done.15.refs_2_ = bf16[512,256]{1,0:T(8,128)(2,1)S(1)} collective-permute-done((bf16[512,256]{1,0:T(8,128)(2,1)S(1)}, bf16[512,256]{1,0:T(8,128)(2,1)S(1)}, u32[]{:S(2)}, u32[]{:S(2)}) %collective-permute-start.15) | collective-permute-done | bytes 262176 | tf_op jit(solution)/shard_map/ppermute | solution.py:255
  44.3 1.8 %collective-permute-start.18 = (bf16[512,256]{1,0:T(8,128)(2,1)S(1)}, bf16[512,256]{1,0:T(8,128)(2,1)S(1)}, u32[]{:S(2)}, u32[]{:S(2)}) collective-permute-start(bf16[512,256]{1,0:T(8,128)(2,1)S(1)} %collective-permute-done.17.refs_3_), channel_id=1, source_target_pairs={{0,12},{1,13},{2,14},{3,15},{4,8},{5,9},{6,10},{7,11},{8,4},{9,5},... | collective-permute-start | bytes 786440 | tf_op jit(solution)/shard_map/ppermute | solution.py:255
  46.1 3.2 %collective-permute-done.21.refs_3_ = bf16[512,256]{1,0:T(8,128)(2,1)S(1)} collective-permute-done((bf16[512,256]{1,0:T(8,128)(2,1)S(1)}, bf16[512,256]{1,0:T(8,128)(2,1)S(1)}, u32[]{:S(2)}, u32[]{:S(2)}) %collective-permute-start.21) | collective-permute-done | bytes 262176 | tf_op jit(solution)/shard_map/ppermute | solution.py:255
  49.3 1.5 %collective-permute-start.16 = (bf16[512,256]{1,0:T(8,128)(2,1)S(1)}, bf16[512,256]{1,0:T(8,128)(2,1)S(1)}, u32[]{:S(2)}, u32[]{:S(2)}) collective-permute-start(bf16[512,256]{1,0:T(8,128)(2,1)S(1)} %collective-permute-done.15.refs_2_), channel_id=1, source_target_pairs={{0,2},{1,3},{2,0},{3,1},{4,6},{5,7},{6,4},{7,5},{8,10},{9,11},{10,... | collective-permute-start | bytes 786440 | tf_op jit(solution)/shard_map/ppermute | solution.py:255
  50.8 3.7 %collective-permute-done.18.refs_3_ = bf16[512,256]{1,0:T(8,128)(2,1)S(1)} collective-permute-done((bf16[512,256]{1,0:T(8,128)(2,1)S(1)}, bf16[512,256]{1,0:T(8,128)(2,1)S(1)}, u32[]{:S(2)}, u32[]{:S(2)}) %collective-permute-start.18) | collective-permute-done | bytes 262176 | tf_op jit(solution)/shard_map/ppermute | solution.py:255
  54.5 0.5 collective-permute-start.19
  55.0 3.5 %collective-permute-done.16.refs_2_ = bf16[512,256]{1,0:T(8,128)(2,1)S(1)} collective-permute-done((bf16[512,256]{1,0:T(8,128)(2,1)S(1)}, bf16[512,256]{1,0:T(8,128)(2,1)S(1)}, u32[]{:S(2)}, u32[]{:S(2)}) %collective-permute-start.16) | collective-permute-done | bytes 262176 | tf_op jit(solution)/shard_map/ppermute | solution.py:255
  58.5 1.7 %collective-permute-start.3 = (bf16[256,256]{1,0:T(8,128)(2,1)S(1)}, bf16[256,256]{1,0:T(8,128)(2,1)S(1)}, u32[]{:S(2)}, u32[]{:S(2)}) collective-permute-start(bf16[256,256]{1,0:T(8,128)(2,1)S(1)} %collective-permute-done.2.refs_3_), channel_id=1, source_target_pairs={{0,12},{1,13},{2,14},{3,15},{4,8},{5,9},{6,10},{7,11},{8,4},{9,5},... | collective-permute-start | bytes 393224 | tf_op jit(solution)/shard_map/ppermute | solution.py:255
  60.2 2.9 %collective-permute-done.19.refs_3_ = bf16[512,256]{1,0:T(8,128)(2,1)S(1)} collective-permute-done((bf16[512,256]{1,0:T(8,128)(2,1)S(1)}, bf16[512,256]{1,0:T(8,128)(2,1)S(1)}, u32[]{:S(2)}, u32[]{:S(2)}) %collective-permute-start.19) | collective-permute-done | bytes 262176 | tf_op jit(solution)/shard_map/ppermute | solution.py:255
  63.1 1.5 %collective-permute-start.6 = (bf16[256,256]{1,0:T(8,128)(2,1)S(1)}, bf16[256,256]{1,0:T(8,128)(2,1)S(1)}, u32[]{:S(2)}, u32[]{:S(2)}) collective-permute-start(bf16[256,256]{1,0:T(8,128)(2,1)S(1)} %collective-permute-done.5.refs_2_), channel_id=1, source_target_pairs={{0,2},{1,3},{2,0},{3,1},{4,6},{5,7},{6,4},{7,5},{8,10},{9,11},{10,... | collective-permute-start | bytes 393224 | tf_op jit(solution)/shard_map/ppermute | solution.py:255
  64.6 1.7 %absorb.14.refs_4_ = f32[2,2,144,256]{3,2,1,0:T(8,128)S(1)} custom-call(bf16[384,256]{1,0:T(8,128)(2,1)S(1)} %collective-permute-done.refs_0_, bf16[384,256]{1,0:T(8,128)(2,1)S(1)} %collective-permute-done.1.refs_1_, bf16[512,256]{1,0:T(8,128)(2,1)S(1)} %collective-permute-done.22.refs_2_, bf16[512,256]{1,0:T(8,128)(2,1)S(1)} %collective-permute-done.17.refs_3_), custom_call_target="tpu_custom_call" | custom-call | flops 268435456 | bytes 786432 | tf_op jit(solution)/shard_map/absorb/pallas_call | solution.py:127
  66.3 1.8 %absorb.15.refs_4_ = f32[2,2,144,256]{3,2,1,0:T(8,128)S(1)} custom-call(bf16[384,256]{1,0:T(8,128)(2,1)S(1)} %collective-permute-done.refs_0_, bf16[384,256]{1,0:T(8,128)(2,1)S(1)} %collective-permute-done.1.refs_1_, bf16[512,256]{1,0:T(8,128)(2,1)S(1)} %collective-permute-done.20.refs_2_, ...), custom_call_target="tpu_custom_call", output_to_operand_aliasing={{}: (4, {})} | custom-call | flops 268435456 | bytes 786432 | tf_op jit(solution)/shard_map/absorb/pallas_call | solution.py:127
  68.1 1.8 %absorb.16.refs_4_ = f32[2,2,144,256]{3,2,1,0:T(8,128)S(1)} custom-call(bf16[384,256]{1,0:T(8,128)(2,1)S(1)} %collective-permute-done.refs_0_, bf16[384,256]{1,0:T(8,128)(2,1)S(1)} %collective-permute-done.1.refs_1_, bf16[512,256]{1,0:T(8,128)(2,1)S(1)} %collective-permute-done.15.refs_2_, ...), custom_call_target="tpu_custom_call", output_to_operand_aliasing={{}: (4, {})} | custom-call | flops 268435456 | bytes 786432 | tf_op jit(solution)/shard_map/absorb/pallas_call | solution.py:127
  69.9 1.9 %absorb.17 = (bf16[256,256]{1,0:T(8,128)(2,1)S(1)}, bf16[256,256]{1,0:T(8,128)(2,1)S(1)}) custom-call(bf16[384,256]{1,0:T(8,128)(2,1)S(1)} %collective-permute-done.refs_0_, bf16[384,256]{1,0:T(8,128)(2,1)S(1)} %collective-permute-done.1.refs_1_, bf16[512,256]{1,0:T(8,128)(2,1)S(1)} %collective-permute-done.16.refs_2_, ...), custom_call_target="tpu_custom_call" | custom-call | flops 268435456 | bytes 786432 | tf_op jit(solution)/shard_map/absorb/pallas_call | solution.py:127
  71.8 0.6 collective-permute-start.4
  72.4 8.1 %collective-permute-start.25 = (bf16[256,256]{1,0:T(8,128)(2,1)S(1)}, bf16[256,256]{1,0:T(8,128)(2,1)S(1)}, u32[]{:S(2)}, u32[]{:S(2)}) collective-permute-start(bf16[256,256]{1,0:T(8,128)(2,1)S(1)} %get-tuple-element.23), channel_id=1, source_target_pairs={{0,5},{1,4},{2,7},{3,6},{4,1},{5,0},{6,3},{7,2},{8,13},{9,12},{10,... | collective-permute-start | bytes 393224 | tf_op jit(solution)/shard_map/ppermute | solution.py:255
  80.4 4.7 %collective-permute-start.23 = (bf16[256,256]{1,0:T(8,128)(2,1)S(1)}, bf16[256,256]{1,0:T(8,128)(2,1)S(1)}, u32[]{:S(2)}, u32[]{:S(2)}) collective-permute-start(bf16[256,256]{1,0:T(8,128)(2,1)S(1)} %get-tuple-element.23), channel_id=1, source_target_pairs={{0,4},{1,5},{2,6},{3,7},{4,0},{5,1},{6,2},{7,3},{8,12},{9,13},{10,... | collective-permute-start | bytes 393224 | tf_op jit(solution)/shard_map/ppermute | solution.py:255
  85.2 0.5 collective-permute-start.24
  85.7 0.9 absorb.9.refs_4_
  86.7 1.0 absorb.10.refs_4_
  87.7 1.0 absorb.11.refs_3_
  88.6 0.7 absorb.12.refs_3_
  89.3 0.8 absorb.13
  90.2 3.5 %collective-permute-start.14 = (bf16[256,128]{1,0:T(8,128)(2,1)S(1)}, bf16[256,128]{1,0:T(8,128)(2,1)S(1)}, u32[]{:S(2)}, u32[]{:S(2)}) collective-permute-start(bf16[256,128]{1,0:T(8,128)(2,1)S(1)} %get-tuple-element.19), channel_id=1, source_target_pairs={{0,5},{1,4},{2,7},{3,6},{4,1},{5,0},{6,3},{7,2},{8,13},{9,12},{10,... | collective-permute-start | bytes 196616 | tf_op jit(solution)/shard_map/ppermute | solution.py:255
  93.7 0.6 collective-permute-start.12
  94.4 4.0 %project.2.refs_7_ = f32[256,1536]{1,0:T(8,128)S(1)} custom-call(s32[2]{0:T(128)S(1)} %pad_add_fusion.refs_0_, bf16[256,256]{1,0:T(8,128)(2,1)S(1)} %collective-permute-done.23.refs_1_, bf16[768,3072]{1,0:T(8,128)(2,1)} %collective-permute-done.11.refs_2_.refs_3_.refs_12_, bf16[768,3072]{1,0:T(8,128)(2,1)} %collective-permute-done.11.refs_2_.refs_3_.refs_12_, ...), custom_call_target="tpu_custom_call" | custom-call | flops 905969664 | bytes 1572864 | tf_op jit(solution)/shard_map/project/pallas_call | solution.py:198
  98.5 3.9 %project.3 = bf16[256,1536]{1,0:T(8,128)(2,1)} custom-call(s32[2]{0:T(128)S(1)} %pad_add_fusion.refs_0_, bf16[256,128]{1,0:T(8,128)(2,1)S(1)} %collective-permute-done.10.refs_1_, bf16[768,3072]{1,0:T(8,128)(2,1)} %collective-permute-done.11.refs_2_.refs_3_.refs_12_, bf16[256,128]{1,0:T(8,128)(2,1)S(1)} %collective-permute-done.12.refs_3_, ...), custom_call_target="tpu_custom_call" | custom-call | flops 301989888 | bytes 1572864 | tf_op jit(solution)/shard_map/project/pallas_call | solution.py:198
  (31 shorter events, 0.2 us)
Async XLA Ops:
  0.0 93.7 %collective-permute-start.11 = (bf16[768,3072]{1,0:T(8,128)(2,1)}, bf16[768,3072]{1,0:T(8,128)(2,1)}, u32[]{:S(2)}, u32[]{:S(2)}) collective-permute-start(bf16[768,3072]{1,0:T(8,128)(2,1)} %bitcast.13), channel_id=1, source_target_pairs={{0,16},{1,17},{2,18},{3,19},{4,20},{5,21},{6,22},{7,23},{8,24},{9,... | collective-permute-start | bytes 14155784 | tf_op jit(solution)/shard_map/ppermute | solution.py:255
  0.5 6.0 %copy-start.1 = (bf16[1,256,768]{2,1,0:T(8,128)(2,1)S(1)}, bf16[1,256,768]{2,1,0:T(8,128)(2,1)}, u32[]{:S(2)}) copy-start(bf16[1,256,768]{2,1,0:T(8,128)(2,1)} %param.8) | copy-start | bytes 1179652
  0.5 6.0 %copy-start.2 = (bf16[1,256,768]{2,1,0:T(8,128)(2,1)S(1)}, bf16[1,256,768]{2,1,0:T(8,128)(2,1)}, u32[]{:S(2)}) copy-start(bf16[1,256,768]{2,1,0:T(8,128)(2,1)} %param.9) | copy-start | bytes 1179652
  0.5 15.3 %copy-start = (bf16[1,256,768]{2,1,0:T(8,128)(2,1)S(1)}, bf16[1,256,768]{2,1,0:T(8,128)(2,1)}, u32[]{:S(2)}) copy-start(bf16[1,256,768]{2,1,0:T(8,128)(2,1)} %param.7) | copy-start | bytes 1179652
  3.9 89.9 %collective-permute-start.13 = (bf16[768,1536]{1,0:T(8,128)(2,1)}, bf16[768,1536]{1,0:T(8,128)(2,1)S(1)}, u32[]{:S(2)}, u32[]{:S(2)}) collective-permute-start(bf16[768,1536]{1,0:T(8,128)(2,1)} %dynamic-slice_bitcast_fusion), channel_id=1, source_target_pairs={{0,17},{1,16},{2,19},{3,18},{4,21},{5,20},{6,23},{7,22},{8,25},{9,... | collective-permute-start | bytes 7077896 | tf_op jit(solution)/shard_map/ppermute | solution.py:255
  6.7 5.7 %collective-permute-start.2 = (bf16[256,256]{1,0:T(8,128)(2,1)S(1)}, bf16[256,256]{1,0:T(8,128)(2,1)S(1)}, u32[]{:S(2)}, u32[]{:S(2)}) collective-permute-start(bf16[256,256]{1,0:T(8,128)(2,1)S(1)} %get-tuple-element.17), channel_id=1, source_target_pairs={{0,20},{1,21},{2,22},{3,23},{4,16},{5,17},{6,18},{7,19},{8,28},{9,... | collective-permute-start | bytes 393224 | tf_op jit(solution)/shard_map/ppermute | solution.py:255
  7.9 8.1 %collective-permute-start.9 = (bf16[256,256]{1,0:T(8,128)(2,1)S(1)}, bf16[256,256]{1,0:T(8,128)(2,1)S(1)}, u32[]{:S(2)}, u32[]{:S(2)}) collective-permute-start(bf16[256,256]{1,0:T(8,128)(2,1)S(1)} %get-tuple-element.18), channel_id=1, source_target_pairs={{0,16},{1,17},{2,18},{3,19},{4,20},{5,21},{6,22},{7,23},{8,24},{9,... | collective-permute-start | bytes 393224 | tf_op jit(solution)/shard_map/ppermute | solution.py:255
  8.4 7.9 %collective-permute-start.7 = (bf16[256,256]{1,0:T(8,128)(2,1)S(1)}, bf16[256,256]{1,0:T(8,128)(2,1)S(1)}, u32[]{:S(2)}, u32[]{:S(2)}) collective-permute-start(bf16[256,256]{1,0:T(8,128)(2,1)S(1)} %get-tuple-element.18), channel_id=1, source_target_pairs={{0,18},{1,19},{2,16},{3,17},{4,22},{5,23},{6,20},{7,21},{8,26},{9,... | collective-permute-start | bytes 393224 | tf_op jit(solution)/shard_map/ppermute | solution.py:255
  12.3 7.5 %collective-permute-start.5 = (bf16[256,256]{1,0:T(8,128)(2,1)S(1)}, bf16[256,256]{1,0:T(8,128)(2,1)S(1)}, u32[]{:S(2)}, u32[]{:S(2)}) collective-permute-start(bf16[256,256]{1,0:T(8,128)(2,1)S(1)} %get-tuple-element.18), channel_id=1, source_target_pairs={{0,28},{1,29},{2,30},{3,31},{4,24},{5,25},{6,26},{7,27},{8,20},{9,... | collective-permute-start | bytes 393224 | tf_op jit(solution)/shard_map/ppermute | solution.py:255
  16.0 5.3 %collective-permute-start = (bf16[384,256]{1,0:T(8,128)(2,1)S(1)}, bf16[384,256]{1,0:T(8,128)(2,1)S(1)}, u32[]{:S(2)}, u32[]{:S(2)}) collective-permute-start(bf16[384,256]{1,0:T(8,128)(2,1)S(1)} %get-tuple-element.15), channel_id=1, source_target_pairs={{0,16},{1,17},{2,18},{3,19},{4,20},{5,21},{6,22},{7,23},{8,24},{9,... | collective-permute-start | bytes 589832 | tf_op jit(solution)/shard_map/ppermute | solution.py:255
  16.3 7.9 %collective-permute-start.1 = (bf16[384,256]{1,0:T(8,128)(2,1)S(1)}, bf16[384,256]{1,0:T(8,128)(2,1)S(1)}, u32[]{:S(2)}, u32[]{:S(2)}) collective-permute-start(bf16[384,256]{1,0:T(8,128)(2,1)S(1)} %get-tuple-element.16), channel_id=1, source_target_pairs={{0,20},{1,21},{2,22},{3,23},{4,16},{5,17},{6,18},{7,19},{8,28},{9,... | collective-permute-start | bytes 589832 | tf_op jit(solution)/shard_map/ppermute | solution.py:255
  19.8 5.9 %collective-permute-start.8 = (bf16[256,256]{1,0:T(8,128)(2,1)S(1)}, bf16[256,256]{1,0:T(8,128)(2,1)S(1)}, u32[]{:S(2)}, u32[]{:S(2)}) collective-permute-start(bf16[256,256]{1,0:T(8,128)(2,1)S(1)} %collective-permute-done.2.refs_3_), channel_id=1, source_target_pairs={{0,2},{1,3},{2,0},{3,1},{4,6},{5,7},{6,4},{7,5},{8,10},{9,11},{10,... | collective-permute-start | bytes 393224 | tf_op jit(solution)/shard_map/ppermute | solution.py:255
  21.3 77.2 %collective-permute-start.26 = (bf16[256,3072]{1,0:T(8,128)(2,1)}, bf16[256,3072]{1,0:T(8,128)(2,1)S(1)}, u32[]{:S(2)}, u32[]{:S(2)}) collective-permute-start(bf16[256,3072]{1,0:T(8,128)(2,1)} %bitcast.14), channel_id=1, source_target_pairs={{0,16},{1,17},{2,18},{3,19},{4,20},{5,21},{6,22},{7,23},{8,24},{9,... | collective-permute-start | bytes 4718600 | tf_op jit(solution)/shard_map/ppermute | solution.py:255
  24.1 8.2 %collective-permute-start.17 = (bf16[512,256]{1,0:T(8,128)(2,1)S(1)}, bf16[512,256]{1,0:T(8,128)(2,1)S(1)}, u32[]{:S(2)}, u32[]{:S(2)}) collective-permute-start(bf16[512,256]{1,0:T(8,128)(2,1)S(1)} %get-tuple-element.22), channel_id=1, source_target_pairs={{0,20},{1,21},{2,22},{3,23},{4,16},{5,17},{6,18},{7,19},{8,28},{9,... | collective-permute-start | bytes 786440 | tf_op jit(solution)/shard_map/ppermute | solution.py:255
  25.7 8.3 %collective-permute-start.22 = (bf16[512,256]{1,0:T(8,128)(2,1)S(1)}, bf16[512,256]{1,0:T(8,128)(2,1)S(1)}, u32[]{:S(2)}, u32[]{:S(2)}) collective-permute-start(bf16[512,256]{1,0:T(8,128)(2,1)S(1)} %get-tuple-element.21), channel_id=1, source_target_pairs={{0,16},{1,17},{2,18},{3,19},{4,20},{5,21},{6,22},{7,23},{8,24},{9,... | collective-permute-start | bytes 786440 | tf_op jit(solution)/shard_map/ppermute | solution.py:255
  32.4 7.9 %collective-permute-start.20 = (bf16[512,256]{1,0:T(8,128)(2,1)S(1)}, bf16[512,256]{1,0:T(8,128)(2,1)S(1)}, u32[]{:S(2)}, u32[]{:S(2)}) collective-permute-start(bf16[512,256]{1,0:T(8,128)(2,1)S(1)} %get-tuple-element.21), channel_id=1, source_target_pairs={{0,18},{1,19},{2,16},{3,17},{4,22},{5,23},{6,20},{7,21},{8,26},{9,... | collective-permute-start | bytes 786440 | tf_op jit(solution)/shard_map/ppermute | solution.py:255
  34.0 10.3 %collective-permute-start.15 = (bf16[512,256]{1,0:T(8,128)(2,1)S(1)}, bf16[512,256]{1,0:T(8,128)(2,1)S(1)}, u32[]{:S(2)}, u32[]{:S(2)}) collective-permute-start(bf16[512,256]{1,0:T(8,128)(2,1)S(1)} %get-tuple-element.21), channel_id=1, source_target_pairs={{0,28},{1,29},{2,30},{3,31},{4,24},{5,25},{6,26},{7,27},{8,20},{9,... | collective-permute-start | bytes 786440 | tf_op jit(solution)/shard_map/ppermute | solution.py:255
  40.3 9.0 %collective-permute-start.21 = (bf16[512,256]{1,0:T(8,128)(2,1)S(1)}, bf16[512,256]{1,0:T(8,128)(2,1)S(1)}, u32[]{:S(2)}, u32[]{:S(2)}) collective-permute-start(bf16[512,256]{1,0:T(8,128)(2,1)S(1)} %collective-permute-done.17.refs_3_), channel_id=1, source_target_pairs={{0,2},{1,3},{2,0},{3,1},{4,6},{5,7},{6,4},{7,5},{8,10},{9,11},{10,... | collective-permute-start | bytes 786440 | tf_op jit(solution)/shard_map/ppermute | solution.py:255
  44.3 10.2 %collective-permute-start.18 = (bf16[512,256]{1,0:T(8,128)(2,1)S(1)}, bf16[512,256]{1,0:T(8,128)(2,1)S(1)}, u32[]{:S(2)}, u32[]{:S(2)}) collective-permute-start(bf16[512,256]{1,0:T(8,128)(2,1)S(1)} %collective-permute-done.17.refs_3_), channel_id=1, source_target_pairs={{0,12},{1,13},{2,14},{3,15},{4,8},{5,9},{6,10},{7,11},{8,4},{9,5},... | collective-permute-start | bytes 786440 | tf_op jit(solution)/shard_map/ppermute | solution.py:255
  49.3 9.2 %collective-permute-start.16 = (bf16[512,256]{1,0:T(8,128)(2,1)S(1)}, bf16[512,256]{1,0:T(8,128)(2,1)S(1)}, u32[]{:S(2)}, u32[]{:S(2)}) collective-permute-start(bf16[512,256]{1,0:T(8,128)(2,1)S(1)} %collective-permute-done.15.refs_2_), channel_id=1, source_target_pairs={{0,2},{1,3},{2,0},{3,1},{4,6},{5,7},{6,4},{7,5},{8,10},{9,11},{10,... | collective-permute-start | bytes 786440 | tf_op jit(solution)/shard_map/ppermute | solution.py:255
  54.5 8.6 %collective-permute-start.19 = (bf16[512,256]{1,0:T(8,128)(2,1)S(1)}, bf16[512,256]{1,0:T(8,128)(2,1)S(1)}, u32[]{:S(2)}, u32[]{:S(2)}) collective-permute-start(bf16[512,256]{1,0:T(8,128)(2,1)S(1)} %collective-permute-done.18.refs_3_), channel_id=1, source_target_pairs={{0,2},{1,3},{2,0},{3,1},{4,6},{5,7},{6,4},{7,5},{8,10},{9,11},{10,... | collective-permute-start | bytes 786440 | tf_op jit(solution)/shard_map/ppermute | solution.py:255
  58.5 13.3 %collective-permute-start.3 = (bf16[256,256]{1,0:T(8,128)(2,1)S(1)}, bf16[256,256]{1,0:T(8,128)(2,1)S(1)}, u32[]{:S(2)}, u32[]{:S(2)}) collective-permute-start(bf16[256,256]{1,0:T(8,128)(2,1)S(1)} %collective-permute-done.2.refs_3_), channel_id=1, source_target_pairs={{0,12},{1,13},{2,14},{3,15},{4,8},{5,9},{6,10},{7,11},{8,4},{9,5},... | collective-permute-start | bytes 393224 | tf_op jit(solution)/shard_map/ppermute | solution.py:255
  63.1 9.3 %collective-permute-start.6 = (bf16[256,256]{1,0:T(8,128)(2,1)S(1)}, bf16[256,256]{1,0:T(8,128)(2,1)S(1)}, u32[]{:S(2)}, u32[]{:S(2)}) collective-permute-start(bf16[256,256]{1,0:T(8,128)(2,1)S(1)} %collective-permute-done.5.refs_2_), channel_id=1, source_target_pairs={{0,2},{1,3},{2,0},{3,1},{4,6},{5,7},{6,4},{7,5},{8,10},{9,11},{10,... | collective-permute-start | bytes 393224 | tf_op jit(solution)/shard_map/ppermute | solution.py:255
  71.8 8.7 %collective-permute-start.4 = (bf16[256,256]{1,0:T(8,128)(2,1)S(1)}, bf16[256,256]{1,0:T(8,128)(2,1)S(1)}, u32[]{:S(2)}, u32[]{:S(2)}) collective-permute-start(bf16[256,256]{1,0:T(8,128)(2,1)S(1)} %collective-permute-done.3.refs_3_), channel_id=1, source_target_pairs={{0,2},{1,3},{2,0},{3,1},{4,6},{5,7},{6,4},{7,5},{8,10},{9,11},{10,... | collective-permute-start | bytes 393224 | tf_op jit(solution)/shard_map/ppermute | solution.py:255
  72.4 12.8 %collective-permute-start.25 = (bf16[256,256]{1,0:T(8,128)(2,1)S(1)}, bf16[256,256]{1,0:T(8,128)(2,1)S(1)}, u32[]{:S(2)}, u32[]{:S(2)}) collective-permute-start(bf16[256,256]{1,0:T(8,128)(2,1)S(1)} %get-tuple-element.23), channel_id=1, source_target_pairs={{0,5},{1,4},{2,7},{3,6},{4,1},{5,0},{6,3},{7,2},{8,13},{9,12},{10,... | collective-permute-start | bytes 393224 | tf_op jit(solution)/shard_map/ppermute | solution.py:255
  80.4 9.7 %collective-permute-start.23 = (bf16[256,256]{1,0:T(8,128)(2,1)S(1)}, bf16[256,256]{1,0:T(8,128)(2,1)S(1)}, u32[]{:S(2)}, u32[]{:S(2)}) collective-permute-start(bf16[256,256]{1,0:T(8,128)(2,1)S(1)} %get-tuple-element.23), channel_id=1, source_target_pairs={{0,4},{1,5},{2,6},{3,7},{4,0},{5,1},{6,2},{7,3},{8,12},{9,13},{10,... | collective-permute-start | bytes 393224 | tf_op jit(solution)/shard_map/ppermute | solution.py:255
  85.2 5.1 %collective-permute-start.24 = (bf16[256,256]{1,0:T(8,128)(2,1)S(1)}, bf16[256,256]{1,0:T(8,128)(2,1)S(1)}, u32[]{:S(2)}, u32[]{:S(2)}) collective-permute-start(bf16[256,256]{1,0:T(8,128)(2,1)S(1)} %get-tuple-element.24.refs_10_), channel_id=1, source_target_pairs={{0,1},{1,0},{2,3},{3,2},{4,5},{5,4},{6,7},{7,6},{8,9},{9,8},{10,11... | collective-permute-start | bytes 393224 | tf_op jit(solution)/shard_map/ppermute | solution.py:255
  86.7 3.5 %copy-start.3 = (f32[1,3072]{1,0:T(1,128)S(1)}, f32[1,3072]{1,0:T(1,128)}, u32[]{:S(2)}) copy-start(f32[1,3072]{1,0:T(1,128)} %param.11) | copy-start | bytes 36868
  90.2 8.3 %collective-permute-start.27 = (f32[1,3072]{1,0:T(1,128)S(1)}, f32[1,3072]{1,0:T(1,128)S(1)}, u32[]{:S(2)}, u32[]{:S(2)}) collective-permute-start(f32[1,3072]{1,0:T(1,128)S(1)} %copy-done.3), channel_id=1, source_target_pairs={{0,16},{1,17},{2,18},{3,19},{4,20},{5,21},{6,22},{7,23},{8,24},{9,... | collective-permute-start | bytes 36872 | tf_op jit(solution)/shard_map/ppermute | solution.py:255
  90.2 8.2 %collective-permute-start.14 = (bf16[256,128]{1,0:T(8,128)(2,1)S(1)}, bf16[256,128]{1,0:T(8,128)(2,1)S(1)}, u32[]{:S(2)}, u32[]{:S(2)}) collective-permute-start(bf16[256,128]{1,0:T(8,128)(2,1)S(1)} %get-tuple-element.19), channel_id=1, source_target_pairs={{0,5},{1,4},{2,7},{3,6},{4,1},{5,0},{6,3},{7,2},{8,13},{9,12},{10,... | collective-permute-start | bytes 196616 | tf_op jit(solution)/shard_map/ppermute | solution.py:255
  93.7 4.7 %collective-permute-start.10 = (bf16[256,128]{1,0:T(8,128)(2,1)S(1)}, bf16[256,128]{1,0:T(8,128)(2,1)S(1)}, u32[]{:S(2)}, u32[]{:S(2)}) collective-permute-start(bf16[256,128]{1,0:T(8,128)(2,1)S(1)} %get-tuple-element.19), channel_id=1, source_target_pairs={{0,4},{1,5},{2,6},{3,7},{4,0},{5,1},{6,2},{7,3},{8,12},{9,13},{10,... | collective-permute-start | bytes 196616 | tf_op jit(solution)/shard_map/ppermute | solution.py:255
  93.7 4.7 %collective-permute-start.12 = (bf16[256,128]{1,0:T(8,128)(2,1)S(1)}, bf16[256,128]{1,0:T(8,128)(2,1)S(1)}, u32[]{:S(2)}, u32[]{:S(2)}) collective-permute-start(bf16[256,128]{1,0:T(8,128)(2,1)S(1)} %get-tuple-element.20.refs_11_), channel_id=1, source_target_pairs={{0,1},{1,0},{2,3},{3,2},{4,5},{5,4},{6,7},{7,6},{8,9},{9,8},{10,11... | collective-permute-start | bytes 196616 | tf_op jit(solution)/shard_map/ppermute | solution.py:255

commit v3 on v2

--- a/solution.py
+++ b/solution.py
@@ -140,66 +140,44 @@
     )(*operands)
 
 
-def project_kernel(uses, finish, *refs):
+def project_kernel(pieces, *refs):
     out = refs[-1]
-    refs = list(refs[1:-1])
+    refs = refs[1:-1]
     total = None
-    if finish:
-        total = refs[-3][...]
-    for weight_count, pieces in uses:
-        lefts = [refs.pop(0)[...] for _ in range(pieces)]
-        rights = [refs.pop(0)[...] for _ in range(weight_count)]
-        left = lefts[0] if pieces == 1 else jnp.concatenate(lefts, axis=1)
-        right = rights[0] if weight_count == 1 else jnp.concatenate(rights, axis=0)
-        term = jnp.dot(left, right, preferred_element_type=jnp.float32)
+    for at in range(pieces):
+        term = jnp.dot(
+            refs[2 * at][...], refs[2 * at + 1][...], preferred_element_type=jnp.float32
+        )
         total = term if total is None else total + term
-    if finish:
-        stream, gate = refs[-2], refs[-1]
-        total = stream[...].astype(jnp.float32) + gate[...] * total
-    out[...] = total.astype(out.dtype)
-
-
-def project(where, sources, cols, wide, finishing=None):
-    rows = sources[0][0][0].shape[0]
+    base, gate = refs[-2], refs[-1]
+    out[...] = (base[...].astype(jnp.float32) + gate[...] * total).astype(out.dtype)
+
+
+def project(where, sources, base, gate, cols, wide, dtype):
+    rows = base.shape[0]
     steps = cols // wide
-    operands, specs, uses = [], [], []
-    for pieces, weight, whole, flip, heads in sources:
-        for piece in pieces:
-            operands.append(piece)
-            specs.append(pl.BlockSpec(piece.shape, lambda j, s: (0, 0)))
-        per_role = weight.shape[0] // HD // 2
-
-        def place(j, s, head, whole=whole, flip=flip, per_role=per_role, unit=HD):
-            role = 1 - s[1] if flip else s[1]
-            at = role if unit != HD else role * per_role + head
-            return at, (s[0] * steps + j if whole else j)
-
-        if tuple(heads) == tuple(range(per_role)):
-            operands.append(weight)
-            specs.append(
-                pl.BlockSpec(
-                    (per_role * HD, wide), functools.partial(place, head=0, unit=per_role * HD)
-                )
-            )
-            uses.append((1, len(pieces)))
-        else:
-            for head in heads:
-                operands.append(weight)
-                specs.append(pl.BlockSpec((HD, wide), functools.partial(place, head=head)))
-            uses.append((len(heads), len(pieces)))
-    if finishing is not None:
-        operands += list(finishing)
-        specs += [
-            pl.BlockSpec((rows, wide), lambda j, s: (0, j)),
-            pl.BlockSpec((rows, wide), lambda j, s: (0, s[0] * steps + j)),
-            pl.BlockSpec((1, wide), lambda j, s: (0, s[0] * steps + j)),
-        ]
-    depth = sum(len(source[4]) for source in sources) * HD
+    operands, specs, depth = [], [], 0
+    for piece, lane, weight, row, whole in sources:
+        width = piece.shape[1] if lane is None else HD
+        depth += width
+
+        def left(j, s, lane=lane):
+            return 0, (0 if lane is None else lane(s))
+
+        def right(j, s, row=row, whole=whole):
+            return row(s), (s[0] * steps + j if whole else j)
+
+        operands += [piece, weight]
+        specs += [pl.BlockSpec((rows, width), left), pl.BlockSpec((width, wide), right)]
+    whole = base.shape[1] != cols
+    operands += [base, gate]
+    specs += [
+        pl.BlockSpec((rows, wide), lambda j, s: (0, s[0] * steps + j if whole else j)),
+        pl.BlockSpec((1, wide), lambda j, s: (0, s[0] * steps + j)),
+    ]
     return pl.pallas_call(
-        functools.partial(project_kernel, uses, finishing is not None),
-        out_shape=jax.ShapeDtypeStruct(
-            (rows, cols), jnp.float32 if finishing is None else jnp.bfloat16
-        ),
+        functools.partial(project_kernel, len(sources)),
+        out_shape=jax.ShapeDtypeStruct((rows, cols), dtype),
         grid_spec=pltpu.PrefetchScalarGridSpec(
             num_scalar_prefetch=1,
             grid=(steps,),
@@ -258,11 +236,26 @@
     share = lax.axis_index("head").astype(jnp.int32)
     role = role_of(lax.axis_index("seq").astype(jnp.int32) // stride)
     role_ref = role.reshape(1)
-    where = jnp.stack([share, role])
-
-    early = local - max(1, local // 3)
-    groups = [tuple(range(early)), tuple(range(early, local))] if early else [tuple(range(local))]
+    column = lax.axis_index("seq").astype(jnp.int32) // stride % 2
+    where = jnp.stack([share, role, column])
+    groups = [(0, 1), (2,)]
     everyone = range(len(groups))
+
+    col_count = out_weight.shape[2] // shares
+    lent = {}
+    for by in range(1, shares):
+        start = lax.rem(share + by, shares) * col_count
+
+        def rows_at(head, count):
+            return lax.dynamic_slice(
+                out_weight[0], (head * HD, start), (count * HD, col_count)
+            )
+
+        lent[by] = [
+            hop(rows_at(role * local + 1 - column, 1), still, 1, by),
+            hop(rows_at(role * local + 2, 1), still, 1, by),
+            hop(rows_at((1 - role) * local, 2), still, 1, by),
+        ]
 
     packed = pack(role_ref, keys[0], values[0], groups)
     mine, give = packed[: len(groups)], packed[len(groups) :]
@@ -271,22 +264,19 @@
     far = [[None] * 2 for _ in groups]
     near = [[None] * 2 for _ in groups]
     own = [None] * len(groups)
+    everyone = range(len(groups))
     for g in everyone:
         got[g] = hop(give[g], partner, 1)
         far[g][0] = hop(mine[g], beyond, 1)
         near[g][0] = hop(mine[g], beside, 1)
         own[g] = hop(mine[g], still, 1)
     asking = [hop(my_query, still, 1), hop(give_query, partner, 1)]
-
-    col_count = out_weight.shape[2] // shares
-    weights = {}
-    for by in range(1, shares):
-        start = lax.rem(share + by, shares) * col_count
-        part = lax.dynamic_slice_in_dim(out_weight[0], start, col_count, 1)
-        weights[by] = hop(part, still, 1, by)
-    weights[0] = hop(out_weight[0], still, 1)
+    weight = hop(out_weight[0], still, 1)
     stream = hop(stream_in[0], still, 1)
     gate = hop(gate_scale, still, 1)
+    for by in range(1, shares):
+        lent[by].append(hop(lent[by][0], beside))
+        lent[by].append(hop(lent[by][1], partner))
 
     def fold(g, blocks, held, last=False):
         return absorb(asking, blocks, groups[g], held, last)
@@ -313,27 +303,37 @@
                 attended.append(fold(g, onward[1:], state, True))
             arrived = following
 
-    sources, late = [], []
+    home = []
     for g in everyone:
         ours, theirs = attended[g]
         back = hop(theirs, partner)
-        pieces = [(ours, 0, False), (back, 0, True)]
-        for by in range(1, shares):
-            pieces.append((hop(ours, still, 0, by), by, False))
-            pieces.append((hop(theirs, partner, 0, by), by, True))
-        for piece, by, flip in pieces:
-            source = ([piece], weights[by], by == 0, flip, groups[g])
-            if g == len(groups) - 1 and (by or flip):
-                late.append(source)
-            else:
-                sources.append(source)
-    if len(groups) > 1:
-        mergeable = [source for source in sources if source[2] and not source[3]]
-        sources = [source for source in sources if not (source[2] and not source[3])]
-        merged = [source[0][0] for source in mergeable]
-        sources.append((merged, weights[0], True, False, sum((s[4] for s in mergeable), ())))
-    total = project(where, sources, col_count, 512)
-    return project(where, late, col_count, 512, (total, stream, gate))[None]
+        over = {by: hop(ours, still, 0, by) for by in range(1, shares)}
+        cross = {by: hop(theirs, partner, 0, by) for by in range(1, shares)}
+        home.append((ours, back, over, cross))
+
+    def top(s):
+        return 0
+
+    def third(role):
+        return role * local + 2
+
+    first, second = home
+    sources = []
+    for head in range(2):
+        pick = lambda s, head=head: head
+        sources.append((first[0], pick, weight, lambda s, h=head: s[1] * local + h, True))
+        sources.append((first[1], pick, weight, lambda s, h=head: (1 - s[1]) * local + h, True))
+    sources.append((second[0], None, weight, lambda s: third(s[1]), True))
+    final = [(second[1], None, weight, lambda s: third(1 - s[1]), True)]
+    for by in range(1, shares):
+        fetched, thirds, pairs, relayed, others = lent[by]
+        sources.append((first[2][by], lambda s: 1 - s[2], fetched, top, False))
+        sources.append((first[2][by], lambda s: s[2], relayed, top, False))
+        sources.append((first[3][by], None, pairs, top, False))
+        final.append((second[2][by], None, thirds, top, False))
+        final.append((second[3][by], None, others, top, False))
+    base = project(where, sources, stream, gate, col_count, 512, jnp.float32)
+    return project(where, final, base, gate, col_count, 512, jnp.bfloat16)[None]
 
 
 def solution(mesh):

time: 103 us -> 120 us (1.17)
  waiting for transfers between devices: 36.6 us -> 43.7 us
  local copies, waits for them, and re-layouts: 3.38 us -> 9.53 us
  Pallas kernels: 19.8 us -> 22.1 us
  starting transfers between devices: 42.4 us -> 44.1 us
    ppermute x28 -> x32, waiting for transfers between devices: 36.6 us -> 43.7 us  [hop(): return lax.ppermute(block, ('segment', 'seq', 'head'), pairs)]
    unnamed x8 -> x30, local copies, waits for them, and re-layouts: 0.02 us -> 6.26 us
    pallas_call x9, Pallas kernels: 11.5 us -> 13.4 us  [absorb(): pl.pallas_call(functools.partial(absorb_kernel, heads, len(blocks), first...]
    ppermute x28 -> x32, starting transfers between devices: 42.4 us -> 44.1 us  [hop(): return lax.ppermute(block, ('segment', 'seq', 'head'), pairs)]
    dynamic_slice x1 -> x2, local copies, waits for them, and re-layouts: 3.36 us -> 3.28 us  [rows_at(): lax.dynamic_slice(out_weight[0], (head * HD, start), (count * HD, col_cou...]
  transfers between devices with their start and end apart: 28 -> 32, of which waited for: 10 -> 12; matrix products, arithmetic and copies ran while one was open for 3% -> 3% of each run, Pallas kernels for 16% -> 15%
where the time goes in v3:
time: 120 us
  starting transfers between devices  44.1 us (37%)
  waiting for transfers between devices  43.7 us (36%)
  Pallas kernels  22.1 us (18%)
  local copies, waits for them, and re-layouts  9.53 us (8%)
    ppermute x32, starting transfers between devices, hop(): return lax.ppermute(block, ('segment', 'seq', 'head'), pairs)  44.1 us
    ppermute x32, waiting for transfers between devices, hop(): return lax.ppermute(block, ('segment', 'seq', 'head'), pairs)  43.7 us
    pallas_call x9, Pallas kernels, absorb(): pl.pallas_call(functools.partial(absorb_kernel, heads, len(blocks), first...  13.4 us
    pallas_call x2, Pallas kernels, project(): pl.pallas_call(functools.partial(project_kernel, len(sources)), out_shape...  8.41 us
    unnamed x30, local copies, waits for them, and re-layouts  6.26 us
    dynamic_slice x2, local copies, waits for them, and re-layouts, rows_at(): lax.dynamic_slice(out_weight[0], (head * HD, start), (count * HD, col_cou...  3.28 us
  transfers between devices with their start and end apart: 32, of which 12 were waited for; matrix products, arithmetic and copies ran while one was open for 3% of the time, Pallas kernels for 15%

profile of v3, /device:TPU:0, one launch (start us, length us, event | category | flops | bytes accessed | tf_op | source)
XLA Modules:
  0.0 119.7 jit_solution(4376107850878173829)
XLA Ops:
  0.5 1.0 copy-done.1
  1.5 1.0 copy-done.2
  2.7 2.7 %collective-permute-start.2 = (bf16[256,256]{1,0:T(8,128)(2,1)S(1)}, bf16[256,256]{1,0:T(8,128)(2,1)S(1)}, u32[]{:S(2)}, u32[]{:S(2)}) collective-permute-start(bf16[256,256]{1,0:T(8,128)(2,1)S(1)} %get-tuple-element.17), channel_id=1, source_target_pairs={{0,20},{1,21},{2,22},{3,23},{4,16},{5,17},{6,18},{7,19},{8,28},{9,... | collective-permute-start | bytes 393224 | tf_op jit(solution)/shard_map/ppermute | solution.py:233
  5.9 1.0 copy-done
  7.1 1.3 %collective-permute-done.31.refs_18_.refs_8_ = f32[1,3072]{1,0:T(1,128)S(1)} collective-permute-done((f32[1,3072]{1,0:T(1,128)}, f32[1,3072]{1,0:T(1,128)S(1)}, u32[]{:S(2)}, u32[]{:S(2)}) %collective-permute-start.31) | collective-permute-done | bytes 12320 | tf_op jit(solution)/shard_map/ppermute | solution.py:233
  8.4 2.7 %collective-permute-start.1 = (bf16[384,256]{1,0:T(8,128)(2,1)S(1)}, bf16[384,256]{1,0:T(8,128)(2,1)S(1)}, u32[]{:S(2)}, u32[]{:S(2)}) collective-permute-start(bf16[384,256]{1,0:T(8,128)(2,1)S(1)} %get-tuple-element.16), channel_id=1, source_target_pairs={{0,20},{1,21},{2,22},{3,23},{4,16},{5,17},{6,18},{7,19},{8,28},{9,... | collective-permute-start | bytes 589832 | tf_op jit(solution)/shard_map/ppermute | solution.py:233
  11.1 1.5 %collective-permute-start.7 = (bf16[256,256]{1,0:T(8,128)(2,1)S(1)}, bf16[256,256]{1,0:T(8,128)(2,1)S(1)}, u32[]{:S(2)}, u32[]{:S(2)}) collective-permute-start(bf16[256,256]{1,0:T(8,128)(2,1)S(1)} %get-tuple-element.18), channel_id=1, source_target_pairs={{0,18},{1,19},{2,16},{3,17},{4,22},{5,23},{6,20},{7,21},{8,26},{9,... | collective-permute-start | bytes 393224 | tf_op jit(solution)/shard_map/ppermute | solution.py:233
  12.6 0.7 copy-done.13
  13.3 2.2 %collective-permute-start.5 = (bf16[256,256]{1,0:T(8,128)(2,1)S(1)}, bf16[256,256]{1,0:T(8,128)(2,1)}, u32[]{:S(2)}, u32[]{:S(2)}) collective-permute-start(bf16[256,256]{1,0:T(8,128)(2,1)S(1)} %get-tuple-element.18), channel_id=1, source_target_pairs={{0,28},{1,29},{2,30},{3,31},{4,24},{5,25},{6,26},{7,27},{8,20},{9,... | collective-permute-start | bytes 393224 | tf_op jit(solution)/shard_map/ppermute | solution.py:233
  15.5 0.9 collective-permute-done.7.refs_2_
  16.4 0.7 copy-done.5
  17.6 4.3 %collective-permute-done.5.refs_2_ = bf16[256,256]{1,0:T(8,128)(2,1)} collective-permute-done((bf16[256,256]{1,0:T(8,128)(2,1)S(1)}, bf16[256,256]{1,0:T(8,128)(2,1)}, u32[]{:S(2)}, u32[]{:S(2)}) %collective-permute-start.5) | collective-permute-done | bytes 131104 | tf_op jit(solution)/shard_map/ppermute | solution.py:233
  22.0 1.4 %collective-permute-start.21 = (bf16[512,256]{1,0:T(8,128)(2,1)S(1)}, bf16[512,256]{1,0:T(8,128)(2,1)S(1)}, u32[]{:S(2)}, u32[]{:S(2)}) collective-permute-start(bf16[512,256]{1,0:T(8,128)(2,1)S(1)} %get-tuple-element.21), channel_id=1, source_target_pairs={{0,18},{1,19},{2,16},{3,17},{4,22},{5,23},{6,20},{7,21},{8,26},{9,... | collective-permute-start | bytes 786440 | tf_op jit(solution)/shard_map/ppermute | solution.py:233
  23.3 1.4 %collective-permute-start.16 = (bf16[512,256]{1,0:T(8,128)(2,1)S(1)}, bf16[512,256]{1,0:T(8,128)(2,1)S(1)}, u32[]{:S(2)}, u32[]{:S(2)}) collective-permute-start(bf16[512,256]{1,0:T(8,128)(2,1)S(1)} %get-tuple-element.21), channel_id=1, source_target_pairs={{0,28},{1,29},{2,30},{3,31},{4,24},{5,25},{6,26},{7,27},{8,20},{9,... | collective-permute-start | bytes 786440 | tf_op jit(solution)/shard_map/ppermute | solution.py:233
  24.7 2.8 %collective-permute-done.18.refs_3_ = bf16[512,256]{1,0:T(8,128)(2,1)S(1)} collective-permute-done((bf16[512,256]{1,0:T(8,128)(2,1)S(1)}, bf16[512,256]{1,0:T(8,128)(2,1)S(1)}, u32[]{:S(2)}, u32[]{:S(2)}) %collective-permute-start.18) | collective-permute-done | bytes 262176 | tf_op jit(solution)/shard_map/ppermute | solution.py:233
  27.7 1.6 %collective-permute-start.8 = (bf16[256,256]{1,0:T(8,128)(2,1)S(1)}, bf16[256,256]{1,0:T(8,128)(2,1)S(1)}, u32[]{:S(2)}, u32[]{:S(2)}) collective-permute-start(bf16[256,256]{1,0:T(8,128)(2,1)S(1)} %collective-permute-done.2.refs_3_), channel_id=1, source_target_pairs={{0,2},{1,3},{2,0},{3,1},{4,6},{5,7},{6,4},{7,5},{8,10},{9,11},{10,... | collective-permute-start | bytes 393224 | tf_op jit(solution)/shard_map/ppermute | solution.py:233
  29.2 0.8 collective-permute-done.21.refs_2_
  30.0 5.9 %collective-permute-start.3 = (bf16[256,256]{1,0:T(8,128)(2,1)S(1)}, bf16[256,256]{1,0:T(8,128)(2,1)}, u32[]{:S(2)}, u32[]{:S(2)}) collective-permute-start(bf16[256,256]{1,0:T(8,128)(2,1)S(1)} %collective-permute-done.2.refs_3_), channel_id=1, source_target_pairs={{0,12},{1,13},{2,14},{3,15},{4,8},{5,9},{6,10},{7,11},{8,4},{9,5},... | collective-permute-start | bytes 393224 | tf_op jit(solution)/shard_map/ppermute | solution.py:233
  36.7 2.1 %dynamic-slice_bitcast_fusion.1 = (bf16[128,1536]{1,0:T(8,128)(2,1)}, bf16[128,1536]{1,0:T(8,128)(2,1)}) fusion(bf16[1,768,3072]{2,1,0:T(8,128)(2,1)} %param.10, s32[]{:T(128)S(6)} %select_n.40, s32[]{:T(128)S(6)} %select_n.39, s32[]{:T(128)S(6)} %select_n.38), kind=kLoop, calls=%fused_computation.1 | loop fusion | bytes 1572876 | tf_op jit(solution)/shard_map/dynamic_slice | solution.py:250
  40.0 1.2 collective-permute-start.13
  41.8 0.7 copy-done.9
  42.5 1.3 %collective-permute-start.4 = (bf16[256,256]{1,0:T(8,128)(2,1)}, bf16[256,256]{1,0:T(8,128)(2,1)}, u32[]{:S(2)}, u32[]{:S(2)}) collective-permute-start(bf16[256,256]{1,0:T(8,128)(2,1)} %collective-permute-done.3.refs_3_), channel_id=1, source_target_pairs={{0,2},{1,3},{2,0},{3,1},{4,6},{5,7},{6,4},{7,5},{8,10},{9,11},{10,... | collective-permute-start | bytes 393224 | tf_op jit(solution)/shard_map/ppermute | solution.py:233
  43.8 4.0 %collective-permute-done.4.refs_2_ = bf16[256,256]{1,0:T(8,128)(2,1)} collective-permute-done((bf16[256,256]{1,0:T(8,128)(2,1)}, bf16[256,256]{1,0:T(8,128)(2,1)}, u32[]{:S(2)}, u32[]{:S(2)}) %collective-permute-start.4) | collective-permute-done | bytes 131104 | tf_op jit(solution)/shard_map/ppermute | solution.py:233
  47.7 1.7 %collective-permute-start.22 = (bf16[512,256]{1,0:T(8,128)(2,1)S(1)}, bf16[512,256]{1,0:T(8,128)(2,1)S(1)}, u32[]{:S(2)}, u32[]{:S(2)}) collective-permute-start(bf16[512,256]{1,0:T(8,128)(2,1)S(1)} %collective-permute-done.18.refs_3_), channel_id=1, source_target_pairs={{0,2},{1,3},{2,0},{3,1},{4,6},{5,7},{6,4},{7,5},{8,10},{9,11},{10,... | collective-permute-start | bytes 786440 | tf_op jit(solution)/shard_map/ppermute | solution.py:233
  49.4 1.2 dynamic-slice_bitcast_fusion
  51.0 1.8 %collective-permute-start.19 = (bf16[512,256]{1,0:T(8,128)(2,1)S(1)}, bf16[512,256]{1,0:T(8,128)(2,1)S(1)}, u32[]{:S(2)}, u32[]{:S(2)}) collective-permute-start(bf16[512,256]{1,0:T(8,128)(2,1)S(1)} %collective-permute-done.18.refs_3_), channel_id=1, source_target_pairs={{0,12},{1,13},{2,14},{3,15},{4,8},{5,9},{6,10},{7,11},{8,4},{9,5},... | collective-permute-start | bytes 786440 | tf_op jit(solution)/shard_map/ppermute | solution.py:233
  52.7 6.7 %collective-permute-done.13.refs_4_ = bf16[128,1536]{1,0:T(8,128)(2,1)S(1)} collective-permute-done((bf16[128,1536]{1,0:T(8,128)(2,1)}, bf16[128,1536]{1,0:T(8,128)(2,1)S(1)}, u32[]{:S(2)}, u32[]{:S(2)}) %collective-permute-start.13) | collective-permute-done | bytes 393248 | tf_op jit(solution)/shard_map/ppermute | solution.py:233
  60.0 1.4 %collective-permute-start.17 = (bf16[512,256]{1,0:T(8,128)(2,1)}, bf16[512,256]{1,0:T(8,128)(2,1)S(1)}, u32[]{:S(2)}, u32[]{:S(2)}) collective-permute-start(bf16[512,256]{1,0:T(8,128)(2,1)} %copy-done.3), channel_id=1, source_target_pairs={{0,2},{1,3},{2,0},{3,1},{4,6},{5,7},{6,4},{7,5},{8,10},{9,11},{10,... | collective-permute-start | bytes 786440 | tf_op jit(solution)/shard_map/ppermute | solution.py:233
  61.3 1.9 %collective-permute-start.27 = (bf16[128,1536]{1,0:T(8,128)(2,1)S(1)}, bf16[128,1536]{1,0:T(8,128)(2,1)S(1)}, u32[]{:S(2)}, u32[]{:S(2)}) collective-permute-start(bf16[128,1536]{1,0:T(8,128)(2,1)S(1)} %collective-permute-done.26.refs_12_), channel_id=1, source_target_pairs={{0,2},{1,3},{2,0},{3,1},{4,6},{5,7},{6,4},{7,5},{8,10},{9,11},{10,... | collective-permute-start | bytes 1179656 | tf_op jit(solution)/shard_map/ppermute | solution.py:233
  63.3 6.1 %collective-permute-done.17.refs_2_ = bf16[512,256]{1,0:T(8,128)(2,1)S(1)} collective-permute-done((bf16[512,256]{1,0:T(8,128)(2,1)}, bf16[512,256]{1,0:T(8,128)(2,1)S(1)}, u32[]{:S(2)}, u32[]{:S(2)}) %collective-permute-start.17) | collective-permute-done | bytes 262176 | tf_op jit(solution)/shard_map/ppermute | solution.py:233
  69.4 1.3 %collective-permute-start.20 = (bf16[512,256]{1,0:T(8,128)(2,1)S(1)}, bf16[512,256]{1,0:T(8,128)(2,1)S(1)}, u32[]{:S(2)}, u32[]{:S(2)}) collective-permute-start(bf16[512,256]{1,0:T(8,128)(2,1)S(1)} %collective-permute-done.19.refs_3_), channel_id=1, source_target_pairs={{0,2},{1,3},{2,0},{3,1},{4,6},{5,7},{6,4},{7,5},{8,10},{9,11},{10,... | collective-permute-start | bytes 786440 | tf_op jit(solution)/shard_map/ppermute | solution.py:233
  70.7 1.7 %absorb.14.refs_4_ = f32[2,2,144,256]{3,2,1,0:T(8,128)S(1)} custom-call(bf16[384,256]{1,0:T(8,128)(2,1)S(1)} %collective-permute-done.refs_0_, bf16[384,256]{1,0:T(8,128)(2,1)S(1)} %collective-permute-done.1.refs_1_, bf16[512,256]{1,0:T(8,128)(2,1)S(1)} %collective-permute-done.23.refs_2_, bf16[512,256]{1,0:T(8,128)(2,1)S(1)} %collective-permute-done.18.refs_3_), custom_call_target="tpu_custom_call" | custom-call | flops 268435456 | bytes 786432 | tf_op jit(solution)/shard_map/absorb/pallas_call | solution.py:127
  72.4 1.8 %absorb.15.refs_4_ = f32[2,2,144,256]{3,2,1,0:T(8,128)S(1)} custom-call(bf16[384,256]{1,0:T(8,128)(2,1)S(1)} %collective-permute-done.refs_0_, bf16[384,256]{1,0:T(8,128)(2,1)S(1)} %collective-permute-done.1.refs_1_, bf16[512,256]{1,0:T(8,128)(2,1)S(1)} %collective-permute-done.21.refs_2_, ...), custom_call_target="tpu_custom_call", output_to_operand_aliasing={{}: (4, {})} | custom-call | flops 268435456 | bytes 786432 | tf_op jit(solution)/shard_map/absorb/pallas_call | solution.py:127
  74.2 1.8 %absorb.16.refs_4_ = f32[2,2,144,256]{3,2,1,0:T(8,128)S(1)} custom-call(bf16[384,256]{1,0:T(8,128)(2,1)S(1)} %collective-permute-done.refs_0_, bf16[384,256]{1,0:T(8,128)(2,1)S(1)} %collective-permute-done.1.refs_1_, bf16[512,256]{1,0:T(8,128)(2,1)S(1)} %copy-done.4, ...), custom_call_target="tpu_custom_call", output_to_operand_aliasing={{}: (4, {})} | custom-call | flops 268435456 | bytes 786432 | tf_op jit(solution)/shard_map/absorb/pallas_call | solution.py:127
  76.0 7.2 %collective-permute-done.20.refs_3_ = bf16[512,256]{1,0:T(8,128)(2,1)S(1)} collective-permute-done((bf16[512,256]{1,0:T(8,128)(2,1)S(1)}, bf16[512,256]{1,0:T(8,128)(2,1)S(1)}, u32[]{:S(2)}, u32[]{:S(2)}) %collective-permute-start.20) | collective-permute-done | bytes 262176 | tf_op jit(solution)/shard_map/ppermute | solution.py:233
  83.2 5.0 %collective-permute-start.15 = (bf16[128,1536]{1,0:T(8,128)(2,1)S(1)}, bf16[128,1536]{1,0:T(8,128)(2,1)S(1)}, u32[]{:S(2)}, u32[]{:S(2)}) collective-permute-start(bf16[128,1536]{1,0:T(8,128)(2,1)S(1)} %collective-permute-done.13.refs_4_), channel_id=1, source_target_pairs={{0,4},{1,5},{2,6},{3,7},{4,0},{5,1},{6,2},{7,3},{8,12},{9,13},{10,... | collective-permute-start | bytes 1179656 | tf_op jit(solution)/shard_map/ppermute | solution.py:233
  88.2 1.8 %absorb.17 = (bf16[256,256]{1,0:T(8,128)(2,1)S(1)}, bf16[256,256]{1,0:T(8,128)(2,1)S(1)}) custom-call(bf16[384,256]{1,0:T(8,128)(2,1)S(1)} %collective-permute-done.refs_0_, bf16[384,256]{1,0:T(8,128)(2,1)S(1)} %collective-permute-done.1.refs_1_, bf16[512,256]{1,0:T(8,128)(2,1)S(1)} %collective-permute-done.17.refs_2_, ...), custom_call_target="tpu_custom_call" | custom-call | flops 268435456 | bytes 786432 | tf_op jit(solution)/shard_map/absorb/pallas_call | solution.py:127
  90.2 1.9 %collective-permute-start.28 = (bf16[256,256]{1,0:T(8,128)(2,1)S(1)}, bf16[256,256]{1,0:T(8,128)(2,1)S(1)}, u32[]{:S(2)}, u32[]{:S(2)}) collective-permute-start(bf16[256,256]{1,0:T(8,128)(2,1)S(1)} %get-tuple-element.24), channel_id=1, source_target_pairs={{0,5},{1,4},{2,7},{3,6},{4,1},{5,0},{6,3},{7,2},{8,13},{9,12},{10,... | collective-permute-start | bytes 393224 | tf_op jit(solution)/shard_map/ppermute | solution.py:233
  92.1 8.7 %collective-permute-done.24.refs_3_.refs_7_ = bf16[256,256]{1,0:T(8,128)(2,1)S(1)} collective-permute-done((bf16[256,256]{1,0:T(8,128)(2,1)S(1)}, bf16[256,256]{1,0:T(8,128)(2,1)S(1)}, u32[]{:S(2)}, u32[]{:S(2)}) %collective-permute-start.24) | collective-permute-done | bytes 131104 | tf_op jit(solution)/shard_map/ppermute | solution.py:233
  101.4 0.9 absorb.9.refs_4_
  102.4 1.0 absorb.10.refs_4_
  103.3 1.9 %absorb.11.refs_3_ = f32[1,2,144,256]{3,2,1,0:T(8,128)S(1)} custom-call(bf16[384,256]{1,0:T(8,128)(2,1)S(1)} %collective-permute-done.refs_0_, bf16[384,256]{1,0:T(8,128)(2,1)S(1)} %collective-permute-done.1.refs_1_, bf16[256,256]{1,0:T(8,128)(2,1)} %collective-permute-done.5.refs_2_, ...), custom_call_target="tpu_custom_call", output_to_operand_aliasing={{}: (4, {})} | custom-call | flops 134217728 | bytes 393216 | tf_op jit(solution)/shard_map/absorb/pallas_call | solution.py:127
  105.3 0.7 absorb.12.refs_3_
  106.0 1.7 %absorb.13 = (bf16[256,128]{1,0:T(8,128)(2,1)S(1)}, bf16[256,128]{1,0:T(8,128)(2,1)S(1)}) custom-call(bf16[384,256]{1,0:T(8,128)(2,1)S(1)} %collective-permute-done.refs_0_, bf16[384,256]{1,0:T(8,128)(2,1)S(1)} %collective-permute-done.1.refs_1_, bf16[256,256]{1,0:T(8,128)(2,1)} %collective-permute-done.4.refs_2_, f32[1,2,144,256]{3,2,1,0:T(8,128)S(1)} %absorb.12.refs_3_), custom_call_target="tpu_custom_call" | custom-call | flops 67108864 | bytes 393216 | tf_op jit(solution)/shard_map/absorb/pallas_call | solution.py:127
  107.7 1.8 %collective-permute-start.10 = (bf16[256,128]{1,0:T(8,128)(2,1)S(1)}, bf16[256,128]{1,0:T(8,128)(2,1)S(1)}, u32[]{:S(2)}, u32[]{:S(2)}) collective-permute-start(bf16[256,128]{1,0:T(8,128)(2,1)S(1)} %get-tuple-element.19), channel_id=1, source_target_pairs={{0,4},{1,5},{2,6},{3,7},{4,0},{5,1},{6,2},{7,3},{8,12},{9,13},{10,... | collective-permute-start | bytes 196616 | tf_op jit(solution)/shard_map/ppermute | solution.py:233
  109.5 1.2 %collective-permute-start.14 = (bf16[256,128]{1,0:T(8,128)(2,1)S(1)}, bf16[256,128]{1,0:T(8,128)(2,1)S(1)}, u32[]{:S(2)}, u32[]{:S(2)}) collective-permute-start(bf16[256,128]{1,0:T(8,128)(2,1)S(1)} %get-tuple-element.19), channel_id=1, source_target_pairs={{0,5},{1,4},{2,7},{3,6},{4,1},{5,0},{6,3},{7,2},{8,13},{9,12},{10,... | collective-permute-start | bytes 196616 | tf_op jit(solution)/shard_map/ppermute | solution.py:233
  111.3 4.5 %project.2.refs_7_ = f32[256,1536]{1,0:T(8,128)S(1)} custom-call(s32[3]{0:T(128)S(1)} %pad_add_fusion.refs_0_, bf16[256,256]{1,0:T(8,128)(2,1)S(1)} %get-tuple-element.23.refs_1_.refs_5_, bf16[768,3072]{1,0:T(8,128)(2,1)} %collective-permute-done.11.refs_2_.refs_4_.refs_6_.refs_8_.refs_10_, bf16[256,256]{1,0:T(8,128)(2,1)S(1)} %collective-permute-done.24.refs_3_.refs_7_, ...), custom_call_target="tpu_custom_call" | custom-call | flops 905969664 | bytes 1572864 | tf_op jit(solution)/shard_map/project/pallas_call | solution.py:178
  115.8 3.9 %project.3 = bf16[256,1536]{1,0:T(8,128)(2,1)} custom-call(s32[3]{0:T(128)S(1)} %pad_add_fusion.refs_0_, bf16[256,128]{1,0:T(8,128)(2,1)S(1)} %collective-permute-done.10.refs_1_, bf16[768,3072]{1,0:T(8,128)(2,1)} %collective-permute-done.11.refs_2_.refs_4_.refs_6_.refs_8_.refs_10_, bf16[256,128]{1,0:T(8,128)(2,1)S(1)} %collective-permute-done.12.refs_3_, ...), custom_call_target="tpu_custom_call" | custom-call | flops 301989888 | bytes 1572864 | tf_op jit(solution)/shard_map/project/pallas_call | solution.py:178
  (62 shorter events, 6.9 us)
Async XLA Ops:
  0.0 111.3 %collective-permute-start.11 = (bf16[768,3072]{1,0:T(8,128)(2,1)}, bf16[768,3072]{1,0:T(8,128)(2,1)}, u32[]{:S(2)}, u32[]{:S(2)}) collective-permute-start(bf16[768,3072]{1,0:T(8,128)(2,1)} %bitcast.18), channel_id=1, source_target_pairs={{0,16},{1,17},{2,18},{3,19},{4,20},{5,21},{6,22},{7,23},{8,24},{9,... | collective-permute-start | bytes 14155784 | tf_op jit(solution)/shard_map/ppermute | solution.py:233
  0.5 1.0 copy-start.1
  1.5 1.0 copy-start.2
  2.7 8.5 %collective-permute-start.2 = (bf16[256,256]{1,0:T(8,128)(2,1)S(1)}, bf16[256,256]{1,0:T(8,128)(2,1)S(1)}, u32[]{:S(2)}, u32[]{:S(2)}) collective-permute-start(bf16[256,256]{1,0:T(8,128)(2,1)S(1)} %get-tuple-element.17), channel_id=1, source_target_pairs={{0,20},{1,21},{2,22},{3,23},{4,16},{5,17},{6,18},{7,19},{8,28},{9,... | collective-permute-start | bytes 393224 | tf_op jit(solution)/shard_map/ppermute | solution.py:233
  5.4 7.2 %collective-permute-start.9 = (bf16[256,256]{1,0:T(8,128)(2,1)S(1)}, bf16[256,256]{1,0:T(8,128)(2,1)S(1)}, u32[]{:S(2)}, u32[]{:S(2)}) collective-permute-start(bf16[256,256]{1,0:T(8,128)(2,1)S(1)} %get-tuple-element.18), channel_id=1, source_target_pairs={{0,16},{1,17},{2,18},{3,19},{4,20},{5,21},{6,22},{7,23},{8,24},{9,... | collective-permute-start | bytes 393224 | tf_op jit(solution)/shard_map/ppermute | solution.py:233
  5.4 3.0 %collective-permute-start.31 = (f32[1,3072]{1,0:T(1,128)}, f32[1,3072]{1,0:T(1,128)S(1)}, u32[]{:S(2)}, u32[]{:S(2)}) collective-permute-start(f32[1,3072]{1,0:T(1,128)} %param.11), channel_id=1, source_target_pairs={{0,16},{1,17},{2,18},{3,19},{4,20},{5,21},{6,22},{7,23},{8,24},{9,... | collective-permute-start | bytes 36872 | tf_op jit(solution)/shard_map/ppermute | solution.py:233
  5.9 1.0 copy-start
  7.1 14.9 %collective-permute-start = (bf16[384,256]{1,0:T(8,128)(2,1)S(1)}, bf16[384,256]{1,0:T(8,128)(2,1)S(1)}, u32[]{:S(2)}, u32[]{:S(2)}) collective-permute-start(bf16[384,256]{1,0:T(8,128)(2,1)S(1)} %get-tuple-element.15), channel_id=1, source_target_pairs={{0,16},{1,17},{2,18},{3,19},{4,20},{5,21},{6,22},{7,23},{8,24},{9,... | collective-permute-start | bytes 589832 | tf_op jit(solution)/shard_map/ppermute | solution.py:233
  8.4 14.9 %collective-permute-start.1 = (bf16[384,256]{1,0:T(8,128)(2,1)S(1)}, bf16[384,256]{1,0:T(8,128)(2,1)S(1)}, u32[]{:S(2)}, u32[]{:S(2)}) collective-permute-start(bf16[384,256]{1,0:T(8,128)(2,1)S(1)} %get-tuple-element.16), channel_id=1, source_target_pairs={{0,20},{1,21},{2,22},{3,23},{4,16},{5,17},{6,18},{7,19},{8,28},{9,... | collective-permute-start | bytes 589832 | tf_op jit(solution)/shard_map/ppermute | solution.py:233
  11.1 5.2 %collective-permute-start.7 = (bf16[256,256]{1,0:T(8,128)(2,1)S(1)}, bf16[256,256]{1,0:T(8,128)(2,1)S(1)}, u32[]{:S(2)}, u32[]{:S(2)}) collective-permute-start(bf16[256,256]{1,0:T(8,128)(2,1)S(1)} %get-tuple-element.18), channel_id=1, source_target_pairs={{0,18},{1,19},{2,16},{3,17},{4,22},{5,23},{6,20},{7,21},{8,26},{9,... | collective-permute-start | bytes 393224 | tf_op jit(solution)/shard_map/ppermute | solution.py:233
  12.6 0.7 copy-start.13
  13.3 8.6 %collective-permute-start.5 = (bf16[256,256]{1,0:T(8,128)(2,1)S(1)}, bf16[256,256]{1,0:T(8,128)(2,1)}, u32[]{:S(2)}, u32[]{:S(2)}) collective-permute-start(bf16[256,256]{1,0:T(8,128)(2,1)S(1)} %get-tuple-element.18), channel_id=1, source_target_pairs={{0,28},{1,29},{2,30},{3,31},{4,24},{5,25},{6,26},{7,27},{8,20},{9,... | collective-permute-start | bytes 393224 | tf_op jit(solution)/shard_map/ppermute | solution.py:233
  16.4 0.7 copy-start.5
  17.0 10.5 %collective-permute-start.18 = (bf16[512,256]{1,0:T(8,128)(2,1)S(1)}, bf16[512,256]{1,0:T(8,128)(2,1)S(1)}, u32[]{:S(2)}, u32[]{:S(2)}) collective-permute-start(bf16[512,256]{1,0:T(8,128)(2,1)S(1)} %get-tuple-element.22), channel_id=1, source_target_pairs={{0,20},{1,21},{2,22},{3,23},{4,16},{5,17},{6,18},{7,19},{8,28},{9,... | collective-permute-start | bytes 786440 | tf_op jit(solution)/shard_map/ppermute | solution.py:233
  21.8 5.9 %collective-permute-start.23 = (bf16[512,256]{1,0:T(8,128)(2,1)S(1)}, bf16[512,256]{1,0:T(8,128)(2,1)S(1)}, u32[]{:S(2)}, u32[]{:S(2)}) collective-permute-start(bf16[512,256]{1,0:T(8,128)(2,1)S(1)} %get-tuple-element.21), channel_id=1, source_target_pairs={{0,16},{1,17},{2,18},{3,19},{4,20},{5,21},{6,22},{7,23},{8,24},{9,... | collective-permute-start | bytes 786440 | tf_op jit(solution)/shard_map/ppermute | solution.py:233
  22.0 8.1 %collective-permute-start.21 = (bf16[512,256]{1,0:T(8,128)(2,1)S(1)}, bf16[512,256]{1,0:T(8,128)(2,1)S(1)}, u32[]{:S(2)}, u32[]{:S(2)}) collective-permute-start(bf16[512,256]{1,0:T(8,128)(2,1)S(1)} %get-tuple-element.21), channel_id=1, source_target_pairs={{0,18},{1,19},{2,16},{3,17},{4,22},{5,23},{6,20},{7,21},{8,26},{9,... | collective-permute-start | bytes 786440 | tf_op jit(solution)/shard_map/ppermute | solution.py:233
  23.3 13.3 %collective-permute-start.16 = (bf16[512,256]{1,0:T(8,128)(2,1)S(1)}, bf16[512,256]{1,0:T(8,128)(2,1)S(1)}, u32[]{:S(2)}, u32[]{:S(2)}) collective-permute-start(bf16[512,256]{1,0:T(8,128)(2,1)S(1)} %get-tuple-element.21), channel_id=1, source_target_pairs={{0,28},{1,29},{2,30},{3,31},{4,24},{5,25},{6,26},{7,27},{8,20},{9,... | collective-permute-start | bytes 786440 | tf_op jit(solution)/shard_map/ppermute | solution.py:233
  27.5 83.2 %collective-permute-start.30 = (bf16[256,3072]{1,0:T(8,128)(2,1)}, bf16[256,3072]{1,0:T(8,128)(2,1)S(1)}, u32[]{:S(2)}, u32[]{:S(2)}) collective-permute-start(bf16[256,3072]{1,0:T(8,128)(2,1)} %bitcast.19), channel_id=1, source_target_pairs={{0,16},{1,17},{2,18},{3,19},{4,20},{5,21},{6,22},{7,23},{8,24},{9,... | collective-permute-start | bytes 4718600 | tf_op jit(solution)/shard_map/ppermute | solution.py:233
  27.7 11.1 %collective-permute-start.8 = (bf16[256,256]{1,0:T(8,128)(2,1)S(1)}, bf16[256,256]{1,0:T(8,128)(2,1)S(1)}, u32[]{:S(2)}, u32[]{:S(2)}) collective-permute-start(bf16[256,256]{1,0:T(8,128)(2,1)S(1)} %collective-permute-done.2.refs_3_), channel_id=1, source_target_pairs={{0,2},{1,3},{2,0},{3,1},{4,6},{5,7},{6,4},{7,5},{8,10},{9,11},{10,... | collective-permute-start | bytes 393224 | tf_op jit(solution)/shard_map/ppermute | solution.py:233
  30.0 10.0 %collective-permute-start.3 = (bf16[256,256]{1,0:T(8,128)(2,1)S(1)}, bf16[256,256]{1,0:T(8,128)(2,1)}, u32[]{:S(2)}, u32[]{:S(2)}) collective-permute-start(bf16[256,256]{1,0:T(8,128)(2,1)S(1)} %collective-permute-done.2.refs_3_), channel_id=1, source_target_pairs={{0,12},{1,13},{2,14},{3,15},{4,8},{5,9},{6,10},{7,11},{8,4},{9,5},... | collective-permute-start | bytes 393224 | tf_op jit(solution)/shard_map/ppermute | solution.py:233
  36.0 0.6 copy-start.11
  36.6 3.4 %copy-start.3 = (bf16[512,256]{1,0:T(8,128)(2,1)}, bf16[512,256]{1,0:T(8,128)(2,1)S(1)}, u32[]{:S(2)}) copy-start(bf16[512,256]{1,0:T(8,128)(2,1)S(1)} %collective-permute-done.16.refs_2_) | copy-start | bytes 786436
  36.6 5.2 %collective-permute-start.6 = (bf16[256,256]{1,0:T(8,128)(2,1)}, bf16[256,256]{1,0:T(8,128)(2,1)S(1)}, u32[]{:S(2)}, u32[]{:S(2)}) collective-permute-start(bf16[256,256]{1,0:T(8,128)(2,1)} %collective-permute-done.5.refs_2_), channel_id=1, source_target_pairs={{0,2},{1,3},{2,0},{3,1},{4,6},{5,7},{6,4},{7,5},{8,10},{9,11},{10,... | collective-permute-start | bytes 393224 | tf_op jit(solution)/shard_map/ppermute | solution.py:233
  38.8 0.6 copy-start.7
  39.4 11.6 %collective-permute-start.26 = (bf16[128,1536]{1,0:T(8,128)(2,1)}, bf16[128,1536]{1,0:T(8,128)(2,1)S(1)}, u32[]{:S(2)}, u32[]{:S(2)}) collective-permute-start(bf16[128,1536]{1,0:T(8,128)(2,1)} %get-tuple-element.25), channel_id=1, source_target_pairs={{0,17},{1,16},{2,19},{3,18},{4,21},{5,20},{6,23},{7,22},{8,25},{9,... | collective-permute-start | bytes 1179656 | tf_op jit(solution)/shard_map/ppermute | solution.py:233
  40.0 19.4 %collective-permute-start.13 = (bf16[128,1536]{1,0:T(8,128)(2,1)}, bf16[128,1536]{1,0:T(8,128)(2,1)S(1)}, u32[]{:S(2)}, u32[]{:S(2)}) collective-permute-start(bf16[128,1536]{1,0:T(8,128)(2,1)} %get-tuple-element.26), channel_id=1, source_target_pairs={{0,17},{1,16},{2,19},{3,18},{4,21},{5,20},{6,23},{7,22},{8,25},{9,... | collective-permute-start | bytes 1179656 | tf_op jit(solution)/shard_map/ppermute | solution.py:233
  41.8 0.7 copy-start.9
  42.5 5.3 %collective-permute-start.4 = (bf16[256,256]{1,0:T(8,128)(2,1)}, bf16[256,256]{1,0:T(8,128)(2,1)}, u32[]{:S(2)}, u32[]{:S(2)}) collective-permute-start(bf16[256,256]{1,0:T(8,128)(2,1)} %collective-permute-done.3.refs_3_), channel_id=1, source_target_pairs={{0,2},{1,3},{2,0},{3,1},{4,6},{5,7},{6,4},{7,5},{8,10},{9,11},{10,... | collective-permute-start | bytes 393224 | tf_op jit(solution)/shard_map/ppermute | solution.py:233
  43.8 30.4 %copy-start.4 = (bf16[512,256]{1,0:T(8,128)(2,1)S(1)}, bf16[512,256]{1,0:T(8,128)(2,1)}, u32[]{:S(2)}) copy-start(bf16[512,256]{1,0:T(8,128)(2,1)} %copy-done.3) | copy-start | bytes 786436
  43.8 57.6 %copy-start.12 = (bf16[256,256]{1,0:T(8,128)(2,1)S(1)}, bf16[256,256]{1,0:T(8,128)(2,1)}, u32[]{:S(2)}) copy-start(bf16[256,256]{1,0:T(8,128)(2,1)} %copy-done.11) | copy-start | bytes 393220
  43.8 57.6 %copy-start.14 = (bf16[256,256]{1,0:T(8,128)(2,1)S(1)}, bf16[256,256]{1,0:T(8,128)(2,1)}, u32[]{:S(2)}) copy-start(bf16[256,256]{1,0:T(8,128)(2,1)} %copy-done.13) | copy-start | bytes 393220
  43.8 58.6 %copy-start.6 = (bf16[256,256]{1,0:T(8,128)(2,1)S(1)}, bf16[256,256]{1,0:T(8,128)(2,1)}, u32[]{:S(2)}) copy-start(bf16[256,256]{1,0:T(8,128)(2,1)} %copy-done.5) | copy-start | bytes 393220
  43.8 58.6 %copy-start.8 = (bf16[256,256]{1,0:T(8,128)(2,1)S(1)}, bf16[256,256]{1,0:T(8,128)(2,1)}, u32[]{:S(2)}) copy-start(bf16[256,256]{1,0:T(8,128)(2,1)} %copy-done.7) | copy-start | bytes 393220
  47.7 12.2 %collective-permute-start.22 = (bf16[512,256]{1,0:T(8,128)(2,1)S(1)}, bf16[512,256]{1,0:T(8,128)(2,1)S(1)}, u32[]{:S(2)}, u32[]{:S(2)}) collective-permute-start(bf16[512,256]{1,0:T(8,128)(2,1)S(1)} %collective-permute-done.18.refs_3_), channel_id=1, source_target_pairs={{0,2},{1,3},{2,0},{3,1},{4,6},{5,7},{6,4},{7,5},{8,10},{9,11},{10,... | collective-permute-start | bytes 786440 | tf_op jit(solution)/shard_map/ppermute | solution.py:233
  51.0 10.4 %collective-permute-start.19 = (bf16[512,256]{1,0:T(8,128)(2,1)S(1)}, bf16[512,256]{1,0:T(8,128)(2,1)S(1)}, u32[]{:S(2)}, u32[]{:S(2)}) collective-permute-start(bf16[512,256]{1,0:T(8,128)(2,1)S(1)} %collective-permute-done.18.refs_3_), channel_id=1, source_target_pairs={{0,12},{1,13},{2,14},{3,15},{4,8},{5,9},{6,10},{7,11},{8,4},{9,5},... | collective-permute-start | bytes 786440 | tf_op jit(solution)/shard_map/ppermute | solution.py:233
  59.4 30.8 %collective-permute-start.29 = (bf16[256,1536]{1,0:T(8,128)(2,1)S(1)}, bf16[256,1536]{1,0:T(8,128)(2,1)S(1)}, u32[]{:S(2)}, u32[]{:S(2)}) collective-permute-start(bf16[256,1536]{1,0:T(8,128)(2,1)S(1)} %dynamic-slice_bitcast_fusion), channel_id=1, source_target_pairs={{0,17},{1,16},{2,19},{3,18},{4,21},{5,20},{6,23},{7,22},{8,25},{9,... | collective-permute-start | bytes 2359304 | tf_op jit(solution)/shard_map/ppermute | solution.py:233
  60.0 9.4 %collective-permute-start.17 = (bf16[512,256]{1,0:T(8,128)(2,1)}, bf16[512,256]{1,0:T(8,128)(2,1)S(1)}, u32[]{:S(2)}, u32[]{:S(2)}) collective-permute-start(bf16[512,256]{1,0:T(8,128)(2,1)} %copy-done.3), channel_id=1, source_target_pairs={{0,2},{1,3},{2,0},{3,1},{4,6},{5,7},{6,4},{7,5},{8,10},{9,11},{10,... | collective-permute-start | bytes 786440 | tf_op jit(solution)/shard_map/ppermute | solution.py:233
  61.3 28.7 %collective-permute-start.27 = (bf16[128,1536]{1,0:T(8,128)(2,1)S(1)}, bf16[128,1536]{1,0:T(8,128)(2,1)S(1)}, u32[]{:S(2)}, u32[]{:S(2)}) collective-permute-start(bf16[128,1536]{1,0:T(8,128)(2,1)S(1)} %collective-permute-done.26.refs_12_), channel_id=1, source_target_pairs={{0,2},{1,3},{2,0},{3,1},{4,6},{5,7},{6,4},{7,5},{8,10},{9,11},{10,... | collective-permute-start | bytes 1179656 | tf_op jit(solution)/shard_map/ppermute | solution.py:233
  69.4 13.9 %collective-permute-start.20 = (bf16[512,256]{1,0:T(8,128)(2,1)S(1)}, bf16[512,256]{1,0:T(8,128)(2,1)S(1)}, u32[]{:S(2)}, u32[]{:S(2)}) collective-permute-start(bf16[512,256]{1,0:T(8,128)(2,1)S(1)} %collective-permute-done.19.refs_3_), channel_id=1, source_target_pairs={{0,2},{1,3},{2,0},{3,1},{4,6},{5,7},{6,4},{7,5},{8,10},{9,11},{10,... | collective-permute-start | bytes 786440 | tf_op jit(solution)/shard_map/ppermute | solution.py:233
  72.4 32.9 %copy-start.10 = (bf16[256,256]{1,0:T(8,128)(2,1)S(1)}, bf16[256,256]{1,0:T(8,128)(2,1)}, u32[]{:S(2)}) copy-start(bf16[256,256]{1,0:T(8,128)(2,1)} %copy-done.9) | copy-start | bytes 393220
  83.2 32.6 %collective-permute-start.15 = (bf16[128,1536]{1,0:T(8,128)(2,1)S(1)}, bf16[128,1536]{1,0:T(8,128)(2,1)S(1)}, u32[]{:S(2)}, u32[]{:S(2)}) collective-permute-start(bf16[128,1536]{1,0:T(8,128)(2,1)S(1)} %collective-permute-done.13.refs_4_), channel_id=1, source_target_pairs={{0,4},{1,5},{2,6},{3,7},{4,0},{5,1},{6,2},{7,3},{8,12},{9,13},{10,... | collective-permute-start | bytes 1179656 | tf_op jit(solution)/shard_map/ppermute | solution.py:233
  90.1 10.7 %collective-permute-start.24 = (bf16[256,256]{1,0:T(8,128)(2,1)S(1)}, bf16[256,256]{1,0:T(8,128)(2,1)S(1)}, u32[]{:S(2)}, u32[]{:S(2)}) collective-permute-start(bf16[256,256]{1,0:T(8,128)(2,1)S(1)} %get-tuple-element.24), channel_id=1, source_target_pairs={{0,4},{1,5},{2,6},{3,7},{4,0},{5,1},{6,2},{7,3},{8,12},{9,13},{10,... | collective-permute-start | bytes 393224 | tf_op jit(solution)/shard_map/ppermute | solution.py:233
  90.2 19.3 %collective-permute-start.28 = (bf16[256,256]{1,0:T(8,128)(2,1)S(1)}, bf16[256,256]{1,0:T(8,128)(2,1)S(1)}, u32[]{:S(2)}, u32[]{:S(2)}) collective-permute-start(bf16[256,256]{1,0:T(8,128)(2,1)S(1)} %get-tuple-element.24), channel_id=1, source_target_pairs={{0,5},{1,4},{2,7},{3,6},{4,1},{5,0},{6,3},{7,2},{8,13},{9,12},{10,... | collective-permute-start | bytes 393224 | tf_op jit(solution)/shard_map/ppermute | solution.py:233
  100.8 6.9 %collective-permute-start.25 = (bf16[256,256]{1,0:T(8,128)(2,1)S(1)}, bf16[256,256]{1,0:T(8,128)(2,1)S(1)}, u32[]{:S(2)}, u32[]{:S(2)}) collective-permute-start(bf16[256,256]{1,0:T(8,128)(2,1)S(1)} %get-tuple-element.23.refs_1_.refs_5_), channel_id=1, source_target_pairs={{0,1},{1,0},{2,3},{3,2},{4,5},{5,4},{6,7},{7,6},{8,9},{9,8},{10,11... | collective-permute-start | bytes 393224 | tf_op jit(solution)/shard_map/ppermute | solution.py:233
  107.7 8.1 %collective-permute-start.10 = (bf16[256,128]{1,0:T(8,128)(2,1)S(1)}, bf16[256,128]{1,0:T(8,128)(2,1)S(1)}, u32[]{:S(2)}, u32[]{:S(2)}) collective-permute-start(bf16[256,128]{1,0:T(8,128)(2,1)S(1)} %get-tuple-element.19), channel_id=1, source_target_pairs={{0,4},{1,5},{2,6},{3,7},{4,0},{5,1},{6,2},{7,3},{8,12},{9,13},{10,... | collective-permute-start | bytes 196616 | tf_op jit(solution)/shard_map/ppermute | solution.py:233
  109.5 6.3 %collective-permute-start.14 = (bf16[256,128]{1,0:T(8,128)(2,1)S(1)}, bf16[256,128]{1,0:T(8,128)(2,1)S(1)}, u32[]{:S(2)}, u32[]{:S(2)}) collective-permute-start(bf16[256,128]{1,0:T(8,128)(2,1)S(1)} %get-tuple-element.19), channel_id=1, source_target_pairs={{0,5},{1,4},{2,7},{3,6},{4,1},{5,0},{6,3},{7,2},{8,13},{9,12},{10,... | collective-permute-start | bytes 196616 | tf_op jit(solution)/shard_map/ppermute | solution.py:233
  110.7 5.0 %collective-permute-start.12 = (bf16[256,128]{1,0:T(8,128)(2,1)S(1)}, bf16[256,128]{1,0:T(8,128)(2,1)S(1)}, u32[]{:S(2)}, u32[]{:S(2)}) collective-permute-start(bf16[256,128]{1,0:T(8,128)(2,1)S(1)} %get-tuple-element.20.refs_9_), channel_id=1, source_target_pairs={{0,1},{1,0},{2,3},{3,2},{4,5},{5,4},{6,7},{7,6},{8,9},{9,8},{10,11... | collective-permute-start | bytes 196616 | tf_op jit(solution)/shard_map/ppermute | solution.py:233

commit v4 on v3

--- a/solution.py
+++ b/solution.py
@@ -19,7 +19,16 @@
     return pltpu.CompilerParams(vmem_limit_bytes=mib << 20)
 
 
-def pack_kernel(groups, role_ref, k_ref, v_ref, *out_refs):
+def pack_kernel(groups, role_ref, k_any, v_any, *rest):
+    out_refs, (k_ref, v_ref, sems) = rest[:-3], rest[-3:]
+    loads = [
+        pltpu.make_async_copy(k_any, k_ref, sems.at[0]),
+        pltpu.make_async_copy(v_any, v_ref, sems.at[1]),
+    ]
+    for load in loads:
+        load.start()
+    for load in loads:
+        load.wait()
     rows, width = k_ref.shape
     half = width // 2
     for side in range(2):
@@ -35,20 +44,31 @@
                 out[base + HD : base + 2 * HD, :] = v_ref[:, lanes].T
 
 
+ANY = pl.BlockSpec(memory_space=pl.ANY)
+HBM = pl.BlockSpec(memory_space=pltpu.HBM)
 SMEM = pl.BlockSpec(memory_space=pltpu.SMEM)
+
+
+def in_hbm(x):
+    return pltpu.with_memory_space_constraint(x, pltpu.HBM)
 
 
 def pack(role, keys, values, groups):
     rows = keys.shape[0]
-    shapes = [jax.ShapeDtypeStruct((len(heads) * 2 * HD, rows), jnp.bfloat16) for heads in groups]
+    shapes = [pltpu.VMEM((len(heads) * 2 * HD, rows), jnp.bfloat16) for heads in groups]
     return pl.pallas_call(
         functools.partial(pack_kernel, groups),
         out_shape=tuple(shapes + shapes),
-        in_specs=[SMEM, VMEM, VMEM],
+        in_specs=[SMEM, HBM, HBM],
         out_specs=(VMEM,) * (2 * len(groups)),
+        scratch_shapes=[
+            pltpu.VMEM(keys.shape, keys.dtype),
+            pltpu.VMEM(values.shape, values.dtype),
+            pltpu.SemaphoreType.DMA((2,)),
+        ],
         compiler_params=limit(8),
         name="pack",
-    )(role, keys, values)
+    )(role, in_hbm(keys), in_hbm(values))
 
 
 def turn_kernel(role_ref, x_ref, mine_ref, give_ref):
@@ -143,14 +163,46 @@
 def project_kernel(pieces, *refs):
     out = refs[-1]
     refs = refs[1:-1]
-    total = None
-    for at in range(pieces):
-        term = jnp.dot(
-            refs[2 * at][...], refs[2 * at + 1][...], preferred_element_type=jnp.float32
-        )
-        total = term if total is None else total + term
+    left = jnp.concatenate([refs[2 * at][...] for at in range(pieces)], axis=1)
+    right = jnp.concatenate([refs[2 * at + 1][...] for at in range(pieces)], axis=0)
     base, gate = refs[-2], refs[-1]
-    out[...] = (base[...].astype(jnp.float32) + gate[...] * total).astype(out.dtype)
+    branch = jnp.dot(left, right, preferred_element_type=jnp.float32)
+    out[...] = (base[...].astype(jnp.float32) + gate[...] * branch).astype(out.dtype)
+
+
+def finish_kernel(pieces, wide, *refs):
+    lefts, rights = refs[:pieces], refs[pieces : 2 * pieces]
+    base, gate, out, held, sems = refs[2 * pieces :]
+    left = jnp.concatenate([ref[...] for ref in lefts], axis=1)
+    copies = []
+    for at in range(base.shape[1] // wide):
+        lanes = slice(at * wide, (at + 1) * wide)
+        right = jnp.concatenate([ref[:, lanes] for ref in rights], axis=0)
+        branch = jnp.dot(left, right, preferred_element_type=jnp.float32)
+        held[:, lanes] = (base[:, lanes] + gate[:, lanes] * branch).astype(held.dtype)
+        copies.append(pltpu.make_async_copy(held.at[:, lanes], out.at[:, lanes], sems.at[at]))
+        copies[-1].start()
+    for copy in copies:
+        copy.wait()
+
+
+def finish(pieces, weights, base, gate, wide):
+    operands = [*pieces, *weights, base, gate]
+    return pl.pallas_call(
+        functools.partial(finish_kernel, len(pieces), wide),
+        out_shape=jax.ShapeDtypeStruct(base.shape, jnp.bfloat16),
+        in_specs=[VMEM] * len(operands),
+        out_specs=ANY,
+        scratch_shapes=[
+            pltpu.VMEM(base.shape, jnp.bfloat16),
+            pltpu.SemaphoreType.DMA((base.shape[1] // wide,)),
+        ],
+        cost_estimate=pl.CostEstimate(
+            flops=2 * len(pieces) * HD * base.size, bytes_accessed=base.size * 2, transcendentals=0
+        ),
+        compiler_params=limit(12),
+        name="finish",
+    )(*operands)
 
 
 def project(where, sources, base, gate, cols, wide, dtype):
@@ -245,17 +297,10 @@
     lent = {}
     for by in range(1, shares):
         start = lax.rem(share + by, shares) * col_count
-
-        def rows_at(head, count):
-            return lax.dynamic_slice(
-                out_weight[0], (head * HD, start), (count * HD, col_count)
-            )
-
-        lent[by] = [
-            hop(rows_at(role * local + 1 - column, 1), still, 1, by),
-            hop(rows_at(role * local + 2, 1), still, 1, by),
-            hop(rows_at((1 - role) * local, 2), still, 1, by),
-        ]
+        lent[by] = []
+        for head, count in ((role * local + 2, 1), (role * local, 2), ((1 - role) * local, 2)):
+            part = lax.dynamic_slice(out_weight[0], (head * HD, start), (count * HD, col_count))
+            lent[by].append(hop(part, still, 1, by))
 
     packed = pack(role_ref, keys[0], values[0], groups)
     mine, give = packed[: len(groups)], packed[len(groups) :]
@@ -275,8 +320,7 @@
     stream = hop(stream_in[0], still, 1)
     gate = hop(gate_scale, still, 1)
     for by in range(1, shares):
-        lent[by].append(hop(lent[by][0], beside))
-        lent[by].append(hop(lent[by][1], partner))
+        lent[by].append(hop(lent[by][0], partner))
 
     def fold(g, blocks, held, last=False):
         return absorb(asking, blocks, groups[g], held, last)
@@ -314,26 +358,27 @@
     def top(s):
         return 0
 
-    def third(role):
-        return role * local + 2
-
     first, second = home
     sources = []
     for head in range(2):
         pick = lambda s, head=head: head
         sources.append((first[0], pick, weight, lambda s, h=head: s[1] * local + h, True))
         sources.append((first[1], pick, weight, lambda s, h=head: (1 - s[1]) * local + h, True))
-    sources.append((second[0], None, weight, lambda s: third(s[1]), True))
-    final = [(second[1], None, weight, lambda s: third(1 - s[1]), True)]
+    sources.append((second[0], None, weight, lambda s: s[1] * local + 2, True))
+    own_start = share * col_count
+    last_pieces = [second[1]]
+    last_weights = [
+        lax.dynamic_slice(weight, (((1 - role) * local + 2) * HD, own_start), (HD, col_count))
+    ]
     for by in range(1, shares):
-        fetched, thirds, pairs, relayed, others = lent[by]
-        sources.append((first[2][by], lambda s: 1 - s[2], fetched, top, False))
-        sources.append((first[2][by], lambda s: s[2], relayed, top, False))
-        sources.append((first[3][by], None, pairs, top, False))
-        final.append((second[2][by], None, thirds, top, False))
-        final.append((second[3][by], None, others, top, False))
+        thirds, pairs, others, relayed = lent[by]
+        sources.append((first[2][by], None, pairs, top, False))
+        sources.append((first[3][by], None, others, top, False))
+        last_pieces += [second[2][by], second[3][by]]
+        last_weights += [thirds, relayed]
     base = project(where, sources, stream, gate, col_count, 512, jnp.float32)
-    return project(where, final, base, gate, col_count, 512, jnp.bfloat16)[None]
+    own_gate = lax.dynamic_slice(gate, (0, own_start), (1, col_count))
+    return finish(last_pieces, last_weights, base, own_gate, 384)[None]
 
 
 def solution(mesh):

time: 120 us -> 112 us (0.933)
  waiting for transfers between devices: 43.7 us -> 28.8 us
  local copies, waits for them, and re-layouts: 9.53 us -> 16.6 us
    ppermute x32 -> x31, waiting for transfers between devices: 43.7 us -> 28.8 us  [hop(): return lax.ppermute(block, ('segment', 'seq', 'head'), pairs)]
    unnamed x30 -> x58, local copies, waits for them, and re-layouts: 6.26 us -> 11.1 us
    pallas_call x2 -> x1, Pallas kernels: 8.41 us -> 4.12 us  [project(): pl.pallas_call(functools.partial(project_kernel, len(sources)), out_shape...]
    dynamic_slice x2 -> x4, local copies, waits for them, and re-layouts: 3.28 us -> 5.44 us  [the longest x2 4.41 us: per_device(): lax.dynamic_slice(out_weight[0], (head * HD, start), (count * HD, col_cou...]
    pallas_call x0 -> x1, Pallas kernels: none -> 1.37 us  [finish(): pl.pallas_call(functools.partial(finish_kernel, len(pieces), wide), out_s...]
    ppermute x32 -> x31, starting transfers between devices: 44.1 us -> 44.2 us  [hop(): return lax.ppermute(block, ('segment', 'seq', 'head'), pairs)]
  transfers between devices with their start and end apart: 32 -> 31, of which waited for: 12 -> 10; matrix products, arithmetic and copies ran while one was open for 3% -> 5% of each run, Pallas kernels for 15% -> 18%
where the time goes in v4:
time: 112 us; the launch traced here: 111 us
  starting transfers between devices  44.2 us (39%)
  waiting for transfers between devices  28.8 us (26%)
  Pallas kernels  21.4 us (19%)
  local copies, waits for them, and re-layouts  16.6 us (15%)
    ppermute x31, starting transfers between devices, hop(): return lax.ppermute(block, ('segment', 'seq', 'head'), pairs)  44.2 us
    ppermute x31, waiting for transfers between devices, hop(): return lax.ppermute(block, ('segment', 'seq', 'head'), pairs)  28.8 us
    pallas_call x9, Pallas kernels, absorb(): pl.pallas_call(functools.partial(absorb_kernel, heads, len(blocks), first...  14.4 us
    unnamed x58, local copies, waits for them, and re-layouts  11.1 us
    dynamic_slice x2, local copies, waits for them, and re-layouts, per_device(): lax.dynamic_slice(out_weight[0], (head * HD, start), (count * HD, col_cou...  4.41 us
    pallas_call x1, Pallas kernels, project(): pl.pallas_call(functools.partial(project_kernel, len(sources)), out_shape...  4.12 us
  transfers between devices with their start and end apart: 31, of which 10 were waited for; matrix products, arithmetic and copies ran while one was open for 5% of the time, Pallas kernels for 18%

profile of v4, /device:TPU:0, one launch (start us, length us, event | category | flops | bytes accessed | tf_op | source)
XLA Modules:
  0.0 111.3 jit_solution(9631629438006501096)
XLA Ops:
  0.5 1.3 %pack.1 = (bf16[512,256]{1,0:T(8,128)(2,1)S(1)}, bf16[256,256]{1,0:T(8,128)(2,1)S(1)}, bf16[512,256]{1,0:T(8,128)(2,1)S(1)}, bf16[256,256]{1,0:T(8,128)(2,1)S(1)}) custom-call(s32[1]{0:T(128)} %bitcast.role_ref, bf16[256,768]{1,0:T(8,128)(2,1)} %bitcast.17, bf16[256,768]{1,0:T(8,128)(2,1)} %bitcast.18), custom_call_target="tpu_custom_call" | custom-call | tf_op jit(solution)/shard_map/pack/pallas_call | solution.py:59
  1.8 2.7 %collective-permute-start.2 = (bf16[256,256]{1,0:T(8,128)(2,1)S(1)}, bf16[256,256]{1,0:T(8,128)(2,1)S(1)}, u32[]{:S(2)}, u32[]{:S(2)}) collective-permute-start(bf16[256,256]{1,0:T(8,128)(2,1)S(1)} %get-tuple-element.17), channel_id=1, source_target_pairs={{0,20},{1,21},{2,22},{3,23},{4,16},{5,17},{6,18},{7,19},{8,28},{9,... | collective-permute-start | bytes 393224 | tf_op jit(solution)/shard_map/ppermute | solution.py:285
  4.5 1.6 %collective-permute-start.7 = (bf16[256,256]{1,0:T(8,128)(2,1)S(1)}, bf16[256,256]{1,0:T(8,128)(2,1)S(1)}, u32[]{:S(2)}, u32[]{:S(2)}) collective-permute-start(bf16[256,256]{1,0:T(8,128)(2,1)S(1)} %get-tuple-element.18), channel_id=1, source_target_pairs={{0,18},{1,19},{2,16},{3,17},{4,22},{5,23},{6,20},{7,21},{8,26},{9,... | collective-permute-start | bytes 393224 | tf_op jit(solution)/shard_map/ppermute | solution.py:285
  6.2 1.0 copy-done
  7.3 1.1 %collective-permute-done.30.refs_16_ = f32[1,3072]{1,0:T(1,128)S(1)} collective-permute-done((f32[1,3072]{1,0:T(1,128)}, f32[1,3072]{1,0:T(1,128)S(1)}, u32[]{:S(2)}, u32[]{:S(2)}) %collective-permute-start.30) | collective-permute-done | bytes 12320 | tf_op jit(solution)/shard_map/ppermute | solution.py:285
  8.8 2.7 %collective-permute-start.1 = (bf16[384,256]{1,0:T(8,128)(2,1)S(1)}, bf16[384,256]{1,0:T(8,128)(2,1)S(1)}, u32[]{:S(2)}, u32[]{:S(2)}) collective-permute-start(bf16[384,256]{1,0:T(8,128)(2,1)S(1)} %get-tuple-element.16), channel_id=1, source_target_pairs={{0,20},{1,21},{2,22},{3,23},{4,16},{5,17},{6,18},{7,19},{8,28},{9,... | collective-permute-start | bytes 589832 | tf_op jit(solution)/shard_map/ppermute | solution.py:285
  12.2 2.2 %collective-permute-start.5 = (bf16[256,256]{1,0:T(8,128)(2,1)S(1)}, bf16[256,256]{1,0:T(8,128)(2,1)S(1)}, u32[]{:S(2)}, u32[]{:S(2)}) collective-permute-start(bf16[256,256]{1,0:T(8,128)(2,1)S(1)} %get-tuple-element.18), channel_id=1, source_target_pairs={{0,28},{1,29},{2,30},{3,31},{4,24},{5,25},{6,26},{7,27},{8,20},{9,... | collective-permute-start | bytes 393224 | tf_op jit(solution)/shard_map/ppermute | solution.py:285
  15.7 5.8 %collective-permute-done.5.refs_2_ = bf16[256,256]{1,0:T(8,128)(2,1)S(1)} collective-permute-done((bf16[256,256]{1,0:T(8,128)(2,1)S(1)}, bf16[256,256]{1,0:T(8,128)(2,1)S(1)}, u32[]{:S(2)}, u32[]{:S(2)}) %collective-permute-start.5) | collective-permute-done | bytes 131104 | tf_op jit(solution)/shard_map/ppermute | solution.py:285
  21.5 0.8 collective-permute-start.23
  22.4 1.1 collective-permute-start.21
  23.5 1.5 %collective-permute-start.16 = (bf16[512,256]{1,0:T(8,128)(2,1)S(1)}, bf16[512,256]{1,0:T(8,128)(2,1)S(1)}, u32[]{:S(2)}, u32[]{:S(2)}) collective-permute-start(bf16[512,256]{1,0:T(8,128)(2,1)S(1)} %get-tuple-element.21), channel_id=1, source_target_pairs={{0,28},{1,29},{2,30},{3,31},{4,24},{5,25},{6,26},{7,27},{8,20},{9,... | collective-permute-start | bytes 786440 | tf_op jit(solution)/shard_map/ppermute | solution.py:285
  25.0 1.0 collective-permute-done.18.refs_3_
  26.0 2.7 %collective-permute-start.3 = (bf16[256,256]{1,0:T(8,128)(2,1)S(1)}, bf16[256,256]{1,0:T(8,128)(2,1)S(1)}, u32[]{:S(2)}, u32[]{:S(2)}) collective-permute-start(bf16[256,256]{1,0:T(8,128)(2,1)S(1)} %collective-permute-done.2.refs_3_), channel_id=1, source_target_pairs={{0,12},{1,13},{2,14},{3,15},{4,8},{5,9},{6,10},{7,11},{8,4},{9,5},... | collective-permute-start | bytes 393224 | tf_op jit(solution)/shard_map/ppermute | solution.py:285
  29.7 1.1 collective-permute-done.21.refs_2_
  30.8 7.3 %collective-permute-start.8 = (bf16[256,256]{1,0:T(8,128)(2,1)S(1)}, bf16[256,256]{1,0:T(8,128)(2,1)S(1)}, u32[]{:S(2)}, u32[]{:S(2)}) collective-permute-start(bf16[256,256]{1,0:T(8,128)(2,1)S(1)} %collective-permute-done.2.refs_3_), channel_id=1, source_target_pairs={{0,2},{1,3},{2,0},{3,1},{4,6},{5,7},{6,4},{7,5},{8,10},{9,11},{10,... | collective-permute-start | bytes 393224 | tf_op jit(solution)/shard_map/ppermute | solution.py:285
  38.8 0.7 copy-done.15
  39.5 1.9 %collective-permute-start.4 = (bf16[256,256]{1,0:T(8,128)(2,1)S(1)}, bf16[256,256]{1,0:T(8,128)(2,1)S(1)}, u32[]{:S(2)}, u32[]{:S(2)}) collective-permute-start(bf16[256,256]{1,0:T(8,128)(2,1)S(1)} %collective-permute-done.3.refs_3_), channel_id=1, source_target_pairs={{0,2},{1,3},{2,0},{3,1},{4,6},{5,7},{6,4},{7,5},{8,10},{9,11},{10,... | collective-permute-start | bytes 393224 | tf_op jit(solution)/shard_map/ppermute | solution.py:285
  41.5 1.8 %dynamic-slice_bitcast_fusion.2 = bf16[128,1536]{1,0:T(8,128)(2,1)} fusion(bf16[1,768,3072]{2,1,0:T(8,128)(2,1)} %param.10, s32[]{:T(128)S(6)} %select_n.46, s32[]{:T(128)S(6)} %select_n.47), kind=kLoop, calls=%fused_computation.2 | loop fusion | bytes 786440 | tf_op jit(solution)/shard_map/dynamic_slice | solution.py:302
  44.3 1.0 collective-permute-done.6.refs_2_
  45.3 2.0 %collective-permute-start.22 = (bf16[512,256]{1,0:T(8,128)(2,1)}, bf16[512,256]{1,0:T(8,128)(2,1)S(1)}, u32[]{:S(2)}, u32[]{:S(2)}) collective-permute-start(bf16[512,256]{1,0:T(8,128)(2,1)} %collective-permute-done.18.refs_3_), channel_id=1, source_target_pairs={{0,2},{1,3},{2,0},{3,1},{4,6},{5,7},{6,4},{7,5},{8,10},{9,11},{10,... | collective-permute-start | bytes 786440 | tf_op jit(solution)/shard_map/ppermute | solution.py:285
  47.7 2.6 %dynamic-slice_bitcast_fusion = (bf16[256,1536]{1,0:T(8,128)(2,1)}, bf16[256,1536]{1,0:T(8,128)(2,1)}) fusion(bf16[1,768,3072]{2,1,0:T(8,128)(2,1)} %param.10, s32[]{:T(128)S(6)} %select_n.50, s32[]{:T(128)S(6)} %select_n.47, s32[]{:T(128)S(6)} %select_n.49), kind=kLoop, calls=%fused_computation | loop fusion | bytes 3145740 | tf_op jit(solution)/shard_map/dynamic_slice | solution.py:302
  50.4 5.1 %collective-permute-done.14.refs_4_ = bf16[128,1536]{1,0:T(8,128)(2,1)S(1)} collective-permute-done((bf16[128,1536]{1,0:T(8,128)(2,1)}, bf16[128,1536]{1,0:T(8,128)(2,1)S(1)}, u32[]{:S(2)}, u32[]{:S(2)}) %collective-permute-start.14) | collective-permute-done | bytes 393248 | tf_op jit(solution)/shard_map/ppermute | solution.py:285
  55.5 0.8 copy-done.1
  57.2 1.5 %collective-permute-start.28 = (bf16[256,1536]{1,0:T(8,128)(2,1)}, bf16[256,1536]{1,0:T(8,128)(2,1)S(1)}, u32[]{:S(2)}, u32[]{:S(2)}) collective-permute-start(bf16[256,1536]{1,0:T(8,128)(2,1)} %get-tuple-element.25), channel_id=1, source_target_pairs={{0,17},{1,16},{2,19},{3,18},{4,21},{5,20},{6,23},{7,22},{8,25},{9,... | collective-permute-start | bytes 2359304 | tf_op jit(solution)/shard_map/ppermute | solution.py:285
  58.7 1.2 %collective-permute-start.17 = (bf16[512,256]{1,0:T(8,128)(2,1)}, bf16[512,256]{1,0:T(8,128)(2,1)S(1)}, u32[]{:S(2)}, u32[]{:S(2)}) collective-permute-start(bf16[512,256]{1,0:T(8,128)(2,1)} %copy-done.7), channel_id=1, source_target_pairs={{0,2},{1,3},{2,0},{3,1},{4,6},{5,7},{6,4},{7,5},{8,10},{9,11},{10,... | collective-permute-start | bytes 786440 | tf_op jit(solution)/shard_map/ppermute | solution.py:285
  59.9 7.5 %collective-permute-done.17.refs_2_ = bf16[512,256]{1,0:T(8,128)(2,1)S(1)} collective-permute-done((bf16[512,256]{1,0:T(8,128)(2,1)}, bf16[512,256]{1,0:T(8,128)(2,1)S(1)}, u32[]{:S(2)}, u32[]{:S(2)}) %collective-permute-start.17) | collective-permute-done | bytes 262176 | tf_op jit(solution)/shard_map/ppermute | solution.py:285
  67.4 0.8 copy-done.5
  68.2 1.2 %collective-permute-start.20 = (bf16[512,256]{1,0:T(8,128)(2,1)}, bf16[512,256]{1,0:T(8,128)(2,1)}, u32[]{:S(2)}, u32[]{:S(2)}) collective-permute-start(bf16[512,256]{1,0:T(8,128)(2,1)} %collective-permute-done.19.refs_3_), channel_id=1, source_target_pairs={{0,2},{1,3},{2,0},{3,1},{4,6},{5,7},{6,4},{7,5},{8,10},{9,11},{10,... | collective-permute-start | bytes 786440 | tf_op jit(solution)/shard_map/ppermute | solution.py:285
  69.5 0.9 copy-done.4
  70.5 2.7 %absorb.14.refs_4_ = f32[2,2,144,256]{3,2,1,0:T(8,128)S(1)} custom-call(bf16[384,256]{1,0:T(8,128)(2,1)S(1)} %collective-permute-done.refs_0_, bf16[384,256]{1,0:T(8,128)(2,1)S(1)} %collective-permute-done.1.refs_1_, bf16[512,256]{1,0:T(8,128)(2,1)S(1)} %copy-done.4, bf16[512,256]{1,0:T(8,128)(2,1)} %collective-permute-done.18.refs_3_), custom_call_target="tpu_custom_call" | custom-call | flops 268435456 | bytes 786432 | tf_op jit(solution)/shard_map/absorb/pallas_call | solution.py:147
  73.2 0.9 copy-done.10
  74.2 0.9 copy-done.12
  75.1 1.8 %absorb.15.refs_4_ = f32[2,2,144,256]{3,2,1,0:T(8,128)S(1)} custom-call(bf16[384,256]{1,0:T(8,128)(2,1)S(1)} %collective-permute-done.refs_0_, bf16[384,256]{1,0:T(8,128)(2,1)S(1)} %collective-permute-done.1.refs_1_, bf16[512,256]{1,0:T(8,128)(2,1)S(1)} %copy-done.10, bf16[512,256]{1,0:T(8,128)(2,1)S(1)} %copy-done.12, ...), custom_call_target="tpu_custom_call", output_to_operand_aliasing={{}: (4, {})} | custom-call | flops 268435456 | bytes 786432 | tf_op jit(solution)/shard_map/absorb/pallas_call | solution.py:147
  76.9 3.7 %collective-permute-start.15 = (bf16[128,1536]{1,0:T(8,128)(2,1)}, bf16[128,1536]{1,0:T(8,128)(2,1)S(1)}, u32[]{:S(2)}, u32[]{:S(2)}) collective-permute-start(bf16[128,1536]{1,0:T(8,128)(2,1)} %copy-done.1), channel_id=1, source_target_pairs={{0,4},{1,5},{2,6},{3,7},{4,0},{5,1},{6,2},{7,3},{8,12},{9,13},{10,... | collective-permute-start | bytes 1179656 | tf_op jit(solution)/shard_map/ppermute | solution.py:285
  80.6 0.9 copy-done.8
  81.5 2.7 %absorb.16.refs_4_ = f32[2,2,144,256]{3,2,1,0:T(8,128)S(1)} custom-call(bf16[384,256]{1,0:T(8,128)(2,1)S(1)} %collective-permute-done.refs_0_, bf16[384,256]{1,0:T(8,128)(2,1)S(1)} %collective-permute-done.1.refs_1_, bf16[512,256]{1,0:T(8,128)(2,1)S(1)} %copy-done.8, ...), custom_call_target="tpu_custom_call", output_to_operand_aliasing={{}: (4, {})} | custom-call | flops 268435456 | bytes 786432 | tf_op jit(solution)/shard_map/absorb/pallas_call | solution.py:147
  84.3 2.8 %absorb.17 = (bf16[256,256]{1,0:T(8,128)(2,1)S(1)}, bf16[256,256]{1,0:T(8,128)(2,1)S(1)}) custom-call(bf16[384,256]{1,0:T(8,128)(2,1)S(1)} %collective-permute-done.refs_0_, bf16[384,256]{1,0:T(8,128)(2,1)S(1)} %collective-permute-done.1.refs_1_, bf16[512,256]{1,0:T(8,128)(2,1)S(1)} %copy-done.6, bf16[512,256]{1,0:T(8,128)(2,1)} %collective-permute-done.20.refs_3_, ...), custom_call_target="tpu_custom_call" | custom-call | flops 268435456 | bytes 786432 | tf_op jit(solution)/shard_map/absorb/pallas_call | solution.py:147
  87.2 5.5 %collective-permute-done.28.refs_14_ = bf16[256,1536]{1,0:T(8,128)(2,1)S(1)} collective-permute-done((bf16[256,1536]{1,0:T(8,128)(2,1)}, bf16[256,1536]{1,0:T(8,128)(2,1)S(1)}, u32[]{:S(2)}, u32[]{:S(2)}) %collective-permute-start.28) | collective-permute-done | bytes 786464 | tf_op jit(solution)/shard_map/ppermute | solution.py:285
  92.7 3.8 %collective-permute-start.27 = (bf16[256,256]{1,0:T(8,128)(2,1)S(1)}, bf16[256,256]{1,0:T(8,128)(2,1)S(1)}, u32[]{:S(2)}, u32[]{:S(2)}) collective-permute-start(bf16[256,256]{1,0:T(8,128)(2,1)S(1)} %get-tuple-element.24), channel_id=1, source_target_pairs={{0,5},{1,4},{2,7},{3,6},{4,1},{5,0},{6,3},{7,2},{8,13},{9,12},{10,... | collective-permute-start | bytes 393224 | tf_op jit(solution)/shard_map/ppermute | solution.py:285
  96.7 0.9 absorb.9.refs_4_
  97.6 1.0 absorb.10.refs_4_
  98.6 1.0 absorb.11.refs_3_
  99.6 0.7 absorb.12.refs_3_
  100.3 0.8 absorb.13
  101.1 1.0 dynamic_slice.21.refs_3_
  103.0 2.5 %collective-permute-start.12 = (bf16[256,128]{1,0:T(8,128)(2,1)S(1)}, bf16[256,128]{1,0:T(8,128)(2,1)S(1)}, u32[]{:S(2)}, u32[]{:S(2)}) collective-permute-start(bf16[256,128]{1,0:T(8,128)(2,1)S(1)} %get-tuple-element.19), channel_id=1, source_target_pairs={{0,5},{1,4},{2,7},{3,6},{4,1},{5,0},{6,3},{7,2},{8,13},{9,12},{10,... | collective-permute-start | bytes 196616 | tf_op jit(solution)/shard_map/ppermute | solution.py:285
  105.7 4.1 %project.1.refs_6_ = f32[256,1536]{1,0:T(8,128)S(1)} custom-call(s32[3]{0:T(128)S(1)} %pad_add_fusion.refs_0_, bf16[256,256]{1,0:T(8,128)(2,1)S(1)} %get-tuple-element.23.refs_1_.refs_5_, bf16[768,3072]{1,0:T(8,128)(2,1)} %collective-permute-done.13.refs_2_.refs_4_.refs_6_.refs_8_.refs_10_, bf16[256,256]{1,0:T(8,128)(2,1)S(1)} %collective-permute-done.24.refs_3_.refs_7_, ...), custom_call_target="tpu_custom_call" | custom-call | flops 905969664 | bytes 1572864 | tf_op jit(solution)/shard_map/project/pallas_call | solution.py:230
  109.9 1.4 %finish.1 = bf16[256,1536]{1,0:T(8,128)(2,1)} custom-call(bf16[256,128]{1,0:T(8,128)(2,1)S(1)} %collective-permute-done.10.refs_0_, bf16[256,128]{1,0:T(8,128)(2,1)S(1)} %collective-permute-done.11.refs_1_, bf16[256,128]{1,0:T(8,128)(2,1)S(1)} %collective-permute-done.12.refs_2_, bf16[128,1536]{1,0:T(8,128)(2,1)S(1)} %dynamic_slice.21.refs_3_, ...), custom_call_target="tpu_custom_call" | custom-call | flops 301989888 | bytes 786432 | tf_op jit(solution)/shard_map/finish/pallas_call | solution.py:191
  (90 shorter events, 8.7 us)
Async XLA Ops:
  0.0 96.4 %collective-permute-start.13 = (bf16[768,3072]{1,0:T(8,128)(2,1)}, bf16[768,3072]{1,0:T(8,128)(2,1)}, u32[]{:S(2)}, u32[]{:S(2)}) collective-permute-start(bf16[768,3072]{1,0:T(8,128)(2,1)} %bitcast.16), channel_id=1, source_target_pairs={{0,16},{1,17},{2,18},{3,19},{4,20},{5,21},{6,22},{7,23},{8,24},{9,... | collective-permute-start | bytes 14155784 | tf_op jit(solution)/shard_map/ppermute | solution.py:285
  1.8 7.0 %collective-permute-start.2 = (bf16[256,256]{1,0:T(8,128)(2,1)S(1)}, bf16[256,256]{1,0:T(8,128)(2,1)S(1)}, u32[]{:S(2)}, u32[]{:S(2)}) collective-permute-start(bf16[256,256]{1,0:T(8,128)(2,1)S(1)} %get-tuple-element.17), channel_id=1, source_target_pairs={{0,20},{1,21},{2,22},{3,23},{4,16},{5,17},{6,18},{7,19},{8,28},{9,... | collective-permute-start | bytes 393224 | tf_op jit(solution)/shard_map/ppermute | solution.py:285
  4.5 7.0 %collective-permute-start.9 = (bf16[256,256]{1,0:T(8,128)(2,1)S(1)}, bf16[256,256]{1,0:T(8,128)(2,1)S(1)}, u32[]{:S(2)}, u32[]{:S(2)}) collective-permute-start(bf16[256,256]{1,0:T(8,128)(2,1)S(1)} %get-tuple-element.18), channel_id=1, source_target_pairs={{0,16},{1,17},{2,18},{3,19},{4,20},{5,21},{6,22},{7,23},{8,24},{9,... | collective-permute-start | bytes 393224 | tf_op jit(solution)/shard_map/ppermute | solution.py:285
  4.5 9.8 %collective-permute-start.7 = (bf16[256,256]{1,0:T(8,128)(2,1)S(1)}, bf16[256,256]{1,0:T(8,128)(2,1)S(1)}, u32[]{:S(2)}, u32[]{:S(2)}) collective-permute-start(bf16[256,256]{1,0:T(8,128)(2,1)S(1)} %get-tuple-element.18), channel_id=1, source_target_pairs={{0,18},{1,19},{2,16},{3,17},{4,22},{5,23},{6,20},{7,21},{8,26},{9,... | collective-permute-start | bytes 393224 | tf_op jit(solution)/shard_map/ppermute | solution.py:285
  6.1 2.3 %collective-permute-start.30 = (f32[1,3072]{1,0:T(1,128)}, f32[1,3072]{1,0:T(1,128)S(1)}, u32[]{:S(2)}, u32[]{:S(2)}) collective-permute-start(f32[1,3072]{1,0:T(1,128)} %param.11), channel_id=1, source_target_pairs={{0,16},{1,17},{2,18},{3,19},{4,20},{5,21},{6,22},{7,23},{8,24},{9,... | collective-permute-start | bytes 36872 | tf_op jit(solution)/shard_map/ppermute | solution.py:285
  6.1 1.0 copy-start
  8.4 13.9 %collective-permute-start = (bf16[384,256]{1,0:T(8,128)(2,1)S(1)}, bf16[384,256]{1,0:T(8,128)(2,1)S(1)}, u32[]{:S(2)}, u32[]{:S(2)}) collective-permute-start(bf16[384,256]{1,0:T(8,128)(2,1)S(1)} %get-tuple-element.15), channel_id=1, source_target_pairs={{0,16},{1,17},{2,18},{3,19},{4,20},{5,21},{6,22},{7,23},{8,24},{9,... | collective-permute-start | bytes 589832 | tf_op jit(solution)/shard_map/ppermute | solution.py:285
  8.8 14.6 %collective-permute-start.1 = (bf16[384,256]{1,0:T(8,128)(2,1)S(1)}, bf16[384,256]{1,0:T(8,128)(2,1)S(1)}, u32[]{:S(2)}, u32[]{:S(2)}) collective-permute-start(bf16[384,256]{1,0:T(8,128)(2,1)S(1)} %get-tuple-element.16), channel_id=1, source_target_pairs={{0,20},{1,21},{2,22},{3,23},{4,16},{5,17},{6,18},{7,19},{8,28},{9,... | collective-permute-start | bytes 589832 | tf_op jit(solution)/shard_map/ppermute | solution.py:285
  12.2 9.4 %collective-permute-start.5 = (bf16[256,256]{1,0:T(8,128)(2,1)S(1)}, bf16[256,256]{1,0:T(8,128)(2,1)S(1)}, u32[]{:S(2)}, u32[]{:S(2)}) collective-permute-start(bf16[256,256]{1,0:T(8,128)(2,1)S(1)} %get-tuple-element.18), channel_id=1, source_target_pairs={{0,28},{1,29},{2,30},{3,31},{4,24},{5,25},{6,26},{7,27},{8,20},{9,... | collective-permute-start | bytes 393224 | tf_op jit(solution)/shard_map/ppermute | solution.py:285
  15.0 11.0 %collective-permute-start.18 = (bf16[512,256]{1,0:T(8,128)(2,1)S(1)}, bf16[512,256]{1,0:T(8,128)(2,1)}, u32[]{:S(2)}, u32[]{:S(2)}) collective-permute-start(bf16[512,256]{1,0:T(8,128)(2,1)S(1)} %get-tuple-element.22), channel_id=1, source_target_pairs={{0,20},{1,21},{2,22},{3,23},{4,16},{5,17},{6,18},{7,19},{8,28},{9,... | collective-permute-start | bytes 786440 | tf_op jit(solution)/shard_map/ppermute | solution.py:285
  21.5 7.2 %collective-permute-start.23 = (bf16[512,256]{1,0:T(8,128)(2,1)S(1)}, bf16[512,256]{1,0:T(8,128)(2,1)S(1)}, u32[]{:S(2)}, u32[]{:S(2)}) collective-permute-start(bf16[512,256]{1,0:T(8,128)(2,1)S(1)} %get-tuple-element.21), channel_id=1, source_target_pairs={{0,16},{1,17},{2,18},{3,19},{4,20},{5,21},{6,22},{7,23},{8,24},{9,... | collective-permute-start | bytes 786440 | tf_op jit(solution)/shard_map/ppermute | solution.py:285
  22.4 8.4 %collective-permute-start.21 = (bf16[512,256]{1,0:T(8,128)(2,1)S(1)}, bf16[512,256]{1,0:T(8,128)(2,1)S(1)}, u32[]{:S(2)}, u32[]{:S(2)}) collective-permute-start(bf16[512,256]{1,0:T(8,128)(2,1)S(1)} %get-tuple-element.21), channel_id=1, source_target_pairs={{0,18},{1,19},{2,16},{3,17},{4,22},{5,23},{6,20},{7,21},{8,26},{9,... | collective-permute-start | bytes 786440 | tf_op jit(solution)/shard_map/ppermute | solution.py:285
  23.5 15.3 %collective-permute-start.16 = (bf16[512,256]{1,0:T(8,128)(2,1)S(1)}, bf16[512,256]{1,0:T(8,128)(2,1)S(1)}, u32[]{:S(2)}, u32[]{:S(2)}) collective-permute-start(bf16[512,256]{1,0:T(8,128)(2,1)S(1)} %get-tuple-element.21), channel_id=1, source_target_pairs={{0,28},{1,29},{2,30},{3,31},{4,24},{5,25},{6,26},{7,27},{8,20},{9,... | collective-permute-start | bytes 786440 | tf_op jit(solution)/shard_map/ppermute | solution.py:285
  26.0 13.5 %collective-permute-start.3 = (bf16[256,256]{1,0:T(8,128)(2,1)S(1)}, bf16[256,256]{1,0:T(8,128)(2,1)S(1)}, u32[]{:S(2)}, u32[]{:S(2)}) collective-permute-start(bf16[256,256]{1,0:T(8,128)(2,1)S(1)} %collective-permute-done.2.refs_3_), channel_id=1, source_target_pairs={{0,12},{1,13},{2,14},{3,15},{4,8},{5,9},{6,10},{7,11},{8,4},{9,5},... | collective-permute-start | bytes 393224 | tf_op jit(solution)/shard_map/ppermute | solution.py:285
  29.4 76.3 %collective-permute-start.29 = (bf16[256,3072]{1,0:T(8,128)(2,1)}, bf16[256,3072]{1,0:T(8,128)(2,1)S(1)}, u32[]{:S(2)}, u32[]{:S(2)}) collective-permute-start(bf16[256,3072]{1,0:T(8,128)(2,1)} %bitcast.19), channel_id=1, source_target_pairs={{0,16},{1,17},{2,18},{3,19},{4,20},{5,21},{6,22},{7,23},{8,24},{9,... | collective-permute-start | bytes 4718600 | tf_op jit(solution)/shard_map/ppermute | solution.py:285
  30.8 12.5 %copy-start.9 = (bf16[512,256]{1,0:T(8,128)(2,1)}, bf16[512,256]{1,0:T(8,128)(2,1)S(1)}, u32[]{:S(2)}) copy-start(bf16[512,256]{1,0:T(8,128)(2,1)S(1)} %collective-permute-done.21.refs_2_) | copy-start | bytes 786436
  30.8 12.5 %collective-permute-start.8 = (bf16[256,256]{1,0:T(8,128)(2,1)S(1)}, bf16[256,256]{1,0:T(8,128)(2,1)S(1)}, u32[]{:S(2)}, u32[]{:S(2)}) collective-permute-start(bf16[256,256]{1,0:T(8,128)(2,1)S(1)} %collective-permute-done.2.refs_3_), channel_id=1, source_target_pairs={{0,2},{1,3},{2,0},{3,1},{4,6},{5,7},{6,4},{7,5},{8,10},{9,11},{10,... | collective-permute-start | bytes 393224 | tf_op jit(solution)/shard_map/ppermute | solution.py:285
  38.8 4.5 %copy-start.7 = (bf16[512,256]{1,0:T(8,128)(2,1)}, bf16[512,256]{1,0:T(8,128)(2,1)S(1)}, u32[]{:S(2)}) copy-start(bf16[512,256]{1,0:T(8,128)(2,1)S(1)} %collective-permute-done.16.refs_2_) | copy-start | bytes 786436
  38.8 6.5 %collective-permute-start.6 = (bf16[256,256]{1,0:T(8,128)(2,1)S(1)}, bf16[256,256]{1,0:T(8,128)(2,1)S(1)}, u32[]{:S(2)}, u32[]{:S(2)}) collective-permute-start(bf16[256,256]{1,0:T(8,128)(2,1)S(1)} %collective-permute-done.5.refs_2_), channel_id=1, source_target_pairs={{0,2},{1,3},{2,0},{3,1},{4,6},{5,7},{6,4},{7,5},{8,10},{9,11},{10,... | collective-permute-start | bytes 393224 | tf_op jit(solution)/shard_map/ppermute | solution.py:285
  39.5 15.9 %copy-start.17 = (bf16[256,256]{1,0:T(8,128)(2,1)}, bf16[256,256]{1,0:T(8,128)(2,1)S(1)}, u32[]{:S(2)}) copy-start(bf16[256,256]{1,0:T(8,128)(2,1)S(1)} %collective-permute-done.3.refs_3_) | copy-start | bytes 393220
  39.5 7.9 %collective-permute-start.4 = (bf16[256,256]{1,0:T(8,128)(2,1)S(1)}, bf16[256,256]{1,0:T(8,128)(2,1)S(1)}, u32[]{:S(2)}, u32[]{:S(2)}) collective-permute-start(bf16[256,256]{1,0:T(8,128)(2,1)S(1)} %collective-permute-done.3.refs_3_), channel_id=1, source_target_pairs={{0,2},{1,3},{2,0},{3,1},{4,6},{5,7},{6,4},{7,5},{8,10},{9,11},{10,... | collective-permute-start | bytes 393224 | tf_op jit(solution)/shard_map/ppermute | solution.py:285
  43.9 11.6 %collective-permute-start.14 = (bf16[128,1536]{1,0:T(8,128)(2,1)}, bf16[128,1536]{1,0:T(8,128)(2,1)S(1)}, u32[]{:S(2)}, u32[]{:S(2)}) collective-permute-start(bf16[128,1536]{1,0:T(8,128)(2,1)} %dynamic-slice_bitcast_fusion.2), channel_id=1, source_target_pairs={{0,17},{1,16},{2,19},{3,18},{4,21},{5,20},{6,23},{7,22},{8,25},{9,... | collective-permute-start | bytes 1179656 | tf_op jit(solution)/shard_map/ppermute | solution.py:285
  45.2 11.2 %copy-start.21 = (bf16[256,256]{1,0:T(8,128)(2,1)}, bf16[256,256]{1,0:T(8,128)(2,1)S(1)}, u32[]{:S(2)}) copy-start(bf16[256,256]{1,0:T(8,128)(2,1)S(1)} %collective-permute-done.6.refs_2_) | copy-start | bytes 393220
  45.3 11.2 %collective-permute-start.22 = (bf16[512,256]{1,0:T(8,128)(2,1)}, bf16[512,256]{1,0:T(8,128)(2,1)S(1)}, u32[]{:S(2)}, u32[]{:S(2)}) collective-permute-start(bf16[512,256]{1,0:T(8,128)(2,1)} %collective-permute-done.18.refs_3_), channel_id=1, source_target_pairs={{0,2},{1,3},{2,0},{3,1},{4,6},{5,7},{6,4},{7,5},{8,10},{9,11},{10,... | collective-permute-start | bytes 786440 | tf_op jit(solution)/shard_map/ppermute | solution.py:285
  47.4 9.0 %copy-start.23 = (bf16[256,256]{1,0:T(8,128)(2,1)}, bf16[256,256]{1,0:T(8,128)(2,1)S(1)}, u32[]{:S(2)}) copy-start(bf16[256,256]{1,0:T(8,128)(2,1)S(1)} %collective-permute-done.4.refs_2_) | copy-start | bytes 393220
  47.4 11.2 %collective-permute-start.19 = (bf16[512,256]{1,0:T(8,128)(2,1)}, bf16[512,256]{1,0:T(8,128)(2,1)}, u32[]{:S(2)}, u32[]{:S(2)}) collective-permute-start(bf16[512,256]{1,0:T(8,128)(2,1)} %collective-permute-done.18.refs_3_), channel_id=1, source_target_pairs={{0,12},{1,13},{2,14},{3,15},{4,8},{5,9},{6,10},{7,11},{8,4},{9,5},... | collective-permute-start | bytes 786440 | tf_op jit(solution)/shard_map/ppermute | solution.py:285
  56.2 30.9 %collective-permute-start.26 = (bf16[256,1536]{1,0:T(8,128)(2,1)}, bf16[256,1536]{1,0:T(8,128)(2,1)S(1)}, u32[]{:S(2)}, u32[]{:S(2)}) collective-permute-start(bf16[256,1536]{1,0:T(8,128)(2,1)} %get-tuple-element.26), channel_id=1, source_target_pairs={{0,17},{1,16},{2,19},{3,18},{4,21},{5,20},{6,23},{7,22},{8,25},{9,... | collective-permute-start | bytes 2359304 | tf_op jit(solution)/shard_map/ppermute | solution.py:285
  57.2 35.5 %collective-permute-start.28 = (bf16[256,1536]{1,0:T(8,128)(2,1)}, bf16[256,1536]{1,0:T(8,128)(2,1)S(1)}, u32[]{:S(2)}, u32[]{:S(2)}) collective-permute-start(bf16[256,1536]{1,0:T(8,128)(2,1)} %get-tuple-element.25), channel_id=1, source_target_pairs={{0,17},{1,16},{2,19},{3,18},{4,21},{5,20},{6,23},{7,22},{8,25},{9,... | collective-permute-start | bytes 2359304 | tf_op jit(solution)/shard_map/ppermute | solution.py:285
  58.7 8.7 %collective-permute-start.17 = (bf16[512,256]{1,0:T(8,128)(2,1)}, bf16[512,256]{1,0:T(8,128)(2,1)S(1)}, u32[]{:S(2)}, u32[]{:S(2)}) collective-permute-start(bf16[512,256]{1,0:T(8,128)(2,1)} %copy-done.7), channel_id=1, source_target_pairs={{0,2},{1,3},{2,0},{3,1},{4,6},{5,7},{6,4},{7,5},{8,10},{9,11},{10,... | collective-permute-start | bytes 786440 | tf_op jit(solution)/shard_map/ppermute | solution.py:285
  68.2 8.8 %collective-permute-start.20 = (bf16[512,256]{1,0:T(8,128)(2,1)}, bf16[512,256]{1,0:T(8,128)(2,1)}, u32[]{:S(2)}, u32[]{:S(2)}) collective-permute-start(bf16[512,256]{1,0:T(8,128)(2,1)} %collective-permute-done.19.refs_3_), channel_id=1, source_target_pairs={{0,2},{1,3},{2,0},{3,1},{4,6},{5,7},{6,4},{7,5},{8,10},{9,11},{10,... | collective-permute-start | bytes 786440 | tf_op jit(solution)/shard_map/ppermute | solution.py:285
  70.4 13.9 %copy-start.6 = (bf16[512,256]{1,0:T(8,128)(2,1)S(1)}, bf16[512,256]{1,0:T(8,128)(2,1)}, u32[]{:S(2)}) copy-start(bf16[512,256]{1,0:T(8,128)(2,1)} %copy-done.5) | copy-start | bytes 786436
  70.4 26.3 %copy-start.26 = (bf16[256,256]{1,0:T(8,128)(2,1)S(1)}, bf16[256,256]{1,0:T(8,128)(2,1)}, u32[]{:S(2)}) copy-start(bf16[256,256]{1,0:T(8,128)(2,1)} %copy-done.25) | copy-start | bytes 393220
  70.4 26.3 %copy-start.28 = (bf16[256,256]{1,0:T(8,128)(2,1)S(1)}, bf16[256,256]{1,0:T(8,128)(2,1)}, u32[]{:S(2)}) copy-start(bf16[256,256]{1,0:T(8,128)(2,1)} %copy-done.27) | copy-start | bytes 393220
  70.4 27.2 %copy-start.14 = (bf16[256,256]{1,0:T(8,128)(2,1)S(1)}, bf16[256,256]{1,0:T(8,128)(2,1)}, u32[]{:S(2)}) copy-start(bf16[256,256]{1,0:T(8,128)(2,1)} %copy-done.13) | copy-start | bytes 393220
  70.4 27.2 %copy-start.20 = (bf16[256,256]{1,0:T(8,128)(2,1)S(1)}, bf16[256,256]{1,0:T(8,128)(2,1)}, u32[]{:S(2)}) copy-start(bf16[256,256]{1,0:T(8,128)(2,1)} %copy-done.19) | copy-start | bytes 393220
  70.4 28.2 %copy-start.16 = (bf16[256,256]{1,0:T(8,128)(2,1)S(1)}, bf16[256,256]{1,0:T(8,128)(2,1)}, u32[]{:S(2)}) copy-start(bf16[256,256]{1,0:T(8,128)(2,1)} %copy-done.15) | copy-start | bytes 393220
  70.4 28.2 %copy-start.18 = (bf16[256,256]{1,0:T(8,128)(2,1)S(1)}, bf16[256,256]{1,0:T(8,128)(2,1)}, u32[]{:S(2)}) copy-start(bf16[256,256]{1,0:T(8,128)(2,1)} %copy-done.17) | copy-start | bytes 393220
  73.2 1.0 copy-start.10
  75.1 24.5 %copy-start.22 = (bf16[256,256]{1,0:T(8,128)(2,1)S(1)}, bf16[256,256]{1,0:T(8,128)(2,1)}, u32[]{:S(2)}) copy-start(bf16[256,256]{1,0:T(8,128)(2,1)} %copy-done.21) | copy-start | bytes 393220
  75.1 25.2 %copy-start.24 = (bf16[256,256]{1,0:T(8,128)(2,1)S(1)}, bf16[256,256]{1,0:T(8,128)(2,1)}, u32[]{:S(2)}) copy-start(bf16[256,256]{1,0:T(8,128)(2,1)} %copy-done.23) | copy-start | bytes 393220
  76.9 33.0 %collective-permute-start.15 = (bf16[128,1536]{1,0:T(8,128)(2,1)}, bf16[128,1536]{1,0:T(8,128)(2,1)S(1)}, u32[]{:S(2)}, u32[]{:S(2)}) collective-permute-start(bf16[128,1536]{1,0:T(8,128)(2,1)} %copy-done.1), channel_id=1, source_target_pairs={{0,4},{1,5},{2,6},{3,7},{4,0},{5,1},{6,2},{7,3},{8,12},{9,13},{10,... | collective-permute-start | bytes 1179656 | tf_op jit(solution)/shard_map/ppermute | solution.py:285
  87.1 15.0 %collective-permute-start.24 = (bf16[256,256]{1,0:T(8,128)(2,1)S(1)}, bf16[256,256]{1,0:T(8,128)(2,1)S(1)}, u32[]{:S(2)}, u32[]{:S(2)}) collective-permute-start(bf16[256,256]{1,0:T(8,128)(2,1)S(1)} %get-tuple-element.24), channel_id=1, source_target_pairs={{0,4},{1,5},{2,6},{3,7},{4,0},{5,1},{6,2},{7,3},{8,12},{9,13},{10,... | collective-permute-start | bytes 393224 | tf_op jit(solution)/shard_map/ppermute | solution.py:285
  92.7 12.8 %collective-permute-start.27 = (bf16[256,256]{1,0:T(8,128)(2,1)S(1)}, bf16[256,256]{1,0:T(8,128)(2,1)S(1)}, u32[]{:S(2)}, u32[]{:S(2)}) collective-permute-start(bf16[256,256]{1,0:T(8,128)(2,1)S(1)} %get-tuple-element.24), channel_id=1, source_target_pairs={{0,5},{1,4},{2,7},{3,6},{4,1},{5,0},{6,3},{7,2},{8,13},{9,12},{10,... | collective-permute-start | bytes 393224 | tf_op jit(solution)/shard_map/ppermute | solution.py:285
  96.4 6.6 %collective-permute-start.25 = (bf16[256,256]{1,0:T(8,128)(2,1)S(1)}, bf16[256,256]{1,0:T(8,128)(2,1)S(1)}, u32[]{:S(2)}, u32[]{:S(2)}) collective-permute-start(bf16[256,256]{1,0:T(8,128)(2,1)S(1)} %get-tuple-element.23.refs_1_.refs_5_), channel_id=1, source_target_pairs={{0,1},{1,0},{2,3},{3,2},{4,5},{5,4},{6,7},{7,6},{8,9},{9,8},{10,11... | collective-permute-start | bytes 393224 | tf_op jit(solution)/shard_map/ppermute | solution.py:285
  102.2 7.7 %collective-permute-start.10 = (bf16[256,128]{1,0:T(8,128)(2,1)S(1)}, bf16[256,128]{1,0:T(8,128)(2,1)S(1)}, u32[]{:S(2)}, u32[]{:S(2)}) collective-permute-start(bf16[256,128]{1,0:T(8,128)(2,1)S(1)} %get-tuple-element.19), channel_id=1, source_target_pairs={{0,4},{1,5},{2,6},{3,7},{4,0},{5,1},{6,2},{7,3},{8,12},{9,13},{10,... | collective-permute-start | bytes 196616 | tf_op jit(solution)/shard_map/ppermute | solution.py:285
  103.0 6.9 %collective-permute-start.12 = (bf16[256,128]{1,0:T(8,128)(2,1)S(1)}, bf16[256,128]{1,0:T(8,128)(2,1)S(1)}, u32[]{:S(2)}, u32[]{:S(2)}) collective-permute-start(bf16[256,128]{1,0:T(8,128)(2,1)S(1)} %get-tuple-element.19), channel_id=1, source_target_pairs={{0,5},{1,4},{2,7},{3,6},{4,1},{5,0},{6,3},{7,2},{8,13},{9,12},{10,... | collective-permute-start | bytes 196616 | tf_op jit(solution)/shard_map/ppermute | solution.py:285
  105.5 4.4 %copy-start.2 = (bf16[128,1536]{1,0:T(8,128)(2,1)S(1)}, bf16[128,1536]{1,0:T(8,128)(2,1)}, u32[]{:S(2)}) copy-start(bf16[128,1536]{1,0:T(8,128)(2,1)} %copy-done.1) | copy-start | bytes 1179652
  105.5 4.4 %collective-permute-start.11 = (bf16[256,128]{1,0:T(8,128)(2,1)S(1)}, bf16[256,128]{1,0:T(8,128)(2,1)S(1)}, u32[]{:S(2)}, u32[]{:S(2)}) collective-permute-start(bf16[256,128]{1,0:T(8,128)(2,1)S(1)} %get-tuple-element.20.refs_9_), channel_id=1, source_target_pairs={{0,1},{1,0},{2,3},{3,2},{4,5},{5,4},{6,7},{7,6},{8,9},{9,8},{10,11... | collective-permute-start | bytes 196616 | tf_op jit(solution)/shard_map/ppermute | solution.py:285
  (12 other events, 9.1 us)

commit v5 on v4

--- a/solution.py
+++ b/solution.py
@@ -19,21 +19,21 @@
     return pltpu.CompilerParams(vmem_limit_bytes=mib << 20)
 
 
-def pack_kernel(groups, role_ref, k_any, v_any, *rest):
-    out_refs, (k_ref, v_ref, sems) = rest[:-3], rest[-3:]
+def pack_kernel(groups, role_ref, k_any, v_any, q_any, *rest):
+    outs, (k_ref, v_ref, q_ref, sems) = rest[:-4], rest[-4:]
     loads = [
-        pltpu.make_async_copy(k_any, k_ref, sems.at[0]),
-        pltpu.make_async_copy(v_any, v_ref, sems.at[1]),
+        pltpu.make_async_copy(source, target, sems.at[at])
+        for at, (source, target) in enumerate(((k_any, k_ref), (v_any, v_ref), (q_any, q_ref)))
     ]
     for load in loads:
         load.start()
-    for load in loads:
-        load.wait()
     rows, width = k_ref.shape
     half = width // 2
+    loads[0].wait()
+    loads[1].wait()
     for side in range(2):
         role = role_ref[0] if side == 0 else 1 - role_ref[0]
-        for heads, out in zip(groups, out_refs[side * len(groups) :]):
+        for heads, out in zip(groups, outs[side * len(groups) :]):
             for place, head in enumerate(heads):
                 lanes = pl.ds(pl.multiple_of(role * half + head * HD, HD), HD)
                 base = place * 2 * HD
@@ -42,53 +42,72 @@
                         piece * HD : (piece + 1) * HD, lanes
                     ]
                 out[base + HD : base + 2 * HD, :] = v_ref[:, lanes].T
-
-
+    loads[2].wait()
+    for side in range(2):
+        role = role_ref[0] if side == 0 else 1 - role_ref[0]
+        for head in range(half // HD):
+            lanes = pl.ds(pl.multiple_of(role * half + head * HD, HD), HD)
+            outs[side - 2][head * HD : (head + 1) * HD, :] = q_ref[:, lanes].T
+
+
+SMEM = pl.BlockSpec(memory_space=pltpu.SMEM)
 ANY = pl.BlockSpec(memory_space=pl.ANY)
-HBM = pl.BlockSpec(memory_space=pltpu.HBM)
-SMEM = pl.BlockSpec(memory_space=pltpu.SMEM)
 
 
 def in_hbm(x):
     return pltpu.with_memory_space_constraint(x, pltpu.HBM)
 
 
-def pack(role, keys, values, groups):
-    rows = keys.shape[0]
-    shapes = [pltpu.VMEM((len(heads) * 2 * HD, rows), jnp.bfloat16) for heads in groups]
+def pack(role, keys, values, queries, groups):
+    rows, width = keys.shape
+    shapes = [
+        jax.ShapeDtypeStruct((len(heads) * 2 * HD, rows), jnp.bfloat16) for heads in groups
+    ]
+    asked = jax.ShapeDtypeStruct((width // 2, rows), jnp.bfloat16)
     return pl.pallas_call(
         functools.partial(pack_kernel, groups),
-        out_shape=tuple(shapes + shapes),
-        in_specs=[SMEM, HBM, HBM],
-        out_specs=(VMEM,) * (2 * len(groups)),
-        scratch_shapes=[
-            pltpu.VMEM(keys.shape, keys.dtype),
-            pltpu.VMEM(values.shape, values.dtype),
-            pltpu.SemaphoreType.DMA((2,)),
-        ],
+        out_shape=tuple(shapes + shapes + [asked, asked]),
+        in_specs=[SMEM, ANY, ANY, ANY],
+        out_specs=(VMEM,) * (2 * len(groups) + 2),
+        scratch_shapes=[pltpu.VMEM((rows, width), jnp.bfloat16)] * 3
+        + [pltpu.SemaphoreType.DMA((3,))],
         compiler_params=limit(8),
         name="pack",
-    )(role, in_hbm(keys), in_hbm(values))
-
-
-def turn_kernel(role_ref, x_ref, mine_ref, give_ref):
-    half = x_ref.shape[1] // 2
-    for out, role in ((mine_ref, role_ref[0]), (give_ref, 1 - role_ref[0])):
-        for head in range(half // HD):
-            lanes = pl.ds(pl.multiple_of(role * half + head * HD, HD), HD)
-            out[head * HD : (head + 1) * HD, :] = x_ref[:, lanes].T
-
-
-def turned(role, x):
-    shape = jax.ShapeDtypeStruct((x.shape[1] // 2, x.shape[0]), x.dtype)
+    )(role, in_hbm(keys), in_hbm(values), in_hbm(queries))
+
+
+def carve_kernel(local, cols, spot_ref, w_any, third_ref, firsts_ref, sems):
+    role, share = spot_ref[0], spot_ref[1]
+    lanes = pl.ds(pl.multiple_of(share * cols, HD), cols)
+    pair = 2 * HD
+
+    def rows(head, count):
+        return w_any.at[pl.ds(pl.multiple_of(head * HD, HD), count), lanes]
+
+    copies = [
+        pltpu.make_async_copy(rows(role * local + 2, HD), third_ref, sems.at[0]),
+        pltpu.make_async_copy(rows(role * local, pair), firsts_ref.at[:pair, :], sems.at[1]),
+        pltpu.make_async_copy(rows((1 - role) * local, pair), firsts_ref.at[pair:, :], sems.at[2]),
+    ]
+    for copy in copies:
+        copy.start()
+    for copy in copies:
+        copy.wait()
+
+
+def carve(spot, weight, local, cols):
     return pl.pallas_call(
-        turn_kernel,
-        out_shape=(shape, shape),
-        in_specs=[SMEM, VMEM],
+        functools.partial(carve_kernel, local, cols),
+        out_shape=(
+            jax.ShapeDtypeStruct((HD, cols), weight.dtype),
+            jax.ShapeDtypeStruct((4 * HD, cols), weight.dtype),
+        ),
+        in_specs=[SMEM, ANY],
         out_specs=(VMEM, VMEM),
-        compiler_params=limit(8),
-        name="turned",
-    )(role, x)
+        scratch_shapes=[pltpu.SemaphoreType.DMA((3,))],
+        compiler_params=limit(4),
+        name="carve",
+    )(spot, in_hbm(weight))
 
 
 def absorb_kernel(heads, count, first, last, *refs):
@@ -161,13 +180,15 @@
 
 
 def project_kernel(pieces, *refs):
-    out = refs[-1]
-    refs = refs[1:-1]
+    out, kept, kept_gate = refs[-3:]
+    refs = refs[1:-3]
     left = jnp.concatenate([refs[2 * at][...] for at in range(pieces)], axis=1)
     right = jnp.concatenate([refs[2 * at + 1][...] for at in range(pieces)], axis=0)
-    base, gate = refs[-2], refs[-1]
+    keep, stream, gate = refs[-3:]
     branch = jnp.dot(left, right, preferred_element_type=jnp.float32)
-    out[...] = (base[...].astype(jnp.float32) + gate[...] * branch).astype(out.dtype)
+    out[...] = stream[...].astype(jnp.float32) + gate[...] * branch
+    kept[...] = keep[...]
+    kept_gate[...] = gate[...]
 
 
 def finish_kernel(pieces, wide, *refs):
@@ -205,36 +226,48 @@
     )(*operands)
 
 
-def project(where, sources, base, gate, cols, wide, dtype):
-    rows = base.shape[0]
+def project(where, sources, keep, weight, stream, gate, cols, wide):
+    rows = stream.shape[0]
     steps = cols // wide
     operands, specs, depth = [], [], 0
-    for piece, lane, weight, row, whole in sources:
+
+    def ours(j, s):
+        return s[0] * steps + j
+
+    for piece, lane, weights, row, whole in sources:
         width = piece.shape[1] if lane is None else HD
         depth += width
 
         def left(j, s, lane=lane):
-            return 0, (0 if lane is None else lane(s))
+            return 0, (0 if lane is None else lane)
 
         def right(j, s, row=row, whole=whole):
-            return row(s), (s[0] * steps + j if whole else j)
-
-        operands += [piece, weight]
+            return row(s), (ours(j, s) if whole else j)
+
+        operands += [piece, weights]
         specs += [pl.BlockSpec((rows, width), left), pl.BlockSpec((width, wide), right)]
-    whole = base.shape[1] != cols
-    operands += [base, gate]
+    operands += [weight, stream, gate]
     specs += [
-        pl.BlockSpec((rows, wide), lambda j, s: (0, s[0] * steps + j if whole else j)),
-        pl.BlockSpec((1, wide), lambda j, s: (0, s[0] * steps + j)),
+        pl.BlockSpec((HD, wide), lambda j, s: (keep(s), ours(j, s))),
+        pl.BlockSpec((rows, wide), lambda j, s: (0, ours(j, s))),
+        pl.BlockSpec((1, wide), lambda j, s: (0, ours(j, s))),
     ]
     return pl.pallas_call(
         functools.partial(project_kernel, len(sources)),
-        out_shape=jax.ShapeDtypeStruct((rows, cols), dtype),
+        out_shape=(
+            jax.ShapeDtypeStruct((rows, cols), jnp.float32),
+            jax.ShapeDtypeStruct((HD, cols), weight.dtype),
+            jax.ShapeDtypeStruct((1, cols), gate.dtype),
+        ),
         grid_spec=pltpu.PrefetchScalarGridSpec(
             num_scalar_prefetch=1,
             grid=(steps,),
             in_specs=specs,
-            out_specs=pl.BlockSpec((rows, wide), lambda j, s: (0, j)),
+            out_specs=(
+                pl.BlockSpec((rows, wide), lambda j, s: (0, j)),
+                pl.BlockSpec((HD, wide), lambda j, s: (0, j)),
+                pl.BlockSpec((1, wide), lambda j, s: (0, j)),
+            ),
         ),
         cost_estimate=pl.CostEstimate(
             flops=2 * rows * depth * cols, bytes_accessed=rows * cols * 4, transcendentals=0
@@ -288,23 +321,12 @@
     share = lax.axis_index("head").astype(jnp.int32)
     role = role_of(lax.axis_index("seq").astype(jnp.int32) // stride)
     role_ref = role.reshape(1)
-    column = lax.axis_index("seq").astype(jnp.int32) // stride % 2
-    where = jnp.stack([share, role, column])
+    where = jnp.stack([share, role])
     groups = [(0, 1), (2,)]
-    everyone = range(len(groups))
-
-    col_count = out_weight.shape[2] // shares
-    lent = {}
-    for by in range(1, shares):
-        start = lax.rem(share + by, shares) * col_count
-        lent[by] = []
-        for head, count in ((role * local + 2, 1), (role * local, 2), ((1 - role) * local, 2)):
-            part = lax.dynamic_slice(out_weight[0], (head * HD, start), (count * HD, col_count))
-            lent[by].append(hop(part, still, 1, by))
-
-    packed = pack(role_ref, keys[0], values[0], groups)
-    mine, give = packed[: len(groups)], packed[len(groups) :]
-    my_query, give_query = turned(role_ref, queries[0])
+
+    packed = pack(role_ref, keys[0], values[0], queries[0], groups)
+    mine, give = packed[: len(groups)], packed[len(groups) : 2 * len(groups)]
+    my_query, give_query = packed[-2:]
     got = [None] * len(groups)
     far = [[None] * 2 for _ in groups]
     near = [[None] * 2 for _ in groups]
@@ -316,11 +338,17 @@
         near[g][0] = hop(mine[g], beside, 1)
         own[g] = hop(mine[g], still, 1)
     asking = [hop(my_query, still, 1), hop(give_query, partner, 1)]
+
+    col_count = out_weight.shape[2] // shares
+    lent = {}
+    for by in range(1, shares):
+        spot = jnp.stack([role, lax.rem(share + by, shares)])
+        parts = carve(spot, out_weight[0], local, col_count)
+        lent[by] = [hop(part, still, 1, by) for part in parts]
+        lent[by].append(hop(lent[by][0], partner))
     weight = hop(out_weight[0], still, 1)
     stream = hop(stream_in[0], still, 1)
     gate = hop(gate_scale, still, 1)
-    for by in range(1, shares):
-        lent[by].append(hop(lent[by][0], partner))
 
     def fold(g, blocks, held, last=False):
         return absorb(asking, blocks, groups[g], held, last)
@@ -329,23 +357,16 @@
     for g in everyone:
         far[g][1] = hop(got[g], beyond)
         near[g][1] = hop(got[g], beside)
-        state = fold(g, [own[g], got[g]], None)
-        state = fold(g, near[g], state)
+        state = fold(g, [own[g], got[g], *near[g]], None)
         arrived = far[g]
         for turn in range(1, rounds):
             onward = [hop(arrived[i], beside) for i in range(2)]
-            following = None
+            state = fold(g, [arrived[0], onward[0], arrived[1]], state)
             if turn < rounds - 1:
-                following = [hop(arrived[i], beyond) for i in range(2)]
-            state = fold(g, arrived, state)
-            if turn < rounds - 1:
-                state = fold(g, onward, state)
-            elif g < len(groups) - 1:
-                attended.append(fold(g, onward, state, True))
+                state = fold(g, onward[1:], state)
+                arrived = [hop(arrived[i], beyond) for i in range(2)]
             else:
-                state = fold(g, onward[:1], state)
                 attended.append(fold(g, onward[1:], state, True))
-            arrived = following
 
     home = []
     for g in everyone:
@@ -361,23 +382,20 @@
     first, second = home
     sources = []
     for head in range(2):
-        pick = lambda s, head=head: head
-        sources.append((first[0], pick, weight, lambda s, h=head: s[1] * local + h, True))
-        sources.append((first[1], pick, weight, lambda s, h=head: (1 - s[1]) * local + h, True))
+        sources.append((first[0], head, weight, lambda s, h=head: s[1] * local + h, True))
+        sources.append((first[1], head, weight, lambda s, h=head: (1 - s[1]) * local + h, True))
     sources.append((second[0], None, weight, lambda s: s[1] * local + 2, True))
-    own_start = share * col_count
-    last_pieces = [second[1]]
-    last_weights = [
-        lax.dynamic_slice(weight, (((1 - role) * local + 2) * HD, own_start), (HD, col_count))
-    ]
     for by in range(1, shares):
-        thirds, pairs, others, relayed = lent[by]
-        sources.append((first[2][by], None, pairs, top, False))
-        sources.append((first[3][by], None, others, top, False))
+        firsts = lent[by][1]
+        sources.append((first[2][by], None, firsts, top, False))
+        sources.append((first[3][by], None, firsts, lambda s: 1, False))
+    base, own_third, own_gate = project(
+        where, sources, lambda s: (1 - s[1]) * local + 2, weight, stream, gate, col_count, 512
+    )
+    last_pieces, last_weights = [second[1]], [own_third]
+    for by in range(1, shares):
         last_pieces += [second[2][by], second[3][by]]
-        last_weights += [thirds, relayed]
-    base = project(where, sources, stream, gate, col_count, 512, jnp.float32)
-    own_gate = lax.dynamic_slice(gate, (0, own_start), (1, col_count))
+        last_weights += [lent[by][0], lent[by][2]]
     return finish(last_pieces, last_weights, base, own_gate, 384)[None]
 
 

time: 112 us -> 106 us (0.946)
  local copies, waits for them, and re-layouts: 16.6 us -> 0.01 us
  waiting for transfers between devices: 28.8 us -> 36.7 us
  starting transfers between devices: 44.2 us -> 49.2 us
  Pallas kernels: 21.4 us -> 19.3 us
    unnamed x58 -> x2, local copies, waits for them, and re-layouts: 11.1 us -> 0.01 us
    ppermute x31 -> x30, waiting for transfers between devices: 28.8 us -> 36.7 us  [hop(): return lax.ppermute(block, ('segment', 'seq', 'head'), pairs)]
    dynamic_slice x4 -> x0, local copies, waits for them, and re-layouts: 5.44 us -> none  [the longest x2 4.41 us: per_device(): lax.dynamic_slice(out_weight[0], (head * HD, start), (count * HD, col_cou...]
    ppermute x31 -> x30, starting transfers between devices: 44.2 us -> 49.2 us  [hop(): return lax.ppermute(block, ('segment', 'seq', 'head'), pairs)]
    pallas_call x9 -> x6, Pallas kernels: 14.4 us -> 10.1 us  [absorb(): pl.pallas_call(functools.partial(absorb_kernel, heads, len(blocks), first...]
    pallas_call x1, Pallas kernels: 0.15 us -> 2.07 us  [carve(): pl.pallas_call(functools.partial(carve_kernel, local, cols), out_shape=(j...]
  transfers between devices with their start and end apart: 31 -> 30, of which waited for: 10 -> 12; matrix products, arithmetic and copies ran while one was open for 5% -> 0% of each run, Pallas kernels for 18% -> 17%
where the time goes in v5:
time: 106 us; the launch traced here: 105 us
  starting transfers between devices  49.2 us (46%)
  waiting for transfers between devices  36.7 us (35%)
  Pallas kernels  19.3 us (18%)
    ppermute x30, starting transfers between devices, hop(): return lax.ppermute(block, ('segment', 'seq', 'head'), pairs)  49.2 us
    ppermute x30, waiting for transfers between devices, hop(): return lax.ppermute(block, ('segment', 'seq', 'head'), pairs)  36.7 us
    pallas_call x6, Pallas kernels, absorb(): pl.pallas_call(functools.partial(absorb_kernel, heads, len(blocks), first...  10.1 us
    pallas_call x1, Pallas kernels, project(): pl.pallas_call(functools.partial(project_kernel, len(sources)), out_shape...  4.3 us
  transfers between devices with their start and end apart: 30, of which 12 were waited for; matrix products, arithmetic and copies ran while one was open for 0% of the time, Pallas kernels for 17%

profile of v5, /device:TPU:0, one launch (start us, length us, event | category | flops | bytes accessed | tf_op | source)
XLA Modules:
  0.0 105.4 jit_solution(9801926432408181992)
XLA Ops:
  0.0 0.5 collective-permute-start.21
  0.5 1.5 %pack.1 = (bf16[512,256]{1,0:T(8,128)(2,1)S(1)}, bf16[256,256]{1,0:T(8,128)(2,1)S(1)}, bf16[512,256]{1,0:T(8,128)(2,1)S(1)}, bf16[256,256]{1,0:T(8,128)(2,1)S(1)...) custom-call(s32[1]{0:T(128)} %bitcast.role_ref, bf16[256,768]{1,0:T(8,128)(2,1)} %bitcast.11, ...), custom_call_target="tpu_custom_call" | custom-call | tf_op jit(solution)/shard_map/pack/pallas_call | solution.py:67
  2.0 2.7 %collective-permute-start.2 = (bf16[256,256]{1,0:T(8,128)(2,1)S(1)}, bf16[256,256]{1,0:T(8,128)(2,1)S(1)}, u32[]{:S(2)}, u32[]{:S(2)}) collective-permute-start(bf16[256,256]{1,0:T(8,128)(2,1)S(1)} %get-tuple-element.22), channel_id=1, source_target_pairs={{0,20},{1,21},{2,22},{3,23},{4,16},{5,17},{6,18},{7,19},{8,28},{9,... | collective-permute-start | bytes 393224 | tf_op jit(solution)/shard_map/ppermute | solution.py:318
  4.7 0.5 collective-permute-start.27
  5.2 1.1 %collective-permute-start.8 = (bf16[256,256]{1,0:T(8,128)(2,1)S(1)}, bf16[256,256]{1,0:T(8,128)(2,1)S(1)}, u32[]{:S(2)}, u32[]{:S(2)}) collective-permute-start(bf16[256,256]{1,0:T(8,128)(2,1)S(1)} %get-tuple-element.23), channel_id=1, source_target_pairs={{0,18},{1,19},{2,16},{3,17},{4,22},{5,23},{6,20},{7,21},{8,26},{9,... | collective-permute-start | bytes 393224 | tf_op jit(solution)/shard_map/ppermute | solution.py:318
  6.3 2.1 %collective-permute-done.27.refs_17_ = f32[1,3072]{1,0:T(1,128)S(1)} collective-permute-done((f32[1,3072]{1,0:T(1,128)}, f32[1,3072]{1,0:T(1,128)S(1)}, u32[]{:S(2)}, u32[]{:S(2)}) %collective-permute-start.27) | collective-permute-done | bytes 12320 | tf_op jit(solution)/shard_map/ppermute | solution.py:318
  8.4 4.7 %collective-permute-start.5 = (bf16[256,256]{1,0:T(8,128)(2,1)S(1)}, bf16[256,256]{1,0:T(8,128)(2,1)S(1)}, u32[]{:S(2)}, u32[]{:S(2)}) collective-permute-start(bf16[256,256]{1,0:T(8,128)(2,1)S(1)} %get-tuple-element.23), channel_id=1, source_target_pairs={{0,28},{1,29},{2,30},{3,31},{4,24},{5,25},{6,26},{7,27},{8,20},{9,... | collective-permute-start | bytes 393224 | tf_op jit(solution)/shard_map/ppermute | solution.py:318
  13.1 0.4 collective-permute-start
  13.5 1.7 %collective-permute-start.13 = (bf16[512,256]{1,0:T(8,128)(2,1)S(1)}, bf16[512,256]{1,0:T(8,128)(2,1)S(1)}, u32[]{:S(2)}, u32[]{:S(2)}) collective-permute-start(bf16[512,256]{1,0:T(8,128)(2,1)S(1)} %get-tuple-element.26), channel_id=1, source_target_pairs={{0,20},{1,21},{2,22},{3,23},{4,16},{5,17},{6,18},{7,19},{8,28},{9,... | collective-permute-start | bytes 786440 | tf_op jit(solution)/shard_map/ppermute | solution.py:318
  15.3 1.8 %collective-permute-done.5.refs_2_ = bf16[256,256]{1,0:T(8,128)(2,1)S(1)} collective-permute-done((bf16[256,256]{1,0:T(8,128)(2,1)S(1)}, bf16[256,256]{1,0:T(8,128)(2,1)S(1)}, u32[]{:S(2)}, u32[]{:S(2)}) %collective-permute-start.5) | collective-permute-done | bytes 131104 | tf_op jit(solution)/shard_map/ppermute | solution.py:318
  17.1 0.5 collective-permute-start.18
  17.6 1.2 %collective-permute-start.19 = (bf16[512,256]{1,0:T(8,128)(2,1)S(1)}, bf16[512,256]{1,0:T(8,128)(2,1)S(1)}, u32[]{:S(2)}, u32[]{:S(2)}) collective-permute-start(bf16[512,256]{1,0:T(8,128)(2,1)S(1)} %get-tuple-element.27), channel_id=1, source_target_pairs={{0,18},{1,19},{2,16},{3,17},{4,22},{5,23},{6,20},{7,21},{8,26},{9,... | collective-permute-start | bytes 786440 | tf_op jit(solution)/shard_map/ppermute | solution.py:318
  18.8 2.7 %collective-permute-done.1.refs_1_ = bf16[384,256]{1,0:T(8,128)(2,1)S(1)} collective-permute-done((bf16[384,256]{1,0:T(8,128)(2,1)S(1)}, bf16[384,256]{1,0:T(8,128)(2,1)S(1)}, u32[]{:S(2)}, u32[]{:S(2)}) %collective-permute-start.1) | collective-permute-done | bytes 196640 | tf_op jit(solution)/shard_map/ppermute | solution.py:318
  21.5 2.3 %collective-permute-start.16 = (bf16[512,256]{1,0:T(8,128)(2,1)S(1)}, bf16[512,256]{1,0:T(8,128)(2,1)S(1)}, u32[]{:S(2)}, u32[]{:S(2)}) collective-permute-start(bf16[512,256]{1,0:T(8,128)(2,1)S(1)} %get-tuple-element.27), channel_id=1, source_target_pairs={{0,28},{1,29},{2,30},{3,31},{4,24},{5,25},{6,26},{7,27},{8,20},{9,... | collective-permute-start | bytes 786440 | tf_op jit(solution)/shard_map/ppermute | solution.py:318
  23.9 2.1 %carve.1 = (bf16[128,1536]{1,0:T(8,128)(2,1)S(1)}, bf16[512,1536]{1,0:T(8,128)(2,1)S(1)}) custom-call(s32[2]{0:T(128)S(1)} %pad_add_fusion.1.spot_ref, bf16[768,3072]{1,0:T(8,128)(2,1)} %bitcast.10), custom_call_target="tpu_custom_call" | custom-call | tf_op jit(solution)/shard_map/carve/pallas_call | solution.py:99
  26.0 1.7 %collective-permute-done.13.refs_3_ = bf16[512,256]{1,0:T(8,128)(2,1)S(1)} collective-permute-done((bf16[512,256]{1,0:T(8,128)(2,1)S(1)}, bf16[512,256]{1,0:T(8,128)(2,1)S(1)}, u32[]{:S(2)}, u32[]{:S(2)}) %collective-permute-start.13) | collective-permute-done | bytes 262176 | tf_op jit(solution)/shard_map/ppermute | solution.py:318
  27.7 1.3 %collective-permute-start.24 = (bf16[512,1536]{1,0:T(8,128)(2,1)S(1)}, bf16[512,1536]{1,0:T(8,128)(2,1)S(1)}, u32[]{:S(2)}, u32[]{:S(2)}) collective-permute-start(bf16[512,1536]{1,0:T(8,128)(2,1)S(1)} %get-tuple-element.30), channel_id=1, source_target_pairs={{0,17},{1,16},{2,19},{3,18},{4,21},{5,20},{6,23},{7,22},{8,25},{9,... | collective-permute-start | bytes 4718600 | tf_op jit(solution)/shard_map/ppermute | solution.py:318
  28.9 0.4 collective-permute-start.26
  29.3 1.5 %collective-permute-start.9 = (bf16[256,256]{1,0:T(8,128)(2,1)S(1)}, bf16[256,256]{1,0:T(8,128)(2,1)S(1)}, u32[]{:S(2)}, u32[]{:S(2)}) collective-permute-start(bf16[256,256]{1,0:T(8,128)(2,1)S(1)} %collective-permute-done.2.refs_3_), channel_id=1, source_target_pairs={{0,2},{1,3},{2,0},{3,1},{4,6},{5,7},{6,4},{7,5},{8,10},{9,11},{10,... | collective-permute-start | bytes 393224 | tf_op jit(solution)/shard_map/ppermute | solution.py:318
  30.8 1.5 %collective-permute-done.16.refs_2_ = bf16[512,256]{1,0:T(8,128)(2,1)S(1)} collective-permute-done((bf16[512,256]{1,0:T(8,128)(2,1)S(1)}, bf16[512,256]{1,0:T(8,128)(2,1)S(1)}, u32[]{:S(2)}, u32[]{:S(2)}) %collective-permute-start.16) | collective-permute-done | bytes 262176 | tf_op jit(solution)/shard_map/ppermute | solution.py:318
  32.3 4.0 %collective-permute-start.3 = (bf16[256,256]{1,0:T(8,128)(2,1)S(1)}, bf16[256,256]{1,0:T(8,128)(2,1)S(1)}, u32[]{:S(2)}, u32[]{:S(2)}) collective-permute-start(bf16[256,256]{1,0:T(8,128)(2,1)S(1)} %collective-permute-done.2.refs_3_), channel_id=1, source_target_pairs={{0,12},{1,13},{2,14},{3,15},{4,8},{5,9},{6,10},{7,11},{8,4},{9,5},... | collective-permute-start | bytes 393224 | tf_op jit(solution)/shard_map/ppermute | solution.py:318
  36.3 1.5 %collective-permute-start.20 = (bf16[512,256]{1,0:T(8,128)(2,1)S(1)}, bf16[512,256]{1,0:T(8,128)(2,1)S(1)}, u32[]{:S(2)}, u32[]{:S(2)}) collective-permute-start(bf16[512,256]{1,0:T(8,128)(2,1)S(1)} %collective-permute-done.13.refs_3_), channel_id=1, source_target_pairs={{0,2},{1,3},{2,0},{3,1},{4,6},{5,7},{6,4},{7,5},{8,10},{9,11},{10,... | collective-permute-start | bytes 786440 | tf_op jit(solution)/shard_map/ppermute | solution.py:318
  37.8 2.4 %collective-permute-done.3.refs_4_ = bf16[256,256]{1,0:T(8,128)(2,1)S(1)} collective-permute-done((bf16[256,256]{1,0:T(8,128)(2,1)S(1)}, bf16[256,256]{1,0:T(8,128)(2,1)S(1)}, u32[]{:S(2)}, u32[]{:S(2)}) %collective-permute-start.3) | collective-permute-done | bytes 131104 | tf_op jit(solution)/shard_map/ppermute | solution.py:318
  40.1 1.5 %collective-permute-start.6 = (bf16[256,256]{1,0:T(8,128)(2,1)S(1)}, bf16[256,256]{1,0:T(8,128)(2,1)S(1)}, u32[]{:S(2)}, u32[]{:S(2)}) collective-permute-start(bf16[256,256]{1,0:T(8,128)(2,1)S(1)} %collective-permute-done.5.refs_2_), channel_id=1, source_target_pairs={{0,2},{1,3},{2,0},{3,1},{4,6},{5,7},{6,4},{7,5},{8,10},{9,11},{10,... | collective-permute-start | bytes 393224 | tf_op jit(solution)/shard_map/ppermute | solution.py:318
  41.6 5.5 %collective-permute-done.6.refs_3_ = bf16[256,256]{1,0:T(8,128)(2,1)S(1)} collective-permute-done((bf16[256,256]{1,0:T(8,128)(2,1)S(1)}, bf16[256,256]{1,0:T(8,128)(2,1)S(1)}, u32[]{:S(2)}, u32[]{:S(2)}) %collective-permute-start.6) | collective-permute-done | bytes 131104 | tf_op jit(solution)/shard_map/ppermute | solution.py:318
  47.2 1.5 %collective-permute-start.14 = (bf16[512,256]{1,0:T(8,128)(2,1)S(1)}, bf16[512,256]{1,0:T(8,128)(2,1)S(1)}, u32[]{:S(2)}, u32[]{:S(2)}) collective-permute-start(bf16[512,256]{1,0:T(8,128)(2,1)S(1)} %collective-permute-done.13.refs_3_), channel_id=1, source_target_pairs={{0,12},{1,13},{2,14},{3,15},{4,8},{5,9},{6,10},{7,11},{8,4},{9,5},... | collective-permute-start | bytes 786440 | tf_op jit(solution)/shard_map/ppermute | solution.py:318
  48.7 1.5 %collective-permute-start.17 = (bf16[512,256]{1,0:T(8,128)(2,1)S(1)}, bf16[512,256]{1,0:T(8,128)(2,1)S(1)}, u32[]{:S(2)}, u32[]{:S(2)}) collective-permute-start(bf16[512,256]{1,0:T(8,128)(2,1)S(1)} %collective-permute-done.16.refs_2_), channel_id=1, source_target_pairs={{0,2},{1,3},{2,0},{3,1},{4,6},{5,7},{6,4},{7,5},{8,10},{9,11},{10,... | collective-permute-start | bytes 786440 | tf_op jit(solution)/shard_map/ppermute | solution.py:318
  50.2 6.1 %collective-permute-done.14.refs_4_ = bf16[512,256]{1,0:T(8,128)(2,1)S(1)} collective-permute-done((bf16[512,256]{1,0:T(8,128)(2,1)S(1)}, bf16[512,256]{1,0:T(8,128)(2,1)S(1)}, u32[]{:S(2)}, u32[]{:S(2)}) %collective-permute-start.14) | collective-permute-done | bytes 262176 | tf_op jit(solution)/shard_map/ppermute | solution.py:318
  56.3 1.5 %collective-permute-start.15 = (bf16[512,256]{1,0:T(8,128)(2,1)S(1)}, bf16[512,256]{1,0:T(8,128)(2,1)S(1)}, u32[]{:S(2)}, u32[]{:S(2)}) collective-permute-start(bf16[512,256]{1,0:T(8,128)(2,1)S(1)} %collective-permute-done.14.refs_4_), channel_id=1, source_target_pairs={{0,2},{1,3},{2,0},{3,1},{4,6},{5,7},{6,4},{7,5},{8,10},{9,11},{10,... | collective-permute-start | bytes 786440 | tf_op jit(solution)/shard_map/ppermute | solution.py:318
  57.8 5.0 %collective-permute-done.15.refs_2_ = bf16[512,256]{1,0:T(8,128)(2,1)S(1)} collective-permute-done((bf16[512,256]{1,0:T(8,128)(2,1)S(1)}, bf16[512,256]{1,0:T(8,128)(2,1)S(1)}, u32[]{:S(2)}, u32[]{:S(2)}) %collective-permute-start.15) | collective-permute-done | bytes 262176 | tf_op jit(solution)/shard_map/ppermute | solution.py:318
  62.8 1.5 %collective-permute-start.4 = (bf16[256,256]{1,0:T(8,128)(2,1)S(1)}, bf16[256,256]{1,0:T(8,128)(2,1)S(1)}, u32[]{:S(2)}, u32[]{:S(2)}) collective-permute-start(bf16[256,256]{1,0:T(8,128)(2,1)S(1)} %collective-permute-done.3.refs_4_), channel_id=1, source_target_pairs={{0,2},{1,3},{2,0},{3,1},{4,6},{5,7},{6,4},{7,5},{8,10},{9,11},{10,... | collective-permute-start | bytes 393224 | tf_op jit(solution)/shard_map/ppermute | solution.py:318
  64.3 2.9 %absorb.9.refs_5_ = f32[2,2,144,256]{3,2,1,0:T(8,128)S(1)} custom-call(bf16[384,256]{1,0:T(8,128)(2,1)S(1)} %collective-permute-done.refs_0_, bf16[384,256]{1,0:T(8,128)(2,1)S(1)} %collective-permute-done.1.refs_1_, bf16[512,256]{1,0:T(8,128)(2,1)S(1)} %collective-permute-done.18.refs_2_, bf16[512,256]{1,0:T(8,128)(2,1)S(1)} %collective-permute-done.13.refs_3_, ...), custom_call_target="tpu_custom_call" | custom-call | flops 536870912 | bytes 786432 | tf_op jit(solution)/shard_map/absorb/pallas_call | solution.py:166
  67.3 2.3 %absorb.10.refs_3_ = f32[2,2,144,256]{3,2,1,0:T(8,128)S(1)} custom-call(bf16[384,256]{1,0:T(8,128)(2,1)S(1)} %collective-permute-done.refs_0_, bf16[384,256]{1,0:T(8,128)(2,1)S(1)} %collective-permute-done.1.refs_1_, bf16[512,256]{1,0:T(8,128)(2,1)S(1)} %collective-permute-done.16.refs_2_, ...), custom_call_target="tpu_custom_call", output_to_operand_aliasing={{}: (5, {})} | custom-call | flops 402653184 | bytes 786432 | tf_op jit(solution)/shard_map/absorb/pallas_call | solution.py:166
  69.6 1.4 %absorb.11 = (bf16[256,256]{1,0:T(8,128)(2,1)S(1)}, bf16[256,256]{1,0:T(8,128)(2,1)S(1)}) custom-call(bf16[384,256]{1,0:T(8,128)(2,1)S(1)} %collective-permute-done.refs_0_, bf16[384,256]{1,0:T(8,128)(2,1)S(1)} %collective-permute-done.1.refs_1_, bf16[512,256]{1,0:T(8,128)(2,1)S(1)} %collective-permute-done.15.refs_2_, f32[2,2,144,256]{3,2,1,0:T(8,128)S(1)} %absorb.10.refs_3_), custom_call_target="tpu_custom_call" | custom-call | flops 134217728 | bytes 786432 | tf_op jit(solution)/shard_map/absorb/pallas_call | solution.py:166
  70.9 7.8 %collective-permute-start.22 = (bf16[256,256]{1,0:T(8,128)(2,1)S(1)}, bf16[256,256]{1,0:T(8,128)(2,1)S(1)}, u32[]{:S(2)}, u32[]{:S(2)}) collective-permute-start(bf16[256,256]{1,0:T(8,128)(2,1)S(1)} %get-tuple-element.29), channel_id=1, source_target_pairs={{0,4},{1,5},{2,6},{3,7},{4,0},{5,1},{6,2},{7,3},{8,12},{9,13},{10,... | collective-permute-start | bytes 393224 | tf_op jit(solution)/shard_map/ppermute | solution.py:318
  78.8 4.3 %collective-permute-done.22.refs_3_.refs_7_ = bf16[256,256]{1,0:T(8,128)(2,1)S(1)} collective-permute-done((bf16[256,256]{1,0:T(8,128)(2,1)S(1)}, bf16[256,256]{1,0:T(8,128)(2,1)S(1)}, u32[]{:S(2)}, u32[]{:S(2)}) %collective-permute-start.22) | collective-permute-done | bytes 131104 | tf_op jit(solution)/shard_map/ppermute | solution.py:318
  83.1 1.5 %collective-permute-start.23 = (bf16[256,256]{1,0:T(8,128)(2,1)S(1)}, bf16[256,256]{1,0:T(8,128)(2,1)S(1)}, u32[]{:S(2)}, u32[]{:S(2)}) collective-permute-start(bf16[256,256]{1,0:T(8,128)(2,1)S(1)} %get-tuple-element.28.refs_1_.refs_5_), channel_id=1, source_target_pairs={{0,1},{1,0},{2,3},{3,2},{4,5},{5,4},{6,7},{7,6},{8,9},{9,8},{10,11... | collective-permute-start | bytes 393224 | tf_op jit(solution)/shard_map/ppermute | solution.py:318
  84.6 3.4 %collective-permute-done.23.refs_11_ = bf16[256,256]{1,0:T(8,128)(2,1)S(1)} collective-permute-done((bf16[256,256]{1,0:T(8,128)(2,1)S(1)}, bf16[256,256]{1,0:T(8,128)(2,1)S(1)}, u32[]{:S(2)}, u32[]{:S(2)}) %collective-permute-start.23) | collective-permute-done | bytes 131104 | tf_op jit(solution)/shard_map/ppermute | solution.py:318
  88.1 3.7 %collective-permute-start.25 = (bf16[256,256]{1,0:T(8,128)(2,1)S(1)}, bf16[256,256]{1,0:T(8,128)(2,1)S(1)}, u32[]{:S(2)}, u32[]{:S(2)}) collective-permute-start(bf16[256,256]{1,0:T(8,128)(2,1)S(1)} %get-tuple-element.29), channel_id=1, source_target_pairs={{0,5},{1,4},{2,7},{3,6},{4,1},{5,0},{6,3},{7,2},{8,13},{9,12},{10,... | collective-permute-start | bytes 393224 | tf_op jit(solution)/shard_map/ppermute | solution.py:318
  91.9 1.5 %absorb.6.refs_5_ = f32[1,2,144,256]{3,2,1,0:T(8,128)S(1)} custom-call(bf16[384,256]{1,0:T(8,128)(2,1)S(1)} %collective-permute-done.refs_0_, bf16[384,256]{1,0:T(8,128)(2,1)S(1)} %collective-permute-done.1.refs_1_, bf16[256,256]{1,0:T(8,128)(2,1)S(1)} %collective-permute-done.7.refs_2_, bf16[256,256]{1,0:T(8,128)(2,1)S(1)} %collective-permute-done.2.refs_3_, ...), custom_call_target="tpu_custom_call" | custom-call | flops 268435456 | bytes 393216 | tf_op jit(solution)/shard_map/absorb/pallas_call | solution.py:166
  93.4 1.2 %absorb.7.refs_3_ = f32[1,2,144,256]{3,2,1,0:T(8,128)S(1)} custom-call(bf16[384,256]{1,0:T(8,128)(2,1)S(1)} %collective-permute-done.refs_0_, bf16[384,256]{1,0:T(8,128)(2,1)S(1)} %collective-permute-done.1.refs_1_, bf16[256,256]{1,0:T(8,128)(2,1)S(1)} %collective-permute-done.5.refs_2_, ...), custom_call_target="tpu_custom_call", output_to_operand_aliasing={{}: (5, {})} | custom-call | flops 201326592 | bytes 393216 | tf_op jit(solution)/shard_map/absorb/pallas_call | solution.py:166
  94.6 0.8 absorb.8
  95.4 0.1 collective-permute-done.25.refs_13_
  95.6 0.9 collective-permute-start.10
  96.4 2.6 %collective-permute-start.12 = (bf16[256,128]{1,0:T(8,128)(2,1)S(1)}, bf16[256,128]{1,0:T(8,128)(2,1)S(1)}, u32[]{:S(2)}, u32[]{:S(2)}) collective-permute-start(bf16[256,128]{1,0:T(8,128)(2,1)S(1)} %get-tuple-element.24), channel_id=1, source_target_pairs={{0,5},{1,4},{2,7},{3,6},{4,1},{5,0},{6,3},{7,2},{8,13},{9,12},{10,... | collective-permute-start | bytes 196616 | tf_op jit(solution)/shard_map/ppermute | solution.py:318
  99.0 0.6 collective-permute-start.11
  99.7 4.3 %project.1 = (f32[256,1536]{1,0:T(8,128)S(1)}, bf16[128,1536]{1,0:T(8,128)(2,1)S(1)}, f32[1,1536]{1,0:T(1,128)S(1)}) custom-call(s32[2]{0:T(128)S(1)} %pad_add_fusion.refs_0_, bf16[256,256]{1,0:T(8,128)(2,1)S(1)} %get-tuple-element.28.refs_1_.refs_5_, bf16[768,3072]{1,0:T(8,128)(2,1)} %collective-permute-done.21.refs_2_.refs_4_.refs_6_.refs_8_.refs_10_.refs_15_, ...), custom_call_target="tpu_custom_call" | custom-call | flops 905969664 | bytes 1572864 | tf_op jit(solution)/shard_map/project/pallas_call | solution.py:255
  104.0 1.4 %finish.1 = bf16[256,1536]{1,0:T(8,128)(2,1)} custom-call(bf16[256,128]{1,0:T(8,128)(2,1)S(1)} %collective-permute-done.10.refs_0_, bf16[256,128]{1,0:T(8,128)(2,1)S(1)} %collective-permute-done.11.refs_1_, bf16[256,128]{1,0:T(8,128)(2,1)S(1)} %collective-permute-done.12.refs_2_, bf16[128,1536]{1,0:T(8,128)(2,1)S(1)} %get-tuple-element.31.refs_3_, ...), custom_call_target="tpu_custom_call" | custom-call | flops 301989888 | bytes 786432 | tf_op jit(solution)/shard_map/finish/pallas_call | solution.py:212
  (26 shorter events, 0.3 us)
Async XLA Ops:
  0.0 99.7 %collective-permute-start.21 = (bf16[768,3072]{1,0:T(8,128)(2,1)}, bf16[768,3072]{1,0:T(8,128)(2,1)}, u32[]{:S(2)}, u32[]{:S(2)}) collective-permute-start(bf16[768,3072]{1,0:T(8,128)(2,1)} %bitcast.9), channel_id=1, source_target_pairs={{0,16},{1,17},{2,18},{3,19},{4,20},{5,21},{6,22},{7,23},{8,24},{9,... | collective-permute-start | bytes 14155784 | tf_op jit(solution)/shard_map/ppermute | solution.py:318
  2.0 11.2 %collective-permute-start.2 = (bf16[256,256]{1,0:T(8,128)(2,1)S(1)}, bf16[256,256]{1,0:T(8,128)(2,1)S(1)}, u32[]{:S(2)}, u32[]{:S(2)}) collective-permute-start(bf16[256,256]{1,0:T(8,128)(2,1)S(1)} %get-tuple-element.22), channel_id=1, source_target_pairs={{0,20},{1,21},{2,22},{3,23},{4,16},{5,17},{6,18},{7,19},{8,28},{9,... | collective-permute-start | bytes 393224 | tf_op jit(solution)/shard_map/ppermute | solution.py:318
  4.7 8.8 %collective-permute-start.7 = (bf16[256,256]{1,0:T(8,128)(2,1)S(1)}, bf16[256,256]{1,0:T(8,128)(2,1)S(1)}, u32[]{:S(2)}, u32[]{:S(2)}) collective-permute-start(bf16[256,256]{1,0:T(8,128)(2,1)S(1)} %get-tuple-element.23), channel_id=1, source_target_pairs={{0,16},{1,17},{2,18},{3,19},{4,20},{5,21},{6,22},{7,23},{8,24},{9,... | collective-permute-start | bytes 393224 | tf_op jit(solution)/shard_map/ppermute | solution.py:318
  4.7 3.7 %collective-permute-start.27 = (f32[1,3072]{1,0:T(1,128)}, f32[1,3072]{1,0:T(1,128)S(1)}, u32[]{:S(2)}, u32[]{:S(2)}) collective-permute-start(f32[1,3072]{1,0:T(1,128)} %param.11), channel_id=1, source_target_pairs={{0,16},{1,17},{2,18},{3,19},{4,20},{5,21},{6,22},{7,23},{8,24},{9,... | collective-permute-start | bytes 36872 | tf_op jit(solution)/shard_map/ppermute | solution.py:318
  5.2 8.3 %collective-permute-start.8 = (bf16[256,256]{1,0:T(8,128)(2,1)S(1)}, bf16[256,256]{1,0:T(8,128)(2,1)S(1)}, u32[]{:S(2)}, u32[]{:S(2)}) collective-permute-start(bf16[256,256]{1,0:T(8,128)(2,1)S(1)} %get-tuple-element.23), channel_id=1, source_target_pairs={{0,18},{1,19},{2,16},{3,17},{4,22},{5,23},{6,20},{7,21},{8,26},{9,... | collective-permute-start | bytes 393224 | tf_op jit(solution)/shard_map/ppermute | solution.py:318
  8.4 8.6 %collective-permute-start.5 = (bf16[256,256]{1,0:T(8,128)(2,1)S(1)}, bf16[256,256]{1,0:T(8,128)(2,1)S(1)}, u32[]{:S(2)}, u32[]{:S(2)}) collective-permute-start(bf16[256,256]{1,0:T(8,128)(2,1)S(1)} %get-tuple-element.23), channel_id=1, source_target_pairs={{0,28},{1,29},{2,30},{3,31},{4,24},{5,25},{6,26},{7,27},{8,20},{9,... | collective-permute-start | bytes 393224 | tf_op jit(solution)/shard_map/ppermute | solution.py:318
  13.1 4.5 %collective-permute-start = (bf16[384,256]{1,0:T(8,128)(2,1)S(1)}, bf16[384,256]{1,0:T(8,128)(2,1)S(1)}, u32[]{:S(2)}, u32[]{:S(2)}) collective-permute-start(bf16[384,256]{1,0:T(8,128)(2,1)S(1)} %get-tuple-element.20), channel_id=1, source_target_pairs={{0,16},{1,17},{2,18},{3,19},{4,20},{5,21},{6,22},{7,23},{8,24},{9,... | collective-permute-start | bytes 589832 | tf_op jit(solution)/shard_map/ppermute | solution.py:318
  13.5 8.0 %collective-permute-start.1 = (bf16[384,256]{1,0:T(8,128)(2,1)S(1)}, bf16[384,256]{1,0:T(8,128)(2,1)S(1)}, u32[]{:S(2)}, u32[]{:S(2)}) collective-permute-start(bf16[384,256]{1,0:T(8,128)(2,1)S(1)} %get-tuple-element.21), channel_id=1, source_target_pairs={{0,20},{1,21},{2,22},{3,23},{4,16},{5,17},{6,18},{7,19},{8,28},{9,... | collective-permute-start | bytes 589832 | tf_op jit(solution)/shard_map/ppermute | solution.py:318
  13.5 14.1 %collective-permute-start.13 = (bf16[512,256]{1,0:T(8,128)(2,1)S(1)}, bf16[512,256]{1,0:T(8,128)(2,1)S(1)}, u32[]{:S(2)}, u32[]{:S(2)}) collective-permute-start(bf16[512,256]{1,0:T(8,128)(2,1)S(1)} %get-tuple-element.26), channel_id=1, source_target_pairs={{0,20},{1,21},{2,22},{3,23},{4,16},{5,17},{6,18},{7,19},{8,28},{9,... | collective-permute-start | bytes 786440 | tf_op jit(solution)/shard_map/ppermute | solution.py:318
  17.1 11.9 %collective-permute-start.18 = (bf16[512,256]{1,0:T(8,128)(2,1)S(1)}, bf16[512,256]{1,0:T(8,128)(2,1)S(1)}, u32[]{:S(2)}, u32[]{:S(2)}) collective-permute-start(bf16[512,256]{1,0:T(8,128)(2,1)S(1)} %get-tuple-element.27), channel_id=1, source_target_pairs={{0,16},{1,17},{2,18},{3,19},{4,20},{5,21},{6,22},{7,23},{8,24},{9,... | collective-permute-start | bytes 786440 | tf_op jit(solution)/shard_map/ppermute | solution.py:318
  17.6 11.7 %collective-permute-start.19 = (bf16[512,256]{1,0:T(8,128)(2,1)S(1)}, bf16[512,256]{1,0:T(8,128)(2,1)S(1)}, u32[]{:S(2)}, u32[]{:S(2)}) collective-permute-start(bf16[512,256]{1,0:T(8,128)(2,1)S(1)} %get-tuple-element.27), channel_id=1, source_target_pairs={{0,18},{1,19},{2,16},{3,17},{4,22},{5,23},{6,20},{7,21},{8,26},{9,... | collective-permute-start | bytes 786440 | tf_op jit(solution)/shard_map/ppermute | solution.py:318
  21.5 10.8 %collective-permute-start.16 = (bf16[512,256]{1,0:T(8,128)(2,1)S(1)}, bf16[512,256]{1,0:T(8,128)(2,1)S(1)}, u32[]{:S(2)}, u32[]{:S(2)}) collective-permute-start(bf16[512,256]{1,0:T(8,128)(2,1)S(1)} %get-tuple-element.27), channel_id=1, source_target_pairs={{0,28},{1,29},{2,30},{3,31},{4,24},{5,25},{6,26},{7,27},{8,20},{9,... | collective-permute-start | bytes 786440 | tf_op jit(solution)/shard_map/ppermute | solution.py:318
  23.9 5.0 %copy-start = (bf16[1,256,3072]{2,1,0:T(8,128)(2,1)S(1)}, bf16[1,256,3072]{2,1,0:T(8,128)(2,1)}, u32[]{:S(2)}) copy-start(bf16[1,256,3072]{2,1,0:T(8,128)(2,1)} %param.6) | copy-start | bytes 4718596
  27.7 68.8 %collective-permute-start.24 = (bf16[512,1536]{1,0:T(8,128)(2,1)S(1)}, bf16[512,1536]{1,0:T(8,128)(2,1)S(1)}, u32[]{:S(2)}, u32[]{:S(2)}) collective-permute-start(bf16[512,1536]{1,0:T(8,128)(2,1)S(1)} %get-tuple-element.30), channel_id=1, source_target_pairs={{0,17},{1,16},{2,19},{3,18},{4,21},{5,20},{6,23},{7,22},{8,25},{9,... | collective-permute-start | bytes 4718600 | tf_op jit(solution)/shard_map/ppermute | solution.py:318
  28.9 70.1 %collective-permute-start.26 = (bf16[256,3072]{1,0:T(8,128)(2,1)S(1)}, bf16[256,3072]{1,0:T(8,128)(2,1)S(1)}, u32[]{:S(2)}, u32[]{:S(2)}) collective-permute-start(bf16[256,3072]{1,0:T(8,128)(2,1)S(1)} %bitcast.14), channel_id=1, source_target_pairs={{0,16},{1,17},{2,18},{3,19},{4,20},{5,21},{6,22},{7,23},{8,24},{9,... | collective-permute-start | bytes 4718600 | tf_op jit(solution)/shard_map/ppermute | solution.py:318
  29.3 7.0 %collective-permute-start.9 = (bf16[256,256]{1,0:T(8,128)(2,1)S(1)}, bf16[256,256]{1,0:T(8,128)(2,1)S(1)}, u32[]{:S(2)}, u32[]{:S(2)}) collective-permute-start(bf16[256,256]{1,0:T(8,128)(2,1)S(1)} %collective-permute-done.2.refs_3_), channel_id=1, source_target_pairs={{0,2},{1,3},{2,0},{3,1},{4,6},{5,7},{6,4},{7,5},{8,10},{9,11},{10,... | collective-permute-start | bytes 393224 | tf_op jit(solution)/shard_map/ppermute | solution.py:318
  32.3 7.9 %collective-permute-start.3 = (bf16[256,256]{1,0:T(8,128)(2,1)S(1)}, bf16[256,256]{1,0:T(8,128)(2,1)S(1)}, u32[]{:S(2)}, u32[]{:S(2)}) collective-permute-start(bf16[256,256]{1,0:T(8,128)(2,1)S(1)} %collective-permute-done.2.refs_3_), channel_id=1, source_target_pairs={{0,12},{1,13},{2,14},{3,15},{4,8},{5,9},{6,10},{7,11},{8,4},{9,5},... | collective-permute-start | bytes 393224 | tf_op jit(solution)/shard_map/ppermute | solution.py:318
  36.3 12.4 %collective-permute-start.20 = (bf16[512,256]{1,0:T(8,128)(2,1)S(1)}, bf16[512,256]{1,0:T(8,128)(2,1)S(1)}, u32[]{:S(2)}, u32[]{:S(2)}) collective-permute-start(bf16[512,256]{1,0:T(8,128)(2,1)S(1)} %collective-permute-done.13.refs_3_), channel_id=1, source_target_pairs={{0,2},{1,3},{2,0},{3,1},{4,6},{5,7},{6,4},{7,5},{8,10},{9,11},{10,... | collective-permute-start | bytes 786440 | tf_op jit(solution)/shard_map/ppermute | solution.py:318
  40.1 7.0 %collective-permute-start.6 = (bf16[256,256]{1,0:T(8,128)(2,1)S(1)}, bf16[256,256]{1,0:T(8,128)(2,1)S(1)}, u32[]{:S(2)}, u32[]{:S(2)}) collective-permute-start(bf16[256,256]{1,0:T(8,128)(2,1)S(1)} %collective-permute-done.5.refs_2_), channel_id=1, source_target_pairs={{0,2},{1,3},{2,0},{3,1},{4,6},{5,7},{6,4},{7,5},{8,10},{9,11},{10,... | collective-permute-start | bytes 393224 | tf_op jit(solution)/shard_map/ppermute | solution.py:318
  47.2 9.1 %collective-permute-start.14 = (bf16[512,256]{1,0:T(8,128)(2,1)S(1)}, bf16[512,256]{1,0:T(8,128)(2,1)S(1)}, u32[]{:S(2)}, u32[]{:S(2)}) collective-permute-start(bf16[512,256]{1,0:T(8,128)(2,1)S(1)} %collective-permute-done.13.refs_3_), channel_id=1, source_target_pairs={{0,12},{1,13},{2,14},{3,15},{4,8},{5,9},{6,10},{7,11},{8,4},{9,5},... | collective-permute-start | bytes 786440 | tf_op jit(solution)/shard_map/ppermute | solution.py:318
  48.7 9.1 %collective-permute-start.17 = (bf16[512,256]{1,0:T(8,128)(2,1)S(1)}, bf16[512,256]{1,0:T(8,128)(2,1)S(1)}, u32[]{:S(2)}, u32[]{:S(2)}) collective-permute-start(bf16[512,256]{1,0:T(8,128)(2,1)S(1)} %collective-permute-done.16.refs_2_), channel_id=1, source_target_pairs={{0,2},{1,3},{2,0},{3,1},{4,6},{5,7},{6,4},{7,5},{8,10},{9,11},{10,... | collective-permute-start | bytes 786440 | tf_op jit(solution)/shard_map/ppermute | solution.py:318
  56.3 6.5 %collective-permute-start.15 = (bf16[512,256]{1,0:T(8,128)(2,1)S(1)}, bf16[512,256]{1,0:T(8,128)(2,1)S(1)}, u32[]{:S(2)}, u32[]{:S(2)}) collective-permute-start(bf16[512,256]{1,0:T(8,128)(2,1)S(1)} %collective-permute-done.14.refs_4_), channel_id=1, source_target_pairs={{0,2},{1,3},{2,0},{3,1},{4,6},{5,7},{6,4},{7,5},{8,10},{9,11},{10,... | collective-permute-start | bytes 786440 | tf_op jit(solution)/shard_map/ppermute | solution.py:318
  57.8 21.0 %collective-permute-start.28 = (bf16[128,1536]{1,0:T(8,128)(2,1)S(1)}, bf16[128,1536]{1,0:T(8,128)(2,1)S(1)}, u32[]{:S(2)}, u32[]{:S(2)}) collective-permute-start(bf16[128,1536]{1,0:T(8,128)(2,1)S(1)} %get-tuple-element.32), channel_id=1, source_target_pairs={{0,17},{1,16},{2,19},{3,18},{4,21},{5,20},{6,23},{7,22},{8,25},{9,... | collective-permute-start | bytes 1179656 | tf_op jit(solution)/shard_map/ppermute | solution.py:318
  62.8 8.1 %collective-permute-start.4 = (bf16[256,256]{1,0:T(8,128)(2,1)S(1)}, bf16[256,256]{1,0:T(8,128)(2,1)S(1)}, u32[]{:S(2)}, u32[]{:S(2)}) collective-permute-start(bf16[256,256]{1,0:T(8,128)(2,1)S(1)} %collective-permute-done.3.refs_4_), channel_id=1, source_target_pairs={{0,2},{1,3},{2,0},{3,1},{4,6},{5,7},{6,4},{7,5},{8,10},{9,11},{10,... | collective-permute-start | bytes 393224 | tf_op jit(solution)/shard_map/ppermute | solution.py:318
  70.9 12.2 %collective-permute-start.22 = (bf16[256,256]{1,0:T(8,128)(2,1)S(1)}, bf16[256,256]{1,0:T(8,128)(2,1)S(1)}, u32[]{:S(2)}, u32[]{:S(2)}) collective-permute-start(bf16[256,256]{1,0:T(8,128)(2,1)S(1)} %get-tuple-element.29), channel_id=1, source_target_pairs={{0,4},{1,5},{2,6},{3,7},{4,0},{5,1},{6,2},{7,3},{8,12},{9,13},{10,... | collective-permute-start | bytes 393224 | tf_op jit(solution)/shard_map/ppermute | solution.py:318
  78.8 25.3 %collective-permute-start.29 = (bf16[128,1536]{1,0:T(8,128)(2,1)S(1)}, bf16[128,1536]{1,0:T(8,128)(2,1)S(1)}, u32[]{:S(2)}, u32[]{:S(2)}) collective-permute-start(bf16[128,1536]{1,0:T(8,128)(2,1)S(1)} %collective-permute-done.28.refs_4_), channel_id=1, source_target_pairs={{0,4},{1,5},{2,6},{3,7},{4,0},{5,1},{6,2},{7,3},{8,12},{9,13},{10,... | collective-permute-start | bytes 1179656 | tf_op jit(solution)/shard_map/ppermute | solution.py:318
  83.1 5.0 %collective-permute-start.23 = (bf16[256,256]{1,0:T(8,128)(2,1)S(1)}, bf16[256,256]{1,0:T(8,128)(2,1)S(1)}, u32[]{:S(2)}, u32[]{:S(2)}) collective-permute-start(bf16[256,256]{1,0:T(8,128)(2,1)S(1)} %get-tuple-element.28.refs_1_.refs_5_), channel_id=1, source_target_pairs={{0,1},{1,0},{2,3},{3,2},{4,5},{5,4},{6,7},{7,6},{8,9},{9,8},{10,11... | collective-permute-start | bytes 393224 | tf_op jit(solution)/shard_map/ppermute | solution.py:318
  88.1 7.5 %collective-permute-start.25 = (bf16[256,256]{1,0:T(8,128)(2,1)S(1)}, bf16[256,256]{1,0:T(8,128)(2,1)S(1)}, u32[]{:S(2)}, u32[]{:S(2)}) collective-permute-start(bf16[256,256]{1,0:T(8,128)(2,1)S(1)} %get-tuple-element.29), channel_id=1, source_target_pairs={{0,5},{1,4},{2,7},{3,6},{4,1},{5,0},{6,3},{7,2},{8,13},{9,12},{10,... | collective-permute-start | bytes 393224 | tf_op jit(solution)/shard_map/ppermute | solution.py:318
  95.6 8.4 %collective-permute-start.10 = (bf16[256,128]{1,0:T(8,128)(2,1)S(1)}, bf16[256,128]{1,0:T(8,128)(2,1)S(1)}, u32[]{:S(2)}, u32[]{:S(2)}) collective-permute-start(bf16[256,128]{1,0:T(8,128)(2,1)S(1)} %get-tuple-element.24), channel_id=1, source_target_pairs={{0,4},{1,5},{2,6},{3,7},{4,0},{5,1},{6,2},{7,3},{8,12},{9,13},{10,... | collective-permute-start | bytes 196616 | tf_op jit(solution)/shard_map/ppermute | solution.py:318
  96.4 7.6 %collective-permute-start.12 = (bf16[256,128]{1,0:T(8,128)(2,1)S(1)}, bf16[256,128]{1,0:T(8,128)(2,1)S(1)}, u32[]{:S(2)}, u32[]{:S(2)}) collective-permute-start(bf16[256,128]{1,0:T(8,128)(2,1)S(1)} %get-tuple-element.24), channel_id=1, source_target_pairs={{0,5},{1,4},{2,7},{3,6},{4,1},{5,0},{6,3},{7,2},{8,13},{9,12},{10,... | collective-permute-start | bytes 196616 | tf_op jit(solution)/shard_map/ppermute | solution.py:318
  99.0 5.0 %collective-permute-start.11 = (bf16[256,128]{1,0:T(8,128)(2,1)S(1)}, bf16[256,128]{1,0:T(8,128)(2,1)S(1)}, u32[]{:S(2)}, u32[]{:S(2)}) collective-permute-start(bf16[256,128]{1,0:T(8,128)(2,1)S(1)} %get-tuple-element.25.refs_9_), channel_id=1, source_target_pairs={{0,1},{1,0},{2,3},{3,2},{4,5},{5,4},{6,7},{7,6},{8,9},{9,8},{10,11... | collective-permute-start | bytes 196616 | tf_op jit(solution)/shard_map/ppermute | solution.py:318
